TPU v7x, 32 devices: a whole 2x2x4 slice. The times are simulated.
32 devices in a mesh: dp: 4 (over y, core), seq: 8 (over z, x).
Axes of the slice: x: 2, y: 2, z: 4, core: 2. Of those that a mesh axis runs over, the one named last changes fastest.
Arguments:
- tokens: bfloat16 [4, 3072, 1024], P('dp', 'seq'), may hold values from -6 to 6
- segment_ids: int32 [4, 3072], P('dp', 'seq'), may hold values from 0 to 7, never falling along the last dimension, each value on 1 to 1536 neighbouring positions
- first_gain: float32 [1024], replicated, may hold values from 0.1 to 1.9
- triple_weight: bfloat16 [1024, 3072], P('dp'), may hold values from -0.1875 to 0.1875
- head_scale: float32 [16], replicated, may hold values from 0.1 to 1.9
- output_weight: bfloat16 [1024, 1024], P('dp'), may hold values from -0.1875 to 0.1875
- post_gain: float32 [1024], replicated, may hold values from 0.1 to 1.9
- second_gain: float32 [1024], replicated, may hold values from 0.1 to 1.9
- up_weight: bfloat16 [1024, 4096], P('dp'), may hold values from -0.1875 to 0.1875
- mid_gain: float32 [4096], replicated, may hold values from 0.1 to 1.9
- down_weight: bfloat16 [4096, 1024], P('dp'), may hold values from -0.09375 to 0.09375
- cotangent: bfloat16 [4, 3072, 1024], P('dp', 'seq'), may hold values from -6 to 6
Outputs:
- layer_out: bfloat16 [4, 3072, 1024], P('dp', 'seq')
- grad_tokens: bfloat16 [4, 3072, 1024], P('dp', 'seq')
- grad_first: float32 [1024], P(('dp', 'seq'))
- grad_triple: float32 [1024, 3072], P(('dp', 'seq'))
- grad_scale: float32 [16], P('seq')
- grad_output: float32 [1024, 1024], P(('dp', 'seq'))
- grad_post: float32 [1024], P(('dp', 'seq'))
- grad_second: float32 [1024], P(('dp', 'seq'))
- grad_up: float32 [1024, 4096], P(('dp', 'seq'))
- grad_mid: float32 [4096], P(('dp', 'seq'))
- grad_down: float32 [4096, 1024], P(('dp', 'seq'))
Inputs may be any that keep to these rules, and one draw needn't show every extreme that they name: `segment_ids`: within each sequence the ids never fall; each of the 8 documents holds 1 to 1536 tokens, and one holds exactly 1536.
All inputs are finite; a program needn't handle non-finite values.
Results may differ from a plain program's by a relative error of at most 0.014.
Values may be sent and summed in bfloat16 or wider, within the bound.
A program may use at most 192 MiB of HBM per device.

v0:
```python
import jax
import jax.numpy as jnp
from jax import lax
from jax.sharding import PartitionSpec as P

HEAD = 64


def layer_norm(values, gains):
    center = values - jnp.mean(values, axis=-1, keepdims=True)
    spread = jnp.mean(center * center, axis=-1, keepdims=True)
    return center * lax.rsqrt(spread + 1e-05) * gains


def gelu_norm(hidden, gains):
    return layer_norm(jax.nn.gelu(hidden, approximate=True), gains)


def transposed_times(left, right):
    return lax.dot_general(
        left, right, (((0,), (0,)), ((), ())), preferred_element_type=jnp.float32
    )


def times_transposed(left, right):
    return lax.dot_general(
        left, right, (((1,), (1,)), ((), ())), preferred_element_type=jnp.float32
    )


def block_scores(queries, keys_all, doc_ids, first_row, block_rows):
    length, width = keys_all.shape
    heads = width // HEAD
    query_block = lax.dynamic_slice_in_dim(queries, first_row, block_rows, 0).reshape(
        block_rows, heads, HEAD
    )
    key_heads = keys_all.reshape(length, heads, HEAD)
    scores = jnp.einsum(
        "qhd,khd->hqk", query_block, key_heads, preferred_element_type=jnp.float32
    ) * HEAD ** (-0.5)
    query_docs = lax.dynamic_slice_in_dim(doc_ids, first_row, block_rows, 0)
    query_pos = first_row + jnp.arange(block_rows, dtype=jnp.int32)
    positions = jnp.arange(length, dtype=jnp.int32)
    allowed = (query_docs[:, None] == doc_ids[None, :]) & (query_pos[:, None] >= positions[None, :])
    return (jnp.where(allowed[None], scores, -1e30), query_block)


def attend_forward(queries, keys_all, values_all, doc_ids):
    length, width = queries.shape
    heads = width // HEAD
    block_rows = min(512, length)
    value_heads = values_all.reshape(length, heads, HEAD)

    def one_block(block_index):
        scores, query_block = block_scores(
            queries, keys_all, doc_ids, block_index * block_rows, block_rows
        )
        highest = jnp.max(scores, axis=-1, keepdims=True)
        exponent = jnp.exp(scores - highest)
        summed = jnp.sum(exponent, axis=-1, keepdims=True)
        weights = (exponent / summed).astype(jnp.bfloat16)
        outputs = jnp.einsum(
            "hqk,khd->qhd", weights, value_heads, preferred_element_type=jnp.float32
        )
        return (outputs.reshape(block_rows, width), (highest + jnp.log(summed))[:, :, 0])

    outputs, logsum = lax.map(one_block, jnp.arange(length // block_rows, dtype=jnp.int32))
    return (outputs.reshape(length, width), logsum)


def attend_backward(queries, keys_all, values_all, doc_ids, logsum, grad_out):
    length, width = queries.shape
    heads = width // HEAD
    block_rows = min(512, length)
    key_heads = keys_all.reshape(length, heads, HEAD)
    value_heads = values_all.reshape(length, heads, HEAD)
    score_scale = HEAD ** (-0.5)

    def one_block(running, block_index):
        grad_keys, grad_values = running
        first_row = block_index * block_rows
        scores, query_block = block_scores(queries, keys_all, doc_ids, first_row, block_rows)
        weights = jnp.exp(scores - logsum[block_index][:, :, None])
        grad_block = lax.dynamic_slice_in_dim(grad_out, first_row, block_rows, 0).reshape(
            block_rows, heads, HEAD
        )
        grad_weights = jnp.einsum(
            "qhd,khd->hqk", grad_block, value_heads, preferred_element_type=jnp.float32
        )
        row_inner = jnp.sum(weights * grad_weights, axis=-1, keepdims=True)
        grad_scores = (weights * (grad_weights - row_inner)).astype(jnp.bfloat16)
        grad_queries = (
            jnp.einsum("hqk,khd->qhd", grad_scores, key_heads, preferred_element_type=jnp.float32)
            * score_scale
        )
        grad_keys = (
            grad_keys
            + jnp.einsum(
                "hqk,qhd->khd", grad_scores, query_block, preferred_element_type=jnp.float32
            )
            * score_scale
        )
        grad_values = grad_values + jnp.einsum(
            "hqk,qhd->khd",
            weights.astype(jnp.bfloat16),
            grad_block,
            preferred_element_type=jnp.float32,
        )
        return ((grad_keys, grad_values), grad_queries.reshape(block_rows, width))

    empty_sums = jnp.zeros((length, heads, HEAD), jnp.float32)
    (grad_keys, grad_values), grad_queries = lax.scan(
        one_block, (empty_sums, empty_sums), jnp.arange(length // block_rows, dtype=jnp.int32)
    )
    return (
        grad_queries.reshape(length, width),
        grad_keys.reshape(length, width),
        grad_values.reshape(length, width),
    )


def per_device(
    tokens,
    segment_ids,
    first_gain,
    triple_weight,
    head_scale,
    output_weight,
    post_gain,
    second_gain,
    up_weight,
    mid_gain,
    down_weight,
    cotangent,
):
    inputs = tokens[0].astype(jnp.float32)
    width = inputs.shape[1]
    doc_ids = lax.all_gather(segment_ids[0], "seq", axis=0, tiled=True)
    triple_full, output_full = (
        lax.all_gather(triple_weight, "dp", axis=0, tiled=True),
        lax.all_gather(output_weight, "dp", axis=0, tiled=True),
    )
    normed, pull_first = jax.vjp(layer_norm, inputs, first_gain)
    normed_low = normed.astype(jnp.bfloat16)
    triple = jnp.dot(normed_low, triple_full, preferred_element_type=jnp.float32).astype(
        jnp.bfloat16
    )
    queries, keys_all, values_all = (
        lax.all_to_all(triple[:, :width], "seq", split_axis=1, concat_axis=0, tiled=True),
        lax.all_to_all(
            triple[:, width : 2 * width], "seq", split_axis=1, concat_axis=0, tiled=True
        ),
        lax.all_to_all(triple[:, 2 * width :], "seq", split_axis=1, concat_axis=0, tiled=True),
    )
    attended, logsum = attend_forward(queries, keys_all, values_all, doc_ids)
    heads_here = queries.shape[1] // HEAD
    own_scale = lax.dynamic_slice_in_dim(
        head_scale, lax.axis_index("seq") * heads_here, heads_here, 0
    )
    scale_wide = jnp.repeat(own_scale, HEAD)
    scaled = (attended * scale_wide).astype(jnp.bfloat16)
    merged = lax.all_to_all(scaled, "seq", split_axis=0, concat_axis=1, tiled=True)
    projected = jnp.dot(merged, output_full, preferred_element_type=jnp.float32)
    post_normed, pull_post = jax.vjp(layer_norm, projected, post_gain)
    middle = inputs + post_normed
    second, pull_second = jax.vjp(layer_norm, middle, second_gain)
    second_low = second.astype(jnp.bfloat16)
    feed_up, feed_down = (
        lax.all_gather(up_weight, "dp", axis=0, tiled=True),
        lax.all_gather(down_weight, "dp", axis=0, tiled=True),
    )
    hidden = jnp.dot(second_low, feed_up, preferred_element_type=jnp.float32)
    activated, pull_mid = jax.vjp(gelu_norm, hidden, mid_gain)
    activated_low = activated.astype(jnp.bfloat16)
    layer_out = (
        middle + jnp.dot(activated_low, feed_down, preferred_element_type=jnp.float32)
    ).astype(jnp.bfloat16)
    upstream = cotangent[0]
    grad_act = times_transposed(upstream, feed_down)
    grad_hidden, grad_mid = pull_mid(grad_act)
    grad_hidden_low = grad_hidden.astype(jnp.bfloat16)
    grad_second_in = times_transposed(grad_hidden_low, feed_up)
    grad_middle_part, grad_second = pull_second(grad_second_in)
    grad_middle = upstream.astype(jnp.float32) + grad_middle_part
    grad_projected, grad_post = pull_post(grad_middle)
    grad_projected_low = grad_projected.astype(jnp.bfloat16)
    grad_merged = times_transposed(grad_projected_low, output_full).astype(jnp.bfloat16)
    grad_scaled = lax.all_to_all(
        grad_merged, "seq", split_axis=1, concat_axis=0, tiled=True
    ).astype(jnp.float32)
    scale_terms = jnp.sum((grad_scaled * attended).reshape(-1, heads_here, HEAD), axis=(0, 2))
    grad_attended = (grad_scaled * scale_wide).astype(jnp.bfloat16)
    grad_queries, grad_keys, grad_values = attend_backward(
        queries, keys_all, values_all, doc_ids, logsum, grad_attended
    )
    back_queries, back_keys, back_values = (
        lax.all_to_all(
            grad_queries.astype(jnp.bfloat16), "seq", split_axis=0, concat_axis=1, tiled=True
        ),
        lax.all_to_all(
            grad_keys.astype(jnp.bfloat16), "seq", split_axis=0, concat_axis=1, tiled=True
        ),
        lax.all_to_all(
            grad_values.astype(jnp.bfloat16), "seq", split_axis=0, concat_axis=1, tiled=True
        ),
    )
    grad_triple_act = jnp.concatenate((back_queries, back_keys, back_values), axis=1)
    grad_normed = times_transposed(grad_triple_act, triple_full)
    grad_input_part, grad_first = pull_first(grad_normed)
    grad_tokens = (grad_middle + grad_input_part).astype(jnp.bfloat16)
    weight_sums = lax.psum_scatter(
        jnp.concatenate(
            (
                transposed_times(normed_low, grad_triple_act),
                transposed_times(merged, grad_projected_low),
                transposed_times(second_low, grad_hidden_low),
            ),
            axis=1,
        ),
        ("dp", "seq"),
        scatter_dimension=0,
        tiled=True,
    )
    grad_down = lax.psum_scatter(
        transposed_times(activated_low, upstream), ("dp", "seq"), scatter_dimension=0, tiled=True
    )
    gain_first, gain_post, gain_second, gain_mid = (
        lax.psum_scatter(grad_first, ("dp", "seq"), scatter_dimension=0, tiled=True),
        lax.psum_scatter(grad_post, ("dp", "seq"), scatter_dimension=0, tiled=True),
        lax.psum_scatter(grad_second, ("dp", "seq"), scatter_dimension=0, tiled=True),
        lax.psum_scatter(grad_mid, ("dp", "seq"), scatter_dimension=0, tiled=True),
    )
    grad_scale = lax.psum(scale_terms, "dp")
    return (
        layer_out[None],
        grad_tokens[None],
        gain_first,
        weight_sums[:, : 3 * width],
        grad_scale,
        weight_sums[:, 3 * width : 4 * width],
        gain_post,
        gain_second,
        weight_sums[:, 4 * width :],
        gain_mid,
        grad_down,
    )


def solution(mesh):
    placed = (
        P("dp", "seq", None),
        P("dp", "seq"),
        P(),
        P("dp", None),
        P(),
        P("dp", None),
        P(),
        P(),
        P("dp", None),
        P(),
        P("dp", None),
        P("dp", "seq", None),
    )
    return jax.shard_map(
        per_device,
        mesh=mesh,
        in_specs=placed,
        out_specs=(
            P("dp", "seq", None),
            P("dp", "seq", None),
            P(("dp", "seq")),
            P(("dp", "seq"), None),
            P("seq"),
            P(("dp", "seq"), None),
            P(("dp", "seq")),
            P(("dp", "seq")),
            P(("dp", "seq"), None),
            P(("dp", "seq")),
            P(("dp", "seq"), None),
        ),
        check_vma=False,
    )
```

profile of v0, /device:TPU:0, one launch (start us, length us, event | category | flops | bytes accessed | tf_op | source)
XLA Modules:
  0.0 1720.9 jit_solution(15729264882951308038)
XLA Ops:
  10.0 48.7 %all-gather.6.cloned.1.call-done = bf16[1024,3072]{1,0:T(8,128)(2,1)} async-done(((bf16[256,3072]{1,0:T(8,128)(2,1)}), bf16[1024,3072]{1,0:T(8,128)(2,1)}) %all-gather.6.cloned.1.call-update) | async-done | bytes 6291472 | tf_op jit(solution)/shard_map/all_gather | solution.py:140
  58.7 5.8 convolution_convert_fusion
  66.1 5.6 all-to-all-start.2
  72.7 19.5 %all-to-all-done.2 = bf16[384,8,128]{2,0,1:T(8,128)(2,1)S(1)} async-done(((bf16[384,8,128]{2,0,1:T(8,128)(2,1)}), bf16[384,8,128]{2,0,1:T(8,128)(2,1)S(1)}, u32[]{:S(2)}, u32[]{:S(2)}) %all-to-all-start.2) | async-done | bytes 786464 | tf_op jit(solution)/shard_map/all_to_all | solution.py:153
  92.3 3.6 all-to-all-start.1
  97.0 19.4 %all-to-all-done.1 = bf16[384,8,128]{2,0,1:T(8,128)(2,1)S(1)} async-done(((bf16[384,8,128]{2,0,1:T(8,128)(2,1)}), bf16[384,8,128]{2,0,1:T(8,128)(2,1)S(1)}, u32[]{:S(2)}, u32[]{:S(2)}) %all-to-all-start.1) | async-done | bytes 786464 | tf_op jit(solution)/shard_map/all_to_all | solution.py:150
  116.3 4.2 all-to-all-start
  121.4 37.1 %all-gather = s32[1,3072]{1,0:T(1,128)S(1)} all-gather(s32[1,384]{1,0:T(1,128)S(1)} %copy-done.55), channel_id=2, replica_groups=mesh['dp'=4,'seq'=8] {'seq'}, dimensions={1}, use_global_device_ids=true | all-gather | bytes 13824 | tf_op jit(solution)/shard_map/all_gather | solution.py:138
  163.9 92.4 %while.29 = (s32[]{:T(128)}, f32[6,512,128]{2,1,0:T(8,128)}, f32[6,2,512]{2,1,0:T(2,128)S(1)}, s32[6]{0:T(128)S(1)}, s32[3072]{0:T(1024)S(1)}, /*index=5*/bf16[3...) while((s32[]{:T(128)}, f32[6,512,128]{2,1,0:T(8,128)}, ...), condition=%wide.region_5.6_spmd.clone, body=%wide.region_2.5_spmd.sunk.clone | while | flops 847773184 | bytes 47372464 | solution.py:67
  171.0 3.6 fusion.140
  174.7 3.7 fusion.141
  186.4 3.6 fusion.140
  190.1 3.7 fusion.141
  201.9 3.6 fusion.140
  205.5 3.7 fusion.141
  217.3 3.6 fusion.140
  220.9 3.7 fusion.141
  232.7 3.6 fusion.140
  236.3 3.7 fusion.141
  248.1 3.6 fusion.140
  251.7 3.7 fusion.141
  258.2 19.6 %all_to_all.131 = bf16[8,384,128]{2,1,0:T(8,128)(2,1)} all-to-all(bf16[8,384,128]{2,1,0:T(8,128)(2,1)S(1)} %multiply_convert_fusion.4), channel_id=1, replica_groups=mesh['dp'=4,'seq'=8] {'seq'}, dimensions={0} | all-to-all | bytes 1572864 | tf_op jit(solution)/shard_map/all_to_all | solution.py:162
  285.3 7.7 fusion.61
  298.4 9.4 multiply_reduce_fusion.1
  307.8 4.2 fusion.64
  312.0 4.6 fusion.27
  316.6 7.9 multiply_reduce_fusion.4
  330.3 4.2 all-to-all-start.4
  338.4 14.2 all-to-all-done.4
  360.6 186.7 %while.30 = (s32[]{:T(128)}, f32[3072,2,64]{0,2,1:T(8,128)S(1)}, f32[3072,2,64]{0,2,1:T(8,128)}, bf16[6,512,128]{2,1,0:T(8,128)(2,1)}, s32[6]{0:T(128)S(1)}, /*i...) while((s32[]{:T(128)}, f32[3072,2,64]{0,2,1:T(8,128)S(1)}, ...), condition=%wide.region_20.21_spmd.clone.clone, body=%wide.region_18.20_spmd.clone.sunk.clone | while | flops 2067267072 | bytes 126798168 | solution.py:112
  368.7 3.8 fusion.155
  372.6 7.4 multiply_reduce_fusion.13
  380.0 7.5 multiply_convert_fusion.11
  399.8 3.8 fusion.155
  403.7 7.4 multiply_reduce_fusion.13
  411.1 7.5 multiply_convert_fusion.11
  430.9 3.8 fusion.155
  434.8 7.4 multiply_reduce_fusion.13
  442.2 7.5 multiply_convert_fusion.11
  462.0 3.8 fusion.155
  465.9 7.4 multiply_reduce_fusion.13
  473.3 7.5 multiply_convert_fusion.11
  493.1 3.8 fusion.155
  497.0 7.4 multiply_reduce_fusion.13
  504.4 7.5 multiply_convert_fusion.11
  524.2 3.8 fusion.155
  528.1 7.4 multiply_reduce_fusion.13
  535.5 7.5 multiply_convert_fusion.11
  547.3 3.6 all-to-all-start.5
  552.1 17.9 %all-to-all-done.5 = bf16[8,384,128]{2,1,0:T(8,128)(2,1)S(1)} async-done(((bf16[8,384,128]{2,1,0:T(8,128)(2,1)}), bf16[8,384,128]{2,1,0:T(8,128)(2,1)S(1)}, u32[]{:S(2)}, u32[]{:S(2)}) %all-to-all-start.5) | async-done | bytes 786464 | tf_op jit(solution)/shard_map/all_to_all | solution.py:197
  576.2 17.5 %all-to-all-done.6 = bf16[8,384,128]{1,2,0:T(8,128)(2,1)S(1)} async-done(((bf16[8,384,128]{1,2,0:T(8,128)(2,1)}), bf16[8,384,128]{1,2,0:T(8,128)(2,1)S(1)}, u32[]{:S(2)}, u32[]{:S(2)}) %all-to-all-start.6) | async-done | bytes 786464 | tf_op jit(solution)/shard_map/all_to_all | solution.py:200
  593.8 4.2 all-to-all-start.7
  598.1 4.8 fusion.55
  603.0 8.4 fusion.59
  612.6 5.3 all-to-all-done.7
  617.9 8.4 fusion.42
  626.3 21.2 %pad_maximum_fusion = f32[1024,8192]{1,0:T(8,128)} fusion(f32[1024,4096]{1,0:T(8,128)} %fusion.59, f32[1024,1024]{1,0:T(8,128)S(1)} %copy-done.2, f32[1024,3072]{1,0:T(8,128)} %fusion.42), kind=kLoop, calls=%fused_computation.35 | loop fusion | flops 16777216 | bytes 67108864 | tf_op jit(solution)/shard_map/concatenate | solution.py:212
  648.7 14.7 fusion.45
  665.9 10.7 fusion.40
  676.6 6.8 psum.7
  683.4 6.6 fusion.39
  692.0 52.8 %all-reduce.4 = (f32[1024]{0:T(1024)S(1)}, f32[1024]{0:T(1024)S(1)}, f32[1024]{0:T(1024)S(1)}, f32[4096]{0:T(1024)S(1)}) all-reduce(f32[1024]{0:T(1024)S(1)} %get-tuple-element.208, f32[1024]{0:T(1024)S(1)} %copy-done.49, f32[1024]{0:T(1024)S(1)} %copy-done.54, ...), channel_id=3, replica_groups=mesh['dp'=4,'seq'=8] {'dp','seq'}, use_global_device_ids=true, to_apply=%region_24.25.clone | all-reduce | flops 7168 | bytes 57344
  750.1 602.9 %reduce-scatter.3.cloned.1.call-done = f32[32,8192]{1,0:T(8,128)} async-done(((f32[1024,8192]{1,0:T(8,128)}), f32[32,8192]{1,0:T(8,128)}) %reduce-scatter.3.cloned.1.call-update) | async-done | bytes 1048592 | tf_op jit(solution)/shard_map/reduce_scatter | solution.py:211
  1358.2 355.6 %reduce-scatter.5.cloned.1.call-done = f32[128,1024]{1,0:T(8,128)} async-done(((f32[4096,1024]{1,0:T(8,128)}), f32[128,1024]{1,0:T(8,128)}) %reduce-scatter.5.cloned.1.call-update) | async-done | bytes 524304 | tf_op jit(solution)/shard_map/reduce_scatter | solution.py:224
  (353 shorter events, 171.6 us)
Async XLA Ops:
  7.2 51.5 %copy-start.27 = (f32[1024]{0:T(1024)S(1)}, f32[1024]{0:T(1024)}, u32[]{:S(2)}) copy-start(f32[1024]{0:T(1024)} %param.18) | copy-start | bytes 12292
  7.2 51.5 %all-gather.6.cloned.1.call-start = ((), (), s32[]{:S(2)}) async-start(), calls=%async_computation.10 | async-start | bytes 7864320 | tf_op jit(solution)/shard_map/all_gather | solution.py:140
  7.9 272.1 %all-gather.8.cloned.1.call-start = ((), (), s32[]{:S(2)}) async-start(), calls=%async_computation.11 | async-start | bytes 2621440 | tf_op jit(solution)/shard_map/all_gather | solution.py:141
  8.7 276.6 %all-gather.10.cloned.1.call-start = ((), (), s32[]{:S(2)}) async-start(), calls=%async_computation.12 | async-start | bytes 10485760 | tf_op jit(solution)/shard_map/all_gather | solution.py:169
  9.6 49.1 %copy-start.31 = (f32[384]{0:T(512)}, f32[384]{0:T(512)S(1)}, u32[]{:S(2)}) copy-start(f32[384]{0:T(512)S(1)} %broadcast_multiply_fusion.3) | copy-start | bytes 4612
  10.0 48.7 %copy-start.44 = (f32[384]{0:T(512)}, f32[384]{0:T(512)S(1)}, u32[]{:S(2)}) copy-start(f32[384]{0:T(512)S(1)} %fusion.38) | copy-start | bytes 4612
  10.0 48.7 %copy-start.33 = (f32[384]{0:T(512)}, f32[384]{0:T(512)S(1)}, u32[]{:S(2)}) copy-start(f32[384]{0:T(512)S(1)} %fusion.49) | copy-start | bytes 4612
  66.1 55.1 %copy-start.56 = (f32[16]{0:T(128)S(1)}, f32[16]{0:T(128)}, u32[]{:S(2)}) copy-start(f32[16]{0:T(128)} %param.20) | copy-start | bytes 196
  66.1 55.3 %copy-start.55 = (s32[1,384]{1,0:T(1,128)S(1)}, s32[1,384]{1,0:T(1,128)}, u32[]{:S(2)}) copy-start(s32[1,384]{1,0:T(1,128)} %param.17) | copy-start | bytes 4612
  66.1 26.2 %all-to-all-start.2 = ((bf16[384,8,128]{2,0,1:T(8,128)(2,1)}), bf16[384,8,128]{2,0,1:T(8,128)(2,1)S(1)}, u32[]{:S(2)}, u32[]{:S(2)}) async-start(bf16[384,8,128]{2,0,1:T(8,128)(2,1)} %bitcast.264), calls=%async_computation.2 | async-start | bytes 1572864 | tf_op jit(solution)/shard_map/all_to_all | solution.py:153
  92.3 24.0 %all-to-all-start.1 = ((bf16[384,8,128]{2,0,1:T(8,128)(2,1)}), bf16[384,8,128]{2,0,1:T(8,128)(2,1)S(1)}, u32[]{:S(2)}, u32[]{:S(2)}) async-start(bf16[384,8,128]{2,0,1:T(8,128)(2,1)} %bitcast.263), calls=%async_computation.1 | async-start | bytes 1572864 | tf_op jit(solution)/shard_map/all_to_all | solution.py:150
  116.3 47.6 %copy-start.15 = (bf16[384,8,128]{2,0,1:T(8,128)(2,1)}, bf16[384,8,128]{2,0,1:T(8,128)(2,1)S(1)}, u32[]{:S(2)}) copy-start(bf16[384,8,128]{2,0,1:T(8,128)(2,1)S(1)} %all-to-all-done.1) | copy-start | bytes 2359300
  116.3 45.3 %all-to-all-start = ((bf16[384,8,128]{2,0,1:T(8,128)(2,1)}), bf16[384,8,128]{2,0,1:T(8,128)(2,1)}, u32[]{:S(2)}, u32[]{:S(2)}) async-start(bf16[384,8,128]{2,0,1:T(8,128)(2,1)} %bitcast.260), calls=%async_computation | async-start | bytes 1572864 | tf_op jit(solution)/shard_map/all_to_all | solution.py:149
  120.6 177.8 %all-gather.12.cloned.1.call-start = ((), (), s32[]{:S(2)}) async-start(), calls=%async_computation.13 | async-start | bytes 10485760 | tf_op jit(solution)/shard_map/all_gather | solution.py:170
  256.3 23.7 %copy-start.5 = (bf16[3072,2,64]{0,2,1:T(8,128)(2,1)}, bf16[3072,2,64]{0,2,1:T(8,128)(2,1)S(1)}, u32[]{:S(2)}) copy-start(bf16[3072,2,64]{0,2,1:T(8,128)(2,1)S(1)} %get-tuple-element.544) | copy-start | bytes 2359300
  258.2 25.2 %copy-start.39 = (f32[1024]{0:T(1024)S(1)}, f32[1024]{0:T(1024)}, u32[]{:S(2)}) copy-start(f32[1024]{0:T(1024)} %param.22) | copy-start | bytes 12292
  280.1 5.3 copy-start.29
  283.9 40.7 %copy-start.35 = (f32[384]{0:T(512)}, f32[384]{0:T(512)S(1)}, u32[]{:S(2)}) copy-start(f32[384]{0:T(512)S(1)} %broadcast_multiply_fusion.1) | copy-start | bytes 4612
  285.3 39.2 %copy-start.37 = (f32[384]{0:T(512)}, f32[384]{0:T(512)S(1)}, u32[]{:S(2)}) copy-start(f32[384]{0:T(512)S(1)} %fusion.51) | copy-start | bytes 4612
  293.0 5.3 copy-start.17
  293.0 5.3 copy-start.46
  293.0 14.8 copy-start.42
  298.3 9.5 copy-start.50
  298.4 9.5 copy-start.1
  312.0 4.6 copy-start.8
  316.6 7.9 copy-start.12
  327.1 8.5 copy-start.52
  328.3 7.3 copy-start.16
  330.3 22.3 %all-to-all-start.4 = ((bf16[384,8,128]{2,0,1:T(8,128)(2,1)}), bf16[384,8,128]{2,0,1:T(8,128)(2,1)}, u32[]{:S(2)}, u32[]{:S(2)}) async-start(bf16[384,8,128]{2,0,1:T(8,128)(2,1)} %bitcast.160), calls=%async_computation.4 | async-start | bytes 1572864 | tf_op jit(solution)/shard_map/all_to_all | solution.py:188
  368.7 3.8 copy-start.6
  372.6 7.4 copy-start.26
  403.7 7.4 copy-start.26
  434.8 7.4 copy-start.26
  462.0 3.8 copy-start.6
  465.9 7.4 copy-start.26
  496.9 7.4 copy-start.26
  524.2 3.8 copy-start.6
  528.1 7.4 copy-start.26
  547.3 22.7 %all-to-all-start.5 = ((bf16[8,384,128]{2,1,0:T(8,128)(2,1)}), bf16[8,384,128]{2,1,0:T(8,128)(2,1)S(1)}, u32[]{:S(2)}, u32[]{:S(2)}) async-start(bf16[8,384,128]{2,1,0:T(8,128)(2,1)} %bitcast.262), calls=%async_computation.5 | async-start | bytes 1572864 | tf_op jit(solution)/shard_map/all_to_all | solution.py:197
  552.1 46.0 %copy-start.14 = (bf16[384,8,128]{0,2,1:T(8,128)(2,1)S(1)}, bf16[384,8,128]{0,2,1:T(8,128)(2,1)}, u32[]{:S(2)}) copy-start(bf16[384,8,128]{0,2,1:T(8,128)(2,1)} %copy.82) | copy-start | bytes 2359300
  552.1 46.0 %copy-start.53 = (f32[384]{0:T(512)S(1)}, f32[384]{0:T(512)}, u32[]{:S(2)}) copy-start(f32[384]{0:T(512)} %copy-done.52) | copy-start | bytes 4612
  570.0 23.7 %copy-start.22 = (bf16[8,384,128]{2,1,0:T(8,128)(2,1)}, bf16[8,384,128]{2,1,0:T(8,128)(2,1)S(1)}, u32[]{:S(2)}) copy-start(bf16[8,384,128]{2,1,0:T(8,128)(2,1)S(1)} %all-to-all-done.5) | copy-start | bytes 2359300
  570.0 23.7 %all-to-all-start.6 = ((bf16[8,384,128]{1,2,0:T(8,128)(2,1)}), bf16[8,384,128]{1,2,0:T(8,128)(2,1)S(1)}, u32[]{:S(2)}, u32[]{:S(2)}) async-start(bf16[8,384,128]{1,2,0:T(8,128)(2,1)} %copy.90), calls=%async_computation.6 | async-start | bytes 1572864 | tf_op jit(solution)/shard_map/all_to_all | solution.py:200
  593.8 4.3 copy-start.21
  593.8 24.1 %all-to-all-start.7 = ((bf16[8,384,128]{1,2,0:T(8,128)(2,1)}), bf16[8,384,128]{1,2,0:T(8,128)(2,1)}, u32[]{:S(2)}, u32[]{:S(2)}) async-start(bf16[8,384,128]{1,2,0:T(8,128)(2,1)} %copy.91), calls=%async_computation.7 | async-start | bytes 1572864 | tf_op jit(solution)/shard_map/all_to_all | solution.py:203
  598.0 5.0 copy-start.9
  598.0 5.0 copy-start.30
  598.0 4.9 copy-start.36
  598.0 4.9 copy-start.38
  598.0 755.0 %reduce-scatter.3.cloned.1.call-start = ((), (), s32[]{:S(2)}) async-start(), calls=%async_computation.14 | async-start | bytes 34603008 | tf_op jit(solution)/shard_map/reduce_scatter | solution.py:211
  598.1 4.9 copy-start.13
  603.0 8.4 copy-start.23
  603.0 14.8 copy-start.4
  603.0 14.8 copy-start.28
  603.0 14.8 copy-start.32
  603.0 14.8 copy-start.34
  617.9 8.5 copy-start.2
  647.6 1066.2 %reduce-scatter.5.cloned.1.call-start = ((), (), s32[]{:S(2)}) async-start(), calls=%async_computation.15 | async-start | bytes 17301504 | tf_op jit(solution)/shard_map/reduce_scatter | solution.py:224
  683.4 6.6 copy-start.45
  683.4 8.5 copy-start.48
  683.4 8.5 copy-start.49
  683.4 8.5 copy-start.54
  683.4 63.6 %copy-start.11 = (f32[384,1024]{1,0:T(8,128)S(1)}, f32[384,1024]{1,0:T(8,128)}, u32[]{:S(2)}) copy-start(f32[384,1024]{1,0:T(8,128)} %copy-done.10) | copy-start | bytes 4718596
  683.4 63.6 %copy-start.41 = (f32[384]{0:T(512)S(1)}, f32[384]{0:T(512)}, u32[]{:S(2)}) copy-start(f32[384]{0:T(512)} %copy-done.40) | copy-start | bytes 4612
  (21 other events, 42.7 us)
Sparse Core Ops, SparseCore 0:
  9.6 49.0 all-gather.5
  60.3 22.5 all-gather.7
  84.5 58.2 all-gather.9
  144.2 58.2 all-gather.11
  647.7 705.2 reduce-scatter.2
  1355.8 358.0 reduce-scatter.4
where the time goes:
time: 1730 us; the launch traced here: 1720 us
  waiting for transfers between devices  1100 us (64%)
  matrix products  227 us (13%)
  other arithmetic  144 us (8%)
  blocking collectives  116 us (7%)
  local copies, waits for them, and re-layouts  65.7 us (4%)
  starting transfers between devices  29.5 us (2%)
  loops' own time  20.5 us (1%)
    reduce_scatter x1, waiting for transfers between devices, per_device(): lax.psum_scatter(jnp.concatenate((transposed_times(normed_low, grad_tripl...  603 us
    reduce_scatter x1, waiting for transfers between devices, per_device(): lax.psum_scatter(transposed_times(activated_low, upstream), ('dp', 'seq')...  356 us
    unnamed x1, blocking collectives  52.8 us
    all_gather x1, waiting for transfers between devices, per_device(): lax.all_gather(triple_weight, 'dp', axis=0, tiled=True)  48.7 us
    convert_element_type x6, other arithmetic, one_block(): grad_scores = (weights * (grad_weights - row_inner)).astype(jnp.bfloat16)  44.8 us
    dot_general x6, matrix products, one_block(): jnp.einsum('qhd,khd->hqk', grad_block, value_heads, preferred_element_typ...  44.5 us
    all_gather x1, blocking collectives, per_device(): doc_ids = lax.all_gather(segment_ids[0], 'seq', axis=0, tiled=True)  37.1 us
    dot_general x4, matrix products, transposed_times(): lax.dot_general(left, right, (((0,), (0,)), ((), ())), preferred_element_...  36.3 us
  transfers between devices with their start and end apart: 13, of which 9 were waited for; matrix products, arithmetic and copies ran while one was open for 11% of the time, Pallas kernels for 0%

commit v1 on v0

v1 whole, which is shorter than its diff:
```python
import functools
import jax
import jax.numpy as jnp
from jax import lax
from jax.sharding import PartitionSpec as P
from jax.experimental import pallas as pl
from jax.experimental.pallas import tpu as pltpu

HEAD = 64
NEG = -1e30
BQ = 256


def nt(a, b):
    return lax.dot_general(a, b, (((1,), (1,)), ((), ())), preferred_element_type=jnp.float32)


def tn(a, b):
    return lax.dot_general(a, b, (((0,), (0,)), ((), ())), preferred_element_type=jnp.float32)


def stack_heads(block, heads):
    if heads == 1:
        return block
    lane = lax.broadcasted_iota(jnp.int32, block.shape, 1)
    zero = jnp.zeros_like(block)
    return jnp.concatenate(
        [jnp.where((lane >= h * HEAD) & (lane < (h + 1) * HEAD), block, zero) for h in range(heads)],
        axis=0,
    )


def unstack_heads(wide, heads):
    rows = wide.shape[1] // heads
    return jnp.concatenate(
        [wide[h * HEAD : (h + 1) * HEAD, h * rows : (h + 1) * rows] for h in range(heads)], axis=0
    )


def forward_kernel(heads, lo_ref, full_ref, q_ref, k_ref, v_ref, start_ref, scale_ref,
                   o_ref, u_ref, lse_ref, m_s, l_s, acc_s):
    i = pl.program_id(0)
    rows = q_ref.shape[0]
    wide = heads * rows
    queries = stack_heads(q_ref[...] * jnp.bfloat16(HEAD ** -0.5), heads)
    starts = jnp.concatenate([start_ref[0]] * heads, axis=1)
    m_s[...] = jnp.full_like(m_s, NEG)
    l_s[...] = jnp.zeros_like(l_s)
    acc_s[...] = jnp.zeros_like(acc_s)

    def step(j, masked, diagonal):
        at = pl.ds(pl.multiple_of(j * rows, rows), rows)
        scores = nt(k_ref[at, :], queries)
        if masked or diagonal:
            key = j * rows + lax.broadcasted_iota(jnp.int32, scores.shape, 0)
            allowed = key >= starts
            if diagonal:
                lane = lax.broadcasted_iota(jnp.int32, scores.shape, 1) & (rows - 1)
                allowed = allowed & (key <= i * rows + lane)
            scores = jnp.where(allowed, scores, NEG)
        before = m_s[...]
        highest = jnp.maximum(before, jnp.max(scores, axis=0, keepdims=True))
        weights = jnp.exp(scores - highest)
        fade = jnp.exp(before - highest)
        if masked:
            weights = jnp.where(scores > 0.5 * NEG, weights, 0.0)
        m_s[...] = highest
        l_s[...] = l_s[...] * fade + jnp.sum(weights, axis=0, keepdims=True)
        acc_s[...] = acc_s[...] * fade + tn(v_ref[at, :], weights.astype(jnp.bfloat16))

    step(i, False, True)
    full = jnp.minimum(full_ref[i], i)

    def plain(j, carry):
        step(j, False, False)
        return carry

    def edge(j, carry):
        step(j, True, False)
        return carry

    lax.fori_loop(full, i, plain, 0)
    lax.fori_loop(lo_ref[i], full, edge, 0)
    total = l_s[...]
    out = unstack_heads(acc_s[...] / total, heads).T
    o_ref[...] = out
    u_ref[...] = (out * scale_ref[...]).astype(jnp.bfloat16)
    lse_ref[0] = m_s[...] + jnp.log(total)


def attend_forward(queries, keys, values, bounds, starts, scale_wide):
    length, width = queries.shape
    heads = width // HEAD
    blocks = length // BQ
    whole = pl.BlockSpec((length, width), lambda i, *_: (0, 0))
    mine = pl.BlockSpec((BQ, width), lambda i, *_: (i, 0))
    return pl.pallas_call(
        functools.partial(forward_kernel, heads),
        out_shape=(
            jax.ShapeDtypeStruct((length, width), jnp.float32),
            jax.ShapeDtypeStruct((length, width), jnp.bfloat16),
            jax.ShapeDtypeStruct((blocks, 1, heads * BQ), jnp.float32),
        ),
        grid_spec=pltpu.PrefetchScalarGridSpec(
            num_scalar_prefetch=2,
            grid=(blocks,),
            in_specs=[
                mine,
                whole,
                whole,
                pl.BlockSpec((1, 1, BQ), lambda i, *_: (i, 0, 0)),
                pl.BlockSpec((1, width), lambda i, *_: (0, 0)),
            ],
            out_specs=(mine, mine, pl.BlockSpec((1, 1, heads * BQ), lambda i, *_: (i, 0, 0))),
            scratch_shapes=[
                pltpu.VMEM((1, heads * BQ), jnp.float32),
                pltpu.VMEM((1, heads * BQ), jnp.float32),
                pltpu.VMEM((width, heads * BQ), jnp.float32),
            ],
        ),
        cost_estimate=pl.CostEstimate(
            flops=length * length * width, bytes_accessed=16 * length * width, transcendentals=0
        ),
        name="attend_forward",
    )(bounds[0], bounds[1], queries, keys, values, starts.reshape(blocks, 1, BQ), scale_wide)


def backward_kernel(heads, hi_ref, full_ref, q_ref, k_ref, v_ref, o_ref, du_ref, start_ref, scale_ref, lse_ref,
                    dq_ref, dk_ref, dv_ref, ds_ref, qs_s, dos_s, delta_s, dqt_s, dk_s, dv_s):
    j = pl.program_id(0)
    rows = k_ref.shape[0]
    blocks = qs_s.shape[0]
    wide = heads * rows

    @pl.when(j == 0)
    def prepare():
        def one(i, total):
            at = pl.ds(pl.multiple_of(i * rows, rows), rows)
            qs_s[i] = stack_heads(q_ref[at, :] * jnp.bfloat16(HEAD ** -0.5), heads)
            grad = du_ref[at, :].astype(jnp.float32)
            out = o_ref[at, :]
            low = (grad * scale_ref[...]).astype(jnp.bfloat16)
            dos_s[i] = stack_heads(low, heads)
            inner = (low.astype(jnp.float32) * out).T
            delta_s[i] = jnp.concatenate(
                [jnp.sum(inner[h * HEAD : (h + 1) * HEAD], axis=0, keepdims=True) for h in range(heads)],
                axis=1,
            )
            return total + jnp.sum(grad * out, axis=0, keepdims=True)

        ds_ref[...] = lax.fori_loop(0, blocks, one, jnp.zeros(ds_ref.shape, jnp.float32))
        dqt_s[...] = jnp.zeros_like(dqt_s)

    keys, values = k_ref[...], v_ref[...]
    dk_s[...] = jnp.zeros_like(dk_s)
    dv_s[...] = jnp.zeros_like(dv_s)

    def step(i, masked, diagonal):
        queries, grads = qs_s[i], dos_s[i]
        scores = nt(keys, queries)
        if masked or diagonal:
            key = j * rows + lax.broadcasted_iota(jnp.int32, scores.shape, 0)
            starts = jnp.concatenate([start_ref[i]] * heads, axis=1)
            allowed = key >= starts
            if diagonal:
                lane = lax.broadcasted_iota(jnp.int32, scores.shape, 1) & (rows - 1)
                allowed = allowed & (key <= i * rows + lane)
            scores = jnp.where(allowed, scores, NEG)
        weights = jnp.exp(scores - lse_ref[i])
        pulls = nt(values, grads)
        low = (weights * (pulls - delta_s[i])).astype(jnp.bfloat16)
        dv_s[...] += jnp.dot(weights.astype(jnp.bfloat16), grads, preferred_element_type=jnp.float32)
        dk_s[...] += jnp.dot(low, queries, preferred_element_type=jnp.float32)
        dqt_s[i] += tn(keys, low)

    step(j, False, True)
    full = jnp.maximum(full_ref[j], j + 1)

    def plain(i, carry):
        step(i, False, False)
        return carry

    def edge(i, carry):
        step(i, True, False)
        return carry

    lax.fori_loop(j + 1, full, plain, 0)
    lax.fori_loop(full, hi_ref[j], edge, 0)
    dk_ref[...] = dk_s[...].astype(jnp.bfloat16)
    dv_ref[...] = dv_s[...].astype(jnp.bfloat16)

    @pl.when(j == blocks - 1)
    def finish():
        def one(i, carry):
            at = pl.ds(pl.multiple_of(i * rows, rows), rows)
            dq_ref[at, :] = (unstack_heads(dqt_s[i], heads).T * HEAD ** -0.5).astype(jnp.bfloat16)
            return carry

        lax.fori_loop(0, blocks, one, 0)


def attend_backward(queries, keys, values, outs, grads, bounds, starts, scale_wide, logsum):
    length, width = queries.shape
    heads = width // HEAD
    blocks = length // BQ
    whole = pl.BlockSpec((length, width), lambda i, *_: (0, 0))
    mine = pl.BlockSpec((BQ, width), lambda i, *_: (i, 0))
    return pl.pallas_call(
        functools.partial(backward_kernel, heads),
        out_shape=(jax.ShapeDtypeStruct((length, width), jnp.bfloat16),) * 3
        + (jax.ShapeDtypeStruct((1, width), jnp.float32),),
        grid_spec=pltpu.PrefetchScalarGridSpec(
            num_scalar_prefetch=2,
            grid=(blocks,),
            in_specs=[
                whole,
                mine,
                mine,
                whole,
                whole,
                pl.BlockSpec((blocks, 1, BQ), lambda i, *_: (0, 0, 0)),
                pl.BlockSpec((1, width), lambda i, *_: (0, 0)),
                pl.BlockSpec((blocks, 1, heads * BQ), lambda i, *_: (0, 0, 0)),
            ],
            out_specs=(whole, mine, mine, pl.BlockSpec((1, width), lambda i, *_: (0, 0))),
            scratch_shapes=[
                pltpu.VMEM((blocks, heads * BQ, width), jnp.bfloat16),
                pltpu.VMEM((blocks, heads * BQ, width), jnp.bfloat16),
                pltpu.VMEM((blocks, 1, heads * BQ), jnp.float32),
                pltpu.VMEM((blocks, width, heads * BQ), jnp.float32),
                pltpu.VMEM((BQ, width), jnp.float32),
                pltpu.VMEM((BQ, width), jnp.float32),
            ],
        ),
        cost_estimate=pl.CostEstimate(
            flops=3 * length * length * width, bytes_accessed=32 * length * width, transcendentals=0
        ),
        name="attend_backward",
    )(bounds[2], bounds[3], queries, keys, values, outs, grads, starts.reshape(blocks, 1, BQ), scale_wide, logsum)


def document_bounds(doc_ids):
    length = doc_ids.shape[0]
    blocks = length // BQ
    counts = jnp.sum(doc_ids[None, :] < jnp.arange(8, dtype=jnp.int32)[:, None], axis=1, dtype=jnp.int32)
    starts = jnp.sum(
        jnp.where(doc_ids[:, None] == jnp.arange(8, dtype=jnp.int32)[None, :], counts[None, :], 0), axis=1, dtype=jnp.int32
    )
    by_block = starts.reshape(blocks, BQ)
    low = by_block[:, 0] // BQ
    full = (by_block[:, BQ - 1] + BQ - 1) // BQ
    index = jnp.arange(blocks, dtype=jnp.int32)
    high = jnp.sum(low[None, :] <= index[:, None], axis=1, dtype=jnp.int32)
    full_high = jnp.sum(full[None, :] <= index[:, None], axis=1, dtype=jnp.int32)
    return (low, full, high, full_high), starts


def layer_norm(values, gains):
    center = values - jnp.mean(values, axis=-1, keepdims=True)
    spread = jnp.mean(center * center, axis=-1, keepdims=True)
    return center * lax.rsqrt(spread + 1e-05) * gains


def gelu_norm(hidden, gains):
    return layer_norm(jax.nn.gelu(hidden, approximate=True), gains)


def transposed_times(left, right):
    return lax.dot_general(
        left, right, (((0,), (0,)), ((), ())), preferred_element_type=jnp.float32
    )


def times_transposed(left, right):
    return lax.dot_general(
        left, right, (((1,), (1,)), ((), ())), preferred_element_type=jnp.float32
    )


def scatter_rows(partial, sizes):
    current = partial
    for axis, size in zip(("dp", "seq"), sizes):
        place = lax.axis_index(axis)
        bits = size.bit_length() - 1
        pieces = current.reshape((2,) * bits + (-1, current.shape[-1]))
        for bit in range(bits):
            at = bits - 1 - bit
            mine = (place >> bit) & 1
            give = lax.dynamic_index_in_dim(pieces, 1 - mine, at, keepdims=False)
            keep = lax.dynamic_index_in_dim(pieces, mine, at, keepdims=False)
            got = lax.ppermute(give, axis, [(i, i ^ (1 << bit)) for i in range(size)])
            pieces = (keep.astype(jnp.float32) + got.astype(jnp.float32)).astype(jnp.bfloat16)
        current = pieces
    return current.astype(jnp.float32)


def per_device(
    sizes,
    tokens,
    segment_ids,
    first_gain,
    triple_weight,
    head_scale,
    output_weight,
    post_gain,
    second_gain,
    up_weight,
    mid_gain,
    down_weight,
    cotangent,
):
    inputs = tokens[0].astype(jnp.float32)
    width = inputs.shape[1]
    doc_ids = lax.all_gather(segment_ids[0], "seq", axis=0, tiled=True)
    triple_full, output_full = (
        lax.all_gather(triple_weight, "dp", axis=0, tiled=True),
        lax.all_gather(output_weight, "dp", axis=0, tiled=True),
    )
    normed, pull_first = jax.vjp(layer_norm, inputs, first_gain)
    normed_low = normed.astype(jnp.bfloat16)
    triple = jnp.dot(normed_low, triple_full, preferred_element_type=jnp.float32).astype(
        jnp.bfloat16
    )
    queries, keys_all, values_all = (
        lax.all_to_all(triple[:, :width], "seq", split_axis=1, concat_axis=0, tiled=True),
        lax.all_to_all(
            triple[:, width : 2 * width], "seq", split_axis=1, concat_axis=0, tiled=True
        ),
        lax.all_to_all(triple[:, 2 * width :], "seq", split_axis=1, concat_axis=0, tiled=True),
    )
    heads_here = queries.shape[1] // HEAD
    own_scale = lax.dynamic_slice_in_dim(
        head_scale, lax.axis_index("seq") * heads_here, heads_here, 0
    )
    scale_wide = jnp.repeat(own_scale, HEAD)[None]
    bounds, starts = document_bounds(doc_ids)
    attended, scaled, logsum = attend_forward(
        queries, keys_all, values_all, bounds, starts, scale_wide
    )
    merged = lax.all_to_all(scaled, "seq", split_axis=0, concat_axis=1, tiled=True)
    projected = jnp.dot(merged, output_full, preferred_element_type=jnp.float32)
    post_normed, pull_post = jax.vjp(layer_norm, projected, post_gain)
    middle = inputs + post_normed
    second, pull_second = jax.vjp(layer_norm, middle, second_gain)
    second_low = second.astype(jnp.bfloat16)
    feed_up, feed_down = (
        lax.all_gather(up_weight, "dp", axis=0, tiled=True),
        lax.all_gather(down_weight, "dp", axis=0, tiled=True),
    )
    hidden = jnp.dot(second_low, feed_up, preferred_element_type=jnp.float32)
    activated, pull_mid = jax.vjp(gelu_norm, hidden, mid_gain)
    activated_low = activated.astype(jnp.bfloat16)
    layer_out = (
        middle + jnp.dot(activated_low, feed_down, preferred_element_type=jnp.float32)
    ).astype(jnp.bfloat16)
    upstream = cotangent[0]
    grad_act = times_transposed(upstream, feed_down)
    grad_hidden, grad_mid = pull_mid(grad_act)
    grad_hidden_low = grad_hidden.astype(jnp.bfloat16)
    grad_second_in = times_transposed(grad_hidden_low, feed_up)
    grad_middle_part, grad_second = pull_second(grad_second_in)
    grad_middle = upstream.astype(jnp.float32) + grad_middle_part
    grad_projected, grad_post = pull_post(grad_middle)
    grad_projected_low = grad_projected.astype(jnp.bfloat16)
    grad_merged = times_transposed(grad_projected_low, output_full).astype(jnp.bfloat16)
    grad_scaled = lax.all_to_all(
        grad_merged, "seq", split_axis=1, concat_axis=0, tiled=True
    )
    grad_queries, grad_keys, grad_values, scale_lanes = attend_backward(
        queries, keys_all, values_all, attended, grad_scaled, bounds, starts, scale_wide, logsum
    )
    scale_terms = jnp.sum(scale_lanes.reshape(heads_here, HEAD), axis=1)
    back_queries, back_keys, back_values = (
        lax.all_to_all(
            grad_queries.astype(jnp.bfloat16), "seq", split_axis=0, concat_axis=1, tiled=True
        ),
        lax.all_to_all(
            grad_keys.astype(jnp.bfloat16), "seq", split_axis=0, concat_axis=1, tiled=True
        ),
        lax.all_to_all(
            grad_values.astype(jnp.bfloat16), "seq", split_axis=0, concat_axis=1, tiled=True
        ),
    )
    grad_triple_act = jnp.concatenate((back_queries, back_keys, back_values), axis=1)
    grad_normed = times_transposed(grad_triple_act, triple_full)
    grad_input_part, grad_first = pull_first(grad_normed)
    grad_tokens = (grad_middle + grad_input_part).astype(jnp.bfloat16)
    low = jnp.bfloat16
    grad_down = scatter_rows(transposed_times(activated_low, upstream).astype(low), sizes)
    grad_up = scatter_rows(transposed_times(second_low, grad_hidden_low).astype(low), sizes)
    grad_output = scatter_rows(transposed_times(merged, grad_projected_low).astype(low), sizes)
    gains = jnp.concatenate(
        (
            grad_first[:, None],
            grad_post[:, None],
            grad_second[:, None],
            grad_mid.reshape(width, -1),
        ),
        axis=1,
    )
    gains = jnp.pad(gains, ((0, 0), (0, 128 - gains.shape[1])))
    grad_triple = scatter_rows(
        jnp.concatenate(
            (transposed_times(normed_low, grad_triple_act).astype(low), gains.astype(low)), axis=1
        ),
        sizes,
    )
    gain_sums = grad_triple[:, 3 * width :]
    grad_scale = lax.psum(scale_terms, "dp")
    return (
        layer_out[None],
        grad_tokens[None],
        gain_sums[:, 0],
        grad_triple[:, : 3 * width],
        grad_scale,
        grad_output,
        gain_sums[:, 1],
        gain_sums[:, 2],
        grad_up,
        gain_sums[:, 3 : 3 + mid_gain.shape[0] // width].reshape(-1),
        grad_down,
    )


def solution(mesh):
    placed = (
        P("dp", "seq", None),
        P("dp", "seq"),
        P(),
        P("dp", None),
        P(),
        P("dp", None),
        P(),
        P(),
        P("dp", None),
        P(),
        P("dp", None),
        P("dp", "seq", None),
    )
    return jax.shard_map(
        functools.partial(per_device, (mesh.shape["dp"], mesh.shape["seq"])),
        mesh=mesh,
        in_specs=placed,
        out_specs=(
            P("dp", "seq", None),
            P("dp", "seq", None),
            P(("dp", "seq")),
            P(("dp", "seq"), None),
            P("seq"),
            P(("dp", "seq"), None),
            P(("dp", "seq")),
            P(("dp", "seq")),
            P(("dp", "seq"), None),
            P(("dp", "seq")),
            P(("dp", "seq"), None),
        ),
        check_vma=False,
    )
```

time: 1730 us -> 634 us (0.37)
  waiting for transfers between devices: 1100 us -> 250 us
  matrix products: 227 us -> 73.5 us
  other arithmetic: 144 us -> 53.4 us
  Pallas kernels: 0 us -> 54.5 us
  blocking collectives: 116 us -> 81.6 us
  starting transfers between devices: 29.5 us -> 52.7 us
  loops' own time: 20.5 us -> 0 us
    reduce_scatter x2 -> x0, waiting for transfers between devices: 958 us -> none  [the longest x1 603 us: per_device(): lax.psum_scatter(jnp.concatenate((transposed_times(normed_low, grad_tripl...]
    dot_general x42 -> x0, matrix products: 138 us -> none  [the longest x6 44.5 us: one_block(): jnp.einsum('qhd,khd->hqk', grad_block, value_heads, preferred_element_typ...]
    ppermute x0 -> x20, waiting for transfers between devices: none -> 115 us  [scatter_rows(): got = lax.ppermute(give, axis, [(i, i ^ 1 << bit) for i in range(size)])]
    pallas_call x0 -> x2, Pallas kernels: none -> 54.5 us  [the longest x1 28.2 us: attend_backward(): pl.pallas_call(functools.partial(backward_kernel, heads), out_shape=(jax....]
    unnamed x1 -> x0, blocking collectives: 52.8 us -> none
    psum x1, blocking collectives: 6.79 us -> 43 us  [per_device(): grad_scale = lax.psum(scale_terms, 'dp')]
    convert_element_type x11 -> x20, other arithmetic: 53.1 us -> 28.5 us  [the longest x16 25.2 us: scatter_rows(): (keep.astype(jnp.float32) + got.astype(jnp.float32)).astype(jnp.bfloat16)]
    and x12 -> x0, other arithmetic: 24.3 us -> none  [block_scores(): (query_docs[:, None] == doc_ids[None, :]) & (query_pos[:, None] >= positi...]
  transfers between devices with their start and end apart: 13 -> 32, of which waited for: 9 -> 14; matrix products, arithmetic and copies ran while one was open for 11% -> 20% of each run, Pallas kernels for 0% -> 4%
where the time goes in v1:
time: 634 us; the launch traced here: 630 us
  waiting for transfers between devices  250 us (39%)
  blocking collectives  81.6 us (13%)
  matrix products  73.5 us (12%)
  Pallas kernels  54.5 us (9%)
  other arithmetic  53.4 us (8%)
  starting transfers between devices  52.7 us (8%)
  local copies, waits for them, and re-layouts  49.6 us (8%)
  between operations  15 us (2%)
    ppermute x20, waiting for transfers between devices, scatter_rows(): got = lax.ppermute(give, axis, [(i, i ^ 1 << bit) for i in range(size)])  115 us
    all_gather x1, waiting for transfers between devices, per_device(): lax.all_gather(triple_weight, 'dp', axis=0, tiled=True)  48.1 us
    psum x1, blocking collectives, per_device(): grad_scale = lax.psum(scale_terms, 'dp')  43 us
    all_gather x1, blocking collectives, per_device(): doc_ids = lax.all_gather(segment_ids[0], 'seq', axis=0, tiled=True)  38.6 us
    pallas_call x1, Pallas kernels, attend_backward(): pl.pallas_call(functools.partial(backward_kernel, heads), out_shape=(jax....  28.2 us
    dot_general x4, matrix products, transposed_times(): lax.dot_general(left, right, (((0,), (0,)), ((), ())), preferred_element_...  28.2 us
    pallas_call x1, Pallas kernels, attend_forward(): pl.pallas_call(functools.partial(forward_kernel, heads), out_shape=(jax.S...  26.3 us
    convert_element_type x16, other arithmetic, scatter_rows(): (keep.astype(jnp.float32) + got.astype(jnp.float32)).astype(jnp.bfloat16)  25.2 us
  transfers between devices with their start and end apart: 32, of which 14 were waited for; matrix products, arithmetic and copies ran while one was open for 20% of the time, Pallas kernels for 4%

profile of v1, /device:TPU:0, one launch (start us, length us, event | category | flops | bytes accessed | tf_op | source)
XLA Modules:
  0.0 630.1 jit_solution(7152415889343649899)
XLA Ops:
  10.6 48.1 %all-gather.6.cloned.1.call-done = bf16[1024,3072]{1,0:T(8,128)(2,1)} async-done(((bf16[256,3072]{1,0:T(8,128)(2,1)}), bf16[1024,3072]{1,0:T(8,128)(2,1)}) %all-gather.6.cloned.1.call-update) | async-done | bytes 6291472 | tf_op jit(solution)/shard_map/all_gather | solution.py:316
  58.7 5.8 convolution_convert_fusion.3
  66.0 5.5 all-to-all-start
  72.6 19.5 %all-to-all-done = bf16[384,8,128]{2,0,1:T(8,128)(2,1)S(1)} async-done(((bf16[384,8,128]{2,0,1:T(8,128)(2,1)}), bf16[384,8,128]{2,0,1:T(8,128)(2,1)S(1)}, u32[]{:S(2)}, u32[]{:S(2)}) %all-to-all-start) | async-done | bytes 786464 | tf_op jit(solution)/shard_map/all_to_all | solution.py:325
  92.1 3.6 all-to-all-start.1
  96.8 19.3 %all-to-all-done.1 = bf16[384,8,128]{2,0,1:T(8,128)(2,1)S(1)} async-done(((bf16[384,8,128]{2,0,1:T(8,128)(2,1)}), bf16[384,8,128]{2,0,1:T(8,128)(2,1)S(1)}, u32[]{:S(2)}, u32[]{:S(2)}) %all-to-all-start.1) | async-done | bytes 786464 | tf_op jit(solution)/shard_map/all_to_all | solution.py:326
  116.1 3.5 all-to-all-start.2
  119.7 38.6 %all-gather = s32[1,3072]{1,0:T(1,128)S(1)} all-gather(s32[1,384]{1,0:T(1,128)S(1)} %copy-done.47), channel_id=2, replica_groups=mesh['dp'=4,'seq'=8] {'seq'}, dimensions={1}, use_global_device_ids=true | all-gather | bytes 13824 | tf_op jit(solution)/shard_map/all_gather | solution.py:314
  161.5 26.3 %attend_forward.1 = (f32[3072,128]{1,0:T(8,128)}, bf16[3072,128]{1,0:T(8,128)(2,1)}, f32[12,1,512]{2,1,0:T(1,128)}) custom-call(s32[12]{0:T(128)} %and_select_fusion.1.lo_ref, s32[12]{0:T(128)} %and_select_fusion.full_ref, bf16[3072,128]{1,0:T(8,128)(2,1)} %bitcast.256, bf16[3072,128]{1,0:T(8,128)(2,1)} %bitcast.258, bf16[3072,128]{1,0:T(8,128)(2,1)} %bitcast.260, ...), custom_call_target="tpu_custom_call" | custom-call | flops 1207959552 | bytes 6291456 | tf_op jit(solution)/shard_map/attend_forward/pallas_call | solution.py:97
  187.8 2.4 copy.74
  190.1 4.1 all-to-all-start.3
  194.2 16.1 %all-to-all-done.3 = bf16[8,384,128]{1,2,0:T(8,128)(2,1)S(1)} async-done(((bf16[8,384,128]{1,2,0:T(8,128)(2,1)}), bf16[8,384,128]{1,2,0:T(8,128)(2,1)S(1)}, u32[]{:S(2)}, u32[]{:S(2)}) %all-to-all-start.3) | async-done | bytes 786464 | tf_op jit(solution)/shard_map/all_to_all | solution.py:340
  210.3 3.0 fusion.74
  215.6 7.7 %fusion.68 = (f32[384]{0:T(512)S(1)}, f32[384,4096]{1,0:T(8,128)S(1)}) fusion(bf16[1024,4096]{1,0:T(8,128)(2,1)} %all-gather.10.cloned.1.call-done, f32[384,1024]{1,0:T(8,128)} %copy-done.7, f32[1024]{0:T(1024)S(1)} %copy-done.46, f32[384]{0:T(512)S(1)} %fusion.60, f32[384]{0:T(512)S(1)} %broadcast_multiply_fusion.1), kind=kOutput, calls=%fused_computation.183 | convolution fusion | flops 3236953600 | bytes 16261632 | tf_op jit(solution)/shard_map/dot_general | solution.py:350
  223.3 2.7 copy-done
  226.0 2.6 multiply_reduce_fusion.2
  228.7 8.9 %multiply_reduce_fusion = (bf16[4096]{0:T(1024)(128)(2,1)S(1)}, f32[384]{0:T(512)S(1)}, f32[384,4096]{1,0:T(8,128)S(1)}) fusion(f32[384]{0:T(512)S(1)} %fusion.61, f32[384]{0:T(512)S(1)} %broadcast_multiply_fusion, f32[384,4096]{1,0:T(8,128)} %copy-done, f32[4096]{0:T(1024)S(1)} %copy-done.39, bf16[4096,1024]{1,0:T(8,128)(2,1)} %all-gather.12.cloned.1.call-done, ...), kind=kOutput, calls=%fused_computation.19 | convolution fusion | flops 3244813824 | bytes 21787136 | tf_op jit(solution)/shard_map/dot_general | solution.py:275
  237.6 4.1 fusion.71
  241.7 4.6 fusion.9
  246.3 1.6 copy-done.17
  248.0 6.3 %multiply_reduce_fusion.3 = (bf16[1024]{0:T(1024)(128)(2,1)S(1)}, f32[384]{0:T(512)S(1)}, f32[384,1024]{1,0:T(8,128)S(1)}) fusion(f32[384,1024]{1,0:T(8,128)S(1)} %copy-done.8, f32[384]{0:T(512)S(1)} %fusion.60, f32[384]{0:T(512)S(1)} %broadcast_multiply_fusion.1, f32[1024]{0:T(1024)S(1)} %copy-done.46, bf16[384,4096]{1,0:T(8,128)(2,1)S(1)} %fusion.9, ...), kind=kOutput, calls=%fused_computation.65 | convolution fusion | flops 3223976448 | bytes 14690816 | tf_op jit(solution)/shard_map/dot_general | solution.py:275
  259.8 3.5 all-to-all-start.4
  264.0 17.5 %all-to-all-done.4 = bf16[384,8,128]{2,0,1:T(8,128)(2,1)S(1)} async-done(((bf16[384,8,128]{2,0,1:T(8,128)(2,1)}), bf16[384,8,128]{2,0,1:T(8,128)(2,1)S(1)}, u32[]{:S(2)}, u32[]{:S(2)}) %all-to-all-start.4) | async-done | bytes 786464 | tf_op jit(solution)/shard_map/all_to_all | solution.py:366
  282.5 28.2 %attend_backward.1 = (bf16[3072,128]{1,0:T(8,128)(2,1)}, bf16[3072,128]{1,0:T(8,128)(2,1)}, bf16[3072,128]{1,0:T(8,128)(2,1)}, f32[1,128]{1,0:T(1,128)}) custom-call(s32[12]{0:T(128)} %get-tuple-element.58.hi_ref, s32[12]{0:T(128)} %get-tuple-element.57.full_ref, bf16[3072,128]{1,0:T(8,128)(2,1)} %bitcast.257, bf16[3072,128]{1,0:T(8,128)(2,1)} %bitcast.259, ...), custom_call_target="tpu_custom_call" | custom-call | flops 3623878656 | bytes 12582912 | tf_op jit(solution)/shard_map/attend_backward/pallas_call | solution.py:208
  310.7 2.3 copy.78
  313.0 4.2 all-to-all-start.7
  317.2 2.7 convolution_convert_fusion.4
  322.3 2.3 copy.77
  324.6 11.2 %all-to-all-done.7 = bf16[8,384,128]{1,2,0:T(8,128)(2,1)} async-done(((bf16[8,384,128]{1,2,0:T(8,128)(2,1)}), bf16[8,384,128]{1,2,0:T(8,128)(2,1)}, u32[]{:S(2)}, u32[]{:S(2)}) %all-to-all-start.7) | async-done | bytes 786464 | tf_op jit(solution)/shard_map/all_to_all | solution.py:380
  335.9 4.2 all-to-all-start.6
  340.1 7.1 %convolution_convert_fusion.1 = bf16[1024,4096]{1,0:T(8,128)(2,1)S(1)} fusion(bf16[384,4096]{1,0:T(8,128)(2,1)} %copy-done.17, f32[384,1024]{1,0:T(8,128)S(1)} %copy-done.9, f32[1024]{0:T(1024)S(1)} %copy-done.46, f32[384]{0:T(512)S(1)} %fusion.60, f32[384]{0:T(512)S(1)} %broadcast_multiply_fusion.1), kind=kOutput, calls=%fused_computation.8 | convolution fusion | flops 3226992640 | bytes 13114368 | tf_op jit(solution)/shard_map/dot_general | solution.py:269
  347.2 2.4 fusion.15
  350.7 2.6 dynamic-slice_bitcast_fusion.1
  354.4 8.6 %collective-permute-done.6 = bf16[256,1024]{1,0:T(8,128)(2,1)} collective-permute-done((bf16[256,1024]{1,0:T(8,128)(2,1)}, bf16[256,1024]{1,0:T(8,128)(2,1)}, u32[]{:S(2)}, u32[]{:S(2)}) %collective-permute-start.6) | collective-permute-done | bytes 524320 | tf_op jit(solution)/shard_map/ppermute | solution.py:291
  364.5 1.8 collective-permute-start.7
  366.3 4.8 all-to-all-start.5
  371.1 12.3 %convolution_convert_fusion = bf16[4096,1024]{1,0:T(8,128)(2,1)} fusion(bf16[1,384,1024]{2,1,0:T(8,128)(2,1)S(1)} %copy-done.14, f32[4096]{0:T(1024)S(1)} %copy-done.39, f32[384]{0:T(512)S(1)} %fusion.61, f32[384]{0:T(512)S(1)} %broadcast_multiply_fusion, f32[384,4096]{1,0:T(8,128)} %copy-done), kind=kOutput, calls=%fused_computation.7 | convolution fusion | flops 3244294144 | bytes 15485952 | tf_op jit(solution)/shard_map/dot_general | solution.py:269
  386.8 2.1 collective-permute-start.8
  388.9 4.7 dynamic-slice_bitcast_fusion
  394.1 1.8 reduce.14
  400.2 2.4 collective-permute-start.9
  402.6 6.3 %fusion.28 = (f32[384]{0:T(512)S(1)}, f32[384,1024]{1,0:T(8,128)S(1)}) fusion(bf16[1,384,1024]{2,1,0:T(8,128)(2,1)S(1)} %copy-done.4, f32[1024]{0:T(1024)} %param.14, f32[384]{0:T(512)S(1)} %broadcast_multiply_fusion.3, bf16[1024,3072]{1,0:T(8,128)(2,1)} %all-gather.6.cloned.1.call-done, bf16[384,1024]{0,1:T(8,128)(2,1)} %bitcast.27, ...), kind=kOutput, calls=%fused_computation.64 | convolution fusion | flops 2424962560 | bytes 11017216 | tf_op jit(solution)/shard_map/dot_general | solution.py:275
  410.6 6.2 convolution_convert_fusion.2
  417.3 2.8 copy-done.2
  420.1 1.9 dynamic-slice_bitcast_fusion.2
  422.2 5.8 fusion.1
  428.0 2.0 copy-done.5
  432.2 6.3 %fusion.29 = bf16[1,384,1024]{2,1,0:T(8,128)(2,1)} fusion(f32[384,1024]{1,0:T(8,128)S(1)} %copy-done.10, bf16[4096,1024]{1,0:T(8,128)(2,1)S(1)} %bitcast.272, f32[4096]{0:T(1024)S(1)} %copy-done.40, f32[384]{0:T(512)S(1)} %copy-done.45, f32[384]{0:T(512)S(1)} %broadcast_multiply_fusion, f32[384,4096]{1,0:T(8,128)S(1)} %bitcast.235), kind=kOutput, calls=%fused_computation.77 | convolution fusion | flops 3240886272 | bytes 17058816 | tf_op jit(solution)/shard_map/dot_general | solution.py:354
  438.5 43.0 %psum.7 = f32[2]{0:T(128)} all-reduce(f32[2]{0:T(128)S(1)} %copy-done.50), channel_id=1, replica_groups=mesh['dp'=4,'seq'=8] {'dp'}, use_global_device_ids=true, to_apply=%region_25.26 | all-reduce | flops 2 | bytes 16 | tf_op jit(solution)/shard_map/psum | solution.py:409
  483.1 3.0 fusion.36
  486.1 5.7 fusion
  492.0 1.8 collective-permute-start.16
  493.8 2.4 fusion.11
  496.3 1.5 collective-permute-start.12
  497.9 2.8 fusion.2
  501.4 39.2 %collective-permute-done.16 = bf16[1024,1024]{1,0:T(8,128)(2,1)S(1)} collective-permute-done((bf16[1024,1024]{1,0:T(8,128)(2,1)S(1)}, bf16[1024,1024]{1,0:T(8,128)(2,1)S(1)}, u32[]{:S(2)}, u32[]{:S(2)}) %collective-permute-start.16) | collective-permute-done | bytes 2097184 | tf_op jit(solution)/shard_map/ppermute | solution.py:291
  541.7 1.5 collective-permute-start.17
  544.2 19.8 %collective-permute-done.17 = bf16[2,2,128,1024]{3,2,1,0:T(8,128)(2,1)S(1)} collective-permute-done((bf16[2,2,128,1024]{3,2,1,0:T(8,128)(2,1)S(1)}, bf16[2,2,128,1024]{3,2,1,0:T(8,128)(2,1)S(1)}, u32[]{:S(2)}, u32[]{:S(2)}) %collective-permute-start.17) | collective-permute-done | bytes 1048608 | tf_op jit(solution)/shard_map/ppermute | solution.py:291
  565.2 9.1 %collective-permute-done.1 = bf16[256,3200]{1,0:T(8,128)(2,1)S(1)} collective-permute-done((bf16[256,3200]{1,0:T(8,128)(2,1)S(1)}, bf16[256,3200]{1,0:T(8,128)(2,1)S(1)}, u32[]{:S(2)}, u32[]{:S(2)}) %collective-permute-start.1) | collective-permute-done | bytes 1638432 | tf_op jit(solution)/shard_map/ppermute | solution.py:291
  574.8 1.5 collective-permute-start.2
  577.3 2.4 collective-permute-start.19
  579.8 13.9 %collective-permute-done.2 = bf16[2,2,32,3200]{3,2,1,0:T(8,128)(2,1)S(1)} collective-permute-done((bf16[2,2,32,3200]{3,2,1,0:T(8,128)(2,1)S(1)}, bf16[2,2,32,3200]{3,2,1,0:T(8,128)(2,1)S(1)}, u32[]{:S(2)}, u32[]{:S(2)}) %collective-permute-start.2) | collective-permute-done | bytes 819232 | tf_op jit(solution)/shard_map/ppermute | solution.py:291
  596.3 13.3 %collective-permute-done.3 = bf16[2,32,3200]{2,1,0:T(8,128)(2,1)S(1)} collective-permute-done((bf16[2,32,3200]{2,1,0:T(8,128)(2,1)S(1)}, bf16[2,32,3200]{2,1,0:T(8,128)(2,1)S(1)}, u32[]{:S(2)}, u32[]{:S(2)}) %collective-permute-start.3) | collective-permute-done | bytes 409632 | tf_op jit(solution)/shard_map/ppermute | solution.py:291
  610.7 10.4 %collective-permute-done.4 = bf16[32,3200]{1,0:T(8,128)(2,1)S(1)} collective-permute-done((bf16[32,3200]{1,0:T(8,128)(2,1)S(1)}, bf16[32,3200]{1,0:T(8,128)(2,1)S(1)}, u32[]{:S(2)}, u32[]{:S(2)}) %collective-permute-start.4) | collective-permute-done | bytes 204832 | tf_op jit(solution)/shard_map/ppermute | solution.py:291
  (241 shorter events, 51.3 us)
Async XLA Ops:
  7.2 51.5 %all-gather.6.cloned.1.call-start = ((), (), s32[]{:S(2)}) async-start(), calls=%async_computation.8 | async-start | bytes 7864320 | tf_op jit(solution)/shard_map/all_gather | solution.py:316
  7.9 50.8 %copy-start.41 = (f32[1024]{0:T(1024)S(1)}, f32[1024]{0:T(1024)}, u32[]{:S(2)}) copy-start(f32[1024]{0:T(1024)} %param.14) | copy-start | bytes 12292
  7.9 186.3 %all-gather.8.cloned.1.call-start = ((), (), s32[]{:S(2)}) async-start(), calls=%async_computation.9 | async-start | bytes 2621440 | tf_op jit(solution)/shard_map/all_gather | solution.py:317
  8.7 206.9 %all-gather.10.cloned.1.call-start = ((), (), s32[]{:S(2)}) async-start(), calls=%async_computation.10 | async-start | bytes 10485760 | tf_op jit(solution)/shard_map/all_gather | solution.py:347
  9.4 219.2 %all-gather.12.cloned.1.call-start = ((), (), s32[]{:S(2)}) async-start(), calls=%async_computation.11 | async-start | bytes 10485760 | tf_op jit(solution)/shard_map/all_gather | solution.py:348
  10.6 54.0 %copy-start.36 = (f32[384]{0:T(512)}, f32[384]{0:T(512)S(1)}, u32[]{:S(2)}) copy-start(f32[384]{0:T(512)S(1)} %fusion.58) | copy-start | bytes 4612
  66.0 26.1 %all-to-all-start = ((bf16[384,8,128]{2,0,1:T(8,128)(2,1)}), bf16[384,8,128]{2,0,1:T(8,128)(2,1)S(1)}, u32[]{:S(2)}, u32[]{:S(2)}) async-start(bf16[384,8,128]{2,0,1:T(8,128)(2,1)} %bitcast.233), calls=%async_computation | async-start | bytes 1572864 | tf_op jit(solution)/shard_map/all_to_all | solution.py:325
  71.6 48.2 %copy-start.47 = (s32[1,384]{1,0:T(1,128)S(1)}, s32[1,384]{1,0:T(1,128)}, u32[]{:S(2)}) copy-start(s32[1,384]{1,0:T(1,128)} %param.13) | copy-start | bytes 4612
  71.6 87.1 %copy-start.51 = (f32[16]{0:T(128)S(1)}, f32[16]{0:T(128)}, u32[]{:S(2)}) copy-start(f32[16]{0:T(128)} %param.16) | copy-start | bytes 196
  92.1 68.5 %copy-start.27 = (bf16[384,8,128]{2,0,1:T(8,128)(2,1)}, bf16[384,8,128]{2,0,1:T(8,128)(2,1)S(1)}, u32[]{:S(2)}) copy-start(bf16[384,8,128]{2,0,1:T(8,128)(2,1)S(1)} %all-to-all-done) | copy-start | bytes 2359300
  92.1 24.0 %all-to-all-start.1 = ((bf16[384,8,128]{2,0,1:T(8,128)(2,1)}), bf16[384,8,128]{2,0,1:T(8,128)(2,1)S(1)}, u32[]{:S(2)}, u32[]{:S(2)}) async-start(bf16[384,8,128]{2,0,1:T(8,128)(2,1)} %bitcast.232), calls=%async_computation.1 | async-start | bytes 1572864 | tf_op jit(solution)/shard_map/all_to_all | solution.py:326
  116.1 44.5 %copy-start.28 = (bf16[384,8,128]{2,0,1:T(8,128)(2,1)}, bf16[384,8,128]{2,0,1:T(8,128)(2,1)S(1)}, u32[]{:S(2)}) copy-start(bf16[384,8,128]{2,0,1:T(8,128)(2,1)S(1)} %all-to-all-done.1) | copy-start | bytes 2359300
  116.1 44.5 %all-to-all-start.2 = ((bf16[384,8,128]{2,0,1:T(8,128)(2,1)}), bf16[384,8,128]{2,0,1:T(8,128)(2,1)S(1)}, u32[]{:S(2)}, u32[]{:S(2)}) async-start(bf16[384,8,128]{2,0,1:T(8,128)(2,1)} %bitcast.231), calls=%async_computation.2 | async-start | bytes 1572864 | tf_op jit(solution)/shard_map/all_to_all | solution.py:329
  190.1 20.2 %all-to-all-start.3 = ((bf16[8,384,128]{1,2,0:T(8,128)(2,1)}), bf16[8,384,128]{1,2,0:T(8,128)(2,1)S(1)}, u32[]{:S(2)}, u32[]{:S(2)}) async-start(bf16[8,384,128]{1,2,0:T(8,128)(2,1)} %copy.74), calls=%async_computation.3 | async-start | bytes 1572864 | tf_op jit(solution)/shard_map/all_to_all | solution.py:340
  194.2 19.4 %copy-start.33 = (f32[1024]{0:T(1024)S(1)}, f32[1024]{0:T(1024)}, u32[]{:S(2)}) copy-start(f32[1024]{0:T(1024)} %param.18) | copy-start | bytes 12292
  228.6 142.5 %copy-start.44 = (f32[384]{0:T(512)}, f32[384]{0:T(512)S(1)}, u32[]{:S(2)}) copy-start(f32[384]{0:T(512)S(1)} %fusion.61) | copy-start | bytes 4612
  228.7 8.9 %copy-start.1 = (f32[384,4096]{1,0:T(8,128)S(1)}, f32[384,4096]{1,0:T(8,128)}, u32[]{:S(2)}) copy-start(f32[384,4096]{1,0:T(8,128)} %copy-done) | copy-start | bytes 18874372
  241.7 6.2 copy-start.8
  257.8 5.6 copy-start.49
  259.8 21.7 %all-to-all-start.4 = ((bf16[384,8,128]{2,0,1:T(8,128)(2,1)}), bf16[384,8,128]{2,0,1:T(8,128)(2,1)S(1)}, u32[]{:S(2)}, u32[]{:S(2)}) async-start(bf16[384,8,128]{2,0,1:T(8,128)(2,1)} %bitcast.230), calls=%async_computation.4 | async-start | bytes 1572864 | tf_op jit(solution)/shard_map/all_to_all | solution.py:366
  282.5 34.7 %copy-start.19 = (bf16[8,384,128]{1,2,0:T(8,128)(2,1)S(1)}, bf16[8,384,128]{1,2,0:T(8,128)(2,1)}, u32[]{:S(2)}) copy-start(bf16[8,384,128]{1,2,0:T(8,128)(2,1)} %copy-done.18) | copy-start | bytes 2359300
  313.0 22.9 %all-to-all-start.7 = ((bf16[8,384,128]{1,2,0:T(8,128)(2,1)}), bf16[8,384,128]{1,2,0:T(8,128)(2,1)}, u32[]{:S(2)}, u32[]{:S(2)}) async-start(bf16[8,384,128]{1,2,0:T(8,128)(2,1)} %copy.78), calls=%async_computation.7 | async-start | bytes 1572864 | tf_op jit(solution)/shard_map/all_to_all | solution.py:380
  320.0 20.1 %copy-start.9 = (f32[384,1024]{1,0:T(8,128)S(1)}, f32[384,1024]{1,0:T(8,128)}, u32[]{:S(2)}) copy-start(f32[384,1024]{1,0:T(8,128)} %copy-done.7) | copy-start | bytes 4718596
  322.3 24.9 %collective-permute-start.5 = (bf16[2,256,1024]{2,1,0:T(8,128)(2,1)}, bf16[2,256,1024]{2,1,0:T(8,128)(2,1)}, u32[]{:S(2)}, u32[]{:S(2)}) collective-permute-start(bf16[2,256,1024]{2,1,0:T(8,128)(2,1)} %dynamic-slice_bitcast_fusion.8), channel_id=1, source_target_pairs={{0,8},{8,0},{16,24},{24,16},{1,9},{9,1},{17,25},{25,17},{2,10},{10... | collective-permute-start | bytes 3145736 | tf_op jit(solution)/shard_map/ppermute | solution.py:291
  335.9 30.4 %all-to-all-start.6 = ((bf16[8,384,128]{1,2,0:T(8,128)(2,1)}), bf16[8,384,128]{1,2,0:T(8,128)(2,1)}, u32[]{:S(2)}, u32[]{:S(2)}) async-start(bf16[8,384,128]{1,2,0:T(8,128)(2,1)} %copy.77), calls=%async_computation.6 | async-start | bytes 1572864 | tf_op jit(solution)/shard_map/all_to_all | solution.py:377
  340.1 7.1 %copy-start.21 = (bf16[1024,1024]{1,0:T(8,128)(2,1)S(1)}, bf16[1024,1024]{1,0:T(8,128)(2,1)}, u32[]{:S(2)}) copy-start(bf16[1024,1024]{1,0:T(8,128)(2,1)} %copy-done.20) | copy-start | bytes 6291460
  347.2 6.1 copy-start.11
  350.7 12.4 %collective-permute-start.6 = (bf16[256,1024]{1,0:T(8,128)(2,1)}, bf16[256,1024]{1,0:T(8,128)(2,1)}, u32[]{:S(2)}, u32[]{:S(2)}) collective-permute-start(bf16[256,1024]{1,0:T(8,128)(2,1)} %dynamic-slice_bitcast_fusion.12), channel_id=1, source_target_pairs={{0,16},{8,24},{16,0},{24,8},{1,17},{9,25},{17,1},{25,9},{2,18},{10... | collective-permute-start | bytes 1572872 | tf_op jit(solution)/shard_map/ppermute | solution.py:291
  353.2 17.9 %copy-start.14 = (bf16[1,384,1024]{2,1,0:T(8,128)(2,1)S(1)}, bf16[1,384,1024]{2,1,0:T(8,128)(2,1)}, u32[]{:S(2)}) copy-start(bf16[1,384,1024]{2,1,0:T(8,128)(2,1)} %param.23) | copy-start | bytes 2359300
  353.2 68.9 %collective-permute-start.10 = (bf16[2,256,4096]{2,1,0:T(8,128)(2,1)}, bf16[2,256,4096]{2,1,0:T(8,128)(2,1)}, u32[]{:S(2)}, u32[]{:S(2)}) collective-permute-start(bf16[2,256,4096]{2,1,0:T(8,128)(2,1)} %dynamic-slice_bitcast_fusion.1), channel_id=1, source_target_pairs={{0,8},{8,0},{16,24},{24,16},{1,9},{9,1},{17,25},{25,17},{2,10},{10... | collective-permute-start | bytes 12582920 | tf_op jit(solution)/shard_map/ppermute | solution.py:291
  364.5 21.3 %collective-permute-start.7 = (bf16[2,2,32,1024]{3,2,1,0:T(8,128)(2,1)S(1)}, bf16[2,2,32,1024]{3,2,1,0:T(8,128)(2,1)}, u32[]{:S(2)}, u32[]{:S(2)}) collective-permute-start(bf16[2,2,32,1024]{3,2,1,0:T(8,128)(2,1)S(1)} %dynamic-slice_bitcast_fusion.16), channel_id=1, source_target_pairs={{0,1},{1,0},{2,3},{3,2},{4,5},{5,4},{6,7},{7,6},{8,9},{9,8},{10,11... | collective-permute-start | bytes 786440 | tf_op jit(solution)/shard_map/ppermute | solution.py:291
  366.3 36.3 %all-to-all-start.5 = ((bf16[8,384,128]{1,2,0:T(8,128)(2,1)}), bf16[8,384,128]{1,2,0:T(8,128)(2,1)}, u32[]{:S(2)}, u32[]{:S(2)}) async-start(bf16[8,384,128]{1,2,0:T(8,128)(2,1)} %copy.76), calls=%async_computation.5 | async-start | bytes 1572864 | tf_op jit(solution)/shard_map/all_to_all | solution.py:374
  386.8 11.7 %collective-permute-start.8 = (bf16[2,32,1024]{2,1,0:T(8,128)(2,1)S(1)}, bf16[2,32,1024]{2,1,0:T(8,128)(2,1)}, u32[]{:S(2)}, u32[]{:S(2)}) collective-permute-start(bf16[2,32,1024]{2,1,0:T(8,128)(2,1)S(1)} %dynamic-slice_bitcast_fusion.18), channel_id=1, source_target_pairs={{0,2},{1,3},{2,0},{3,1},{4,6},{5,7},{6,4},{7,5},{8,10},{9,11},{10,... | collective-permute-start | bytes 393224 | tf_op jit(solution)/shard_map/ppermute | solution.py:291
  388.9 13.7 %copy-start.4 = (bf16[1,384,1024]{2,1,0:T(8,128)(2,1)S(1)}, bf16[1,384,1024]{2,1,0:T(8,128)(2,1)}, u32[]{:S(2)}) copy-start(bf16[1,384,1024]{2,1,0:T(8,128)(2,1)} %param.12) | copy-start | bytes 2359300
  393.6 92.5 %collective-permute-start.15 = (bf16[2,1024,1024]{2,1,0:T(8,128)(2,1)}, bf16[2,1024,1024]{2,1,0:T(8,128)(2,1)}, u32[]{:S(2)}, u32[]{:S(2)}) collective-permute-start(bf16[2,1024,1024]{2,1,0:T(8,128)(2,1)} %dynamic-slice_bitcast_fusion), channel_id=1, source_target_pairs={{0,8},{8,0},{16,24},{24,16},{1,9},{9,1},{17,25},{25,17},{2,10},{10... | collective-permute-start | bytes 12582920 | tf_op jit(solution)/shard_map/ppermute | solution.py:291
  400.2 81.3 %collective-permute-start.9 = (bf16[32,1024]{1,0:T(8,128)(2,1)}, bf16[32,1024]{1,0:T(8,128)(2,1)}, u32[]{:S(2)}, u32[]{:S(2)}) collective-permute-start(bf16[32,1024]{1,0:T(8,128)(2,1)} %dynamic-slice_bitcast_fusion.19), channel_id=1, source_target_pairs={{0,4},{1,5},{2,6},{3,7},{4,0},{5,1},{6,2},{7,3},{8,12},{9,13},{10,... | collective-permute-start | bytes 196616 | tf_op jit(solution)/shard_map/ppermute | solution.py:291
  402.6 6.4 %copy-start.37 = (f32[384]{0:T(512)S(1)}, f32[384]{0:T(512)}, u32[]{:S(2)}) copy-start(f32[384]{0:T(512)} %copy-done.36) | copy-start | bytes 4612
  402.6 6.4 %copy-start.42 = (f32[1024]{0:T(1024)S(1)}, f32[1024]{0:T(1024)}, u32[]{:S(2)}) copy-start(f32[1024]{0:T(1024)} %param.14) | copy-start | bytes 12292
  402.6 7.6 %copy-start.24 = (bf16[1024,1]{1,0:T(8,128)(2,1)S(1)}, bf16[1024,1]{1,0:T(8,128)(2,1)}, u32[]{:S(2)}) copy-start(bf16[1024,1]{1,0:T(8,128)(2,1)} %broadcast_in_dim.96) | copy-start | bytes 6148
  402.6 7.6 %copy-start.25 = (bf16[1024,1]{1,0:T(8,128)(2,1)S(1)}, bf16[1024,1]{1,0:T(8,128)(2,1)}, u32[]{:S(2)}) copy-start(bf16[1024,1]{1,0:T(8,128)(2,1)} %broadcast_in_dim.95) | copy-start | bytes 6148
  420.1 11.8 %slice-start = ((s8[6291456]{0:T(1024)(128)(4,1)}), s8[4194304]{0:T(1024)(128)(4,1)S(1)}, s32[]{:S(2)}) async-start(s8[6291456]{0:T(1024)(128)(4,1)} %bitcast.234), calls=%async_computation.12 | async-start | bytes 8388608
  420.1 11.8 %slice-start.4 = ((s8[8388608]{0:T(1024)(128)(4,1)}), s8[4194304]{0:T(1024)(128)(4,1)S(1)}, s32[]{:S(2)}) async-start(s8[8388608]{0:T(1024)(128)(4,1)} %bitcast.271), calls=%async_computation.16 | async-start | bytes 8388608
  422.0 9.9 %slice-start.1 = ((s8[6291456]{0:T(1024)(128)(4,1)}), s8[2097152]{0:T(1024)(128)(4,1)S(1)}, s32[]{:S(2)}) async-start(s8[6291456]{0:T(1024)(128)(4,1)} %bitcast.234), calls=%async_computation.13 | async-start | bytes 4194304
  422.0 9.9 %slice-start.5 = ((s8[8388608]{0:T(1024)(128)(4,1)}), s8[4194304]{0:T(1024)(128)(4,1)S(1)}, s32[]{:S(2)}) async-start(s8[8388608]{0:T(1024)(128)(4,1)} %bitcast.271), calls=%async_computation.17 | async-start | bytes 8388608
  422.0 75.9 %collective-permute-start = (bf16[2,256,3200]{2,1,0:T(8,128)(2,1)}, bf16[2,256,3200]{2,1,0:T(8,128)(2,1)}, u32[]{:S(2)}, u32[]{:S(2)}) collective-permute-start(bf16[2,256,3200]{2,1,0:T(8,128)(2,1)} %dynamic-slice_bitcast_fusion.2), channel_id=1, source_target_pairs={{0,8},{8,0},{16,24},{24,16},{1,9},{9,1},{17,25},{25,17},{2,10},{10... | collective-permute-start | bytes 9830408 | tf_op jit(solution)/shard_map/ppermute | solution.py:291
  431.4 7.1 %copy-start.50 = (f32[2]{0:T(128)S(1)}, f32[2]{0:T(128)}, u32[]{:S(2)}) copy-start(f32[2]{0:T(128)} %reduce_sum.297) | copy-start | bytes 28
  431.4 51.6 %copy-start.35 = (f32[384]{0:T(512)S(1)}, f32[384]{0:T(512)}, u32[]{:S(2)}) copy-start(f32[384]{0:T(512)} %copy-done.34) | copy-start | bytes 4612
  431.4 51.6 %copy-start.38 = (f32[384]{0:T(512)S(1)}, f32[384]{0:T(512)}, u32[]{:S(2)}) copy-start(f32[384]{0:T(512)} %copy-done.36) | copy-start | bytes 4612
  431.5 51.6 %copy-start.43 = (f32[1024]{0:T(1024)S(1)}, f32[1024]{0:T(1024)}, u32[]{:S(2)}) copy-start(f32[1024]{0:T(1024)} %param.14) | copy-start | bytes 12292
  431.5 62.3 %collective-permute-start.11 = (bf16[256,4096]{1,0:T(8,128)(2,1)}, bf16[256,4096]{1,0:T(8,128)(2,1)}, u32[]{:S(2)}, u32[]{:S(2)}) collective-permute-start(bf16[256,4096]{1,0:T(8,128)(2,1)} %dynamic-slice_bitcast_fusion.4), channel_id=1, source_target_pairs={{0,16},{8,24},{16,0},{24,8},{1,17},{9,25},{17,1},{25,9},{2,18},{10... | collective-permute-start | bytes 6291464 | tf_op jit(solution)/shard_map/ppermute | solution.py:291
  486.1 7.8 %copy-start.6 = (bf16[2,256,4096]{2,1,0:T(8,128)(2,1)S(1)}, bf16[2,256,4096]{2,1,0:T(8,128)(2,1)}, u32[]{:S(2)}) copy-start(bf16[2,256,4096]{2,1,0:T(8,128)(2,1)} %copy-done.5) | copy-start | bytes 12582916
  491.8 6.1 slice-start.2
  492.0 5.9 slice-start.3
  492.0 48.6 %collective-permute-start.16 = (bf16[1024,1024]{1,0:T(8,128)(2,1)S(1)}, bf16[1024,1024]{1,0:T(8,128)(2,1)S(1)}, u32[]{:S(2)}, u32[]{:S(2)}) collective-permute-start(bf16[1024,1024]{1,0:T(8,128)(2,1)S(1)} %dynamic-slice_bitcast_fusion.3), channel_id=1, source_target_pairs={{0,16},{8,24},{16,0},{24,8},{1,17},{9,25},{17,1},{25,9},{2,18},{10... | collective-permute-start | bytes 6291464 | tf_op jit(solution)/shard_map/ppermute | solution.py:291
  496.3 47.0 %collective-permute-start.12 = (bf16[2,2,32,4096]{3,2,1,0:T(8,128)(2,1)S(1)}, bf16[2,2,32,4096]{3,2,1,0:T(8,128)(2,1)S(1)}, u32[]{:S(2)}, u32[]{:S(2)}) collective-permute-start(bf16[2,2,32,4096]{3,2,1,0:T(8,128)(2,1)S(1)} %dynamic-slice_bitcast_fusion.7), channel_id=1, source_target_pairs={{0,1},{1,0},{2,3},{3,2},{4,5},{5,4},{6,7},{7,6},{8,9},{9,8},{10,11... | collective-permute-start | bytes 3145736 | tf_op jit(solution)/shard_map/ppermute | solution.py:291
  500.8 73.5 %collective-permute-start.1 = (bf16[256,3200]{1,0:T(8,128)(2,1)S(1)}, bf16[256,3200]{1,0:T(8,128)(2,1)S(1)}, u32[]{:S(2)}, u32[]{:S(2)}) collective-permute-start(bf16[256,3200]{1,0:T(8,128)(2,1)S(1)} %dynamic-slice_bitcast_fusion.5), channel_id=1, source_target_pairs={{0,16},{8,24},{16,0},{24,8},{1,17},{9,25},{17,1},{25,9},{2,18},{10... | collective-permute-start | bytes 4915208 | tf_op jit(solution)/shard_map/ppermute | solution.py:291
  541.7 22.3 %collective-permute-start.17 = (bf16[2,2,128,1024]{3,2,1,0:T(8,128)(2,1)S(1)}, bf16[2,2,128,1024]{3,2,1,0:T(8,128)(2,1)S(1)}, u32[]{:S(2)}, u32[]{:S(2)}) collective-permute-start(bf16[2,2,128,1024]{3,2,1,0:T(8,128)(2,1)S(1)} %dynamic-slice_bitcast_fusion.6), channel_id=1, source_target_pairs={{0,1},{1,0},{2,3},{3,2},{4,5},{5,4},{6,7},{7,6},{8,9},{9,8},{10,11... | collective-permute-start | bytes 3145736 | tf_op jit(solution)/shard_map/ppermute | solution.py:291
  543.6 32.7 %collective-permute-start.13 = (bf16[2,32,4096]{2,1,0:T(8,128)(2,1)S(1)}, bf16[2,32,4096]{2,1,0:T(8,128)(2,1)S(1)}, u32[]{:S(2)}, u32[]{:S(2)}) collective-permute-start(bf16[2,32,4096]{2,1,0:T(8,128)(2,1)S(1)} %dynamic-slice_bitcast_fusion.11), channel_id=1, source_target_pairs={{0,2},{1,3},{2,0},{3,1},{4,6},{5,7},{6,4},{7,5},{8,10},{9,11},{10,... | collective-permute-start | bytes 1572872 | tf_op jit(solution)/shard_map/ppermute | solution.py:291
  564.5 12.6 %collective-permute-start.18 = (bf16[2,128,1024]{2,1,0:T(8,128)(2,1)S(1)}, bf16[2,128,1024]{2,1,0:T(8,128)(2,1)S(1)}, u32[]{:S(2)}, u32[]{:S(2)}) collective-permute-start(bf16[2,128,1024]{2,1,0:T(8,128)(2,1)S(1)} %dynamic-slice_bitcast_fusion.10), channel_id=1, source_target_pairs={{0,2},{1,3},{2,0},{3,1},{4,6},{5,7},{6,4},{7,5},{8,10},{9,11},{10,... | collective-permute-start | bytes 1572872 | tf_op jit(solution)/shard_map/ppermute | solution.py:291
  574.8 18.9 %collective-permute-start.2 = (bf16[2,2,32,3200]{3,2,1,0:T(8,128)(2,1)S(1)}, bf16[2,2,32,3200]{3,2,1,0:T(8,128)(2,1)S(1)}, u32[]{:S(2)}, u32[]{:S(2)}) collective-permute-start(bf16[2,2,32,3200]{3,2,1,0:T(8,128)(2,1)S(1)} %dynamic-slice_bitcast_fusion.9), channel_id=1, source_target_pairs={{0,1},{1,0},{2,3},{3,2},{4,5},{5,4},{6,7},{7,6},{8,9},{9,8},{10,11... | collective-permute-start | bytes 2457608 | tf_op jit(solution)/shard_map/ppermute | solution.py:291
  576.5 19.0 %collective-permute-start.14 = (bf16[32,4096]{1,0:T(8,128)(2,1)S(1)}, bf16[32,4096]{1,0:T(8,128)(2,1)S(1)}, u32[]{:S(2)}, u32[]{:S(2)}) collective-permute-start(bf16[32,4096]{1,0:T(8,128)(2,1)S(1)} %dynamic-slice_bitcast_fusion.15), channel_id=1, source_target_pairs={{0,4},{1,5},{2,6},{3,7},{4,0},{5,1},{6,2},{7,3},{8,12},{9,13},{10,... | collective-permute-start | bytes 786440 | tf_op jit(solution)/shard_map/ppermute | solution.py:291
  577.3 32.5 %collective-permute-start.19 = (bf16[128,1024]{1,0:T(8,128)(2,1)S(1)}, bf16[128,1024]{1,0:T(8,128)(2,1)S(1)}, u32[]{:S(2)}, u32[]{:S(2)}) collective-permute-start(bf16[128,1024]{1,0:T(8,128)(2,1)S(1)} %dynamic-slice_bitcast_fusion.14), channel_id=1, source_target_pairs={{0,4},{1,5},{2,6},{3,7},{4,0},{5,1},{6,2},{7,3},{8,12},{9,13},{10,... | collective-permute-start | bytes 786440 | tf_op jit(solution)/shard_map/ppermute | solution.py:291
  593.9 15.7 %collective-permute-start.3 = (bf16[2,32,3200]{2,1,0:T(8,128)(2,1)S(1)}, bf16[2,32,3200]{2,1,0:T(8,128)(2,1)S(1)}, u32[]{:S(2)}, u32[]{:S(2)}) collective-permute-start(bf16[2,32,3200]{2,1,0:T(8,128)(2,1)S(1)} %dynamic-slice_bitcast_fusion.13), channel_id=1, source_target_pairs={{0,2},{1,3},{2,0},{3,1},{4,6},{5,7},{6,4},{7,5},{8,10},{9,11},{10,... | collective-permute-start | bytes 1228808 | tf_op jit(solution)/shard_map/ppermute | solution.py:291
  609.8 11.3 %collective-permute-start.4 = (bf16[32,3200]{1,0:T(8,128)(2,1)S(1)}, bf16[32,3200]{1,0:T(8,128)(2,1)S(1)}, u32[]{:S(2)}, u32[]{:S(2)}) collective-permute-start(bf16[32,3200]{1,0:T(8,128)(2,1)S(1)} %dynamic-slice_bitcast_fusion.17), channel_id=1, source_target_pairs={{0,4},{1,5},{2,6},{3,7},{4,0},{5,1},{6,2},{7,3},{8,12},{9,13},{10,... | collective-permute-start | bytes 614408 | tf_op jit(solution)/shard_map/ppermute | solution.py:291
  (26 other events, 63.5 us)
Sparse Core Ops, SparseCore 0:
  9.6 49.0 all-gather.5
  60.3 22.5 all-gather.7
  84.4 58.2 all-gather.9
  144.2 58.3 all-gather.11

commit v2 on v1

--- a/solution.py
+++ b/solution.py
@@ -294,6 +294,400 @@
     return current.astype(jnp.float32)
 
 
+MESH = pl.DeviceIdType.MESH
+LOW = jnp.bfloat16
+BLOCK = 1024
+VMEM_BYTES = 66_000_000
+
+
+class Place:
+    def __init__(self):
+        self.dp, self.seq = lax.axis_index("dp"), lax.axis_index("seq")
+        self.core, self.y = self.dp % 2, self.dp // 2
+        self.x, self.z = self.seq % 2, self.seq // 2
+        self.z0, self.z1 = self.z % 2, self.z // 2
+
+    def core_partner(self):
+        return (self.dp + 1 - 2 * self.core, self.seq)
+
+    def y_partner(self):
+        return (self.dp + 2 - 4 * self.y, self.seq)
+
+    def x_partner(self):
+        return (self.dp, self.seq + 1 - 2 * self.x)
+
+    def near_partner(self):
+        return (self.dp, self.seq + 2 - 4 * self.z0)
+
+    def far_partner(self):
+        return (self.dp, self.seq + 4 - 8 * self.z1)
+
+
+def meet(devices):
+    barrier = pltpu.get_barrier_semaphore()
+    for device in devices:
+        pl.semaphore_signal(barrier, inc=1, device_id=device, device_id_type=MESH)
+    pl.semaphore_wait(barrier, len(devices))
+
+
+def remote(source, target, send, receive, device):
+    return pltpu.make_async_remote_copy(
+        src_ref=source,
+        dst_ref=target,
+        send_sem=send,
+        recv_sem=receive,
+        device_id=device,
+        device_id_type=MESH,
+    )
+
+
+class Scatter:
+    def __init__(self, place, refs, sems, base, left, right, write):
+        self.place, self.base, self.left, self.right, self.write = place, base, left, right, write
+        self.whole, self.first, self.second, self.near, self.far = refs
+        self.send, self.receive = sems
+        self.rows, self.columns = self.whole.shape[-2:]
+
+    def axes(self, p):
+        place = self.place
+        if p % 2 == 0:
+            return place.y, place.x, place.y_partner(), place.x_partner()
+        return place.x, place.y, place.x_partner(), place.y_partner()
+
+    def copy(self, p, stage):
+        place = self.place
+        mine, other, partner, second = self.axes(p)
+        if stage == 0:
+            source, target, device = self.whole.at[p, 1 - mine], self.first.at[p], partner
+        elif stage == 1:
+            source, target, device = self.first.at[p, :, :, 1 - other], self.second.at[p], second
+        elif stage == 2:
+            source, target, device = self.second.at[p, :, 1 - place.z0], self.near.at[p], place.near_partner()
+        else:
+            source, target, device = self.near.at[p, 1 - place.z1], self.far.at[p], place.far_partner()
+        index = self.base + p
+        return remote(source, target, self.send.at[stage, index], self.receive.at[stage, index], device)
+
+    def compute(self, p):
+        left, right = self.left(p), self.right(p)
+        rows = self.rows
+
+        def one(y, carry):
+            for half in range(2):
+                span = 4 * rows
+                at = pl.ds(pl.multiple_of(y * 8 * rows + half * span, 128), span)
+                block = tn(left[:, at], right[...]).astype(LOW)
+                for k in range(4):
+                    x = k % 2
+                    part = block[k * rows : (k + 1) * rows]
+                    if p % 2 == 0:
+                        self.whole[p, y, half, k // 2, x] = part
+                    else:
+                        self.whole[p, x, half, k // 2, y] = part
+            return carry
+
+        lax.fori_loop(0, 2, one, 0)
+        self.copy(p, 0).start()
+
+    def advance(self, p, stage):
+        place = self.place
+        mine, other, _, _ = self.axes(p)
+        wide = jnp.float32
+        self.copy(p, stage - 1).wait_recv()
+        if stage == 1:
+
+            def add(k, carry):
+                a, b, s = k // 4, k // 2 % 2, k % 2
+                total = self.first[p, a, b, s].astype(wide) + self.whole[p, mine, a, b, s].astype(wide)
+                self.first[p, a, b, s] = total.astype(LOW)
+                return carry
+
+            lax.fori_loop(0, 8, add, 0)
+        elif stage == 2:
+
+            def add(z, carry):
+                a, b = z // 2, z % 2
+                total = self.second[p, a, b].astype(wide) + self.first[p, a, b, other].astype(wide)
+                self.second[p, a, b] = total.astype(LOW)
+                return carry
+
+            lax.fori_loop(0, 4, add, 0)
+        elif stage == 3:
+
+            def add(a, carry):
+                total = self.near[p, a].astype(wide) + self.second[p, a, place.z0].astype(wide)
+                self.near[p, a] = total.astype(LOW)
+                return carry
+
+            lax.fori_loop(0, 2, add, 0)
+        else:
+            self.write(p, self.near[p, place.z1].astype(wide) + self.far[p].astype(wide))
+            return
+        self.copy(p, stage).start()
+
+    def settle(self, p):
+        for stage in range(4):
+            self.copy(p, stage).wait_send()
+
+
+def scatter_scratch(pieces, rows, columns):
+    return [
+        pltpu.VMEM((pieces, 2, 2, 2, 2, rows, columns), LOW),
+        pltpu.VMEM((pieces, 2, 2, 2, rows, columns), LOW),
+        pltpu.VMEM((pieces, 2, 2, rows, columns), LOW),
+        pltpu.VMEM((pieces, 2, rows, columns), LOW),
+        pltpu.VMEM((pieces, rows, columns), LOW),
+    ]
+
+
+def own_columns(source, core, columns):
+    half = source.shape[1] // 2
+    return [
+        source.at[:, pl.ds(pl.multiple_of(y * half + core * columns, 128), columns)] for y in range(2)
+    ]
+
+
+def tail_kernel(
+    dq, dk, dv, tokens, gain, middle, triple, act_down, act_up, act_out, act_in, g_down, g_up, g_out, gains,
+    o_tokens, o_triple, o_out, o_up, o_down, o_gains,
+    d_left, d_right, d_whole, d_first, d_second, d_near, d_far,
+    e_left, e_right, e_whole, e_first, e_second, e_near, e_far,
+    grad_s, gain_s, gain_r,
+    local_sem, core_send, core_recv, a2a_send, a2a_recv, s_send, s_recv, gain_send, gain_recv,
+):
+    place = Place()
+    partner = place.core_partner()
+    peers = [(place.dp, (place.seq + k) % 8) for k in range(1, 8)]
+    local, width = tokens.shape
+    heads_width = dq.shape[1]
+    meet(peers + [partner, place.y_partner()])
+
+    moves = []
+    column = pl.ds(pl.multiple_of(place.seq * heads_width, 128), heads_width)
+    for t, source in enumerate((dv, dk, dq)):
+        slot = 5 + (2 - t)
+        for k in range(1, 8):
+            peer = (place.seq + k) % 8
+            rows = pl.ds(pl.multiple_of(peer * local, 128), local)
+            move = remote(
+                source.at[rows, :],
+                e_right.at[slot, pl.ds(0, local), column],
+                a2a_send.at[t, k - 1],
+                a2a_recv.at[t, k - 1],
+                (place.dp, peer),
+            )
+            move.start()
+            moves.append(move)
+        rows = pl.ds(pl.multiple_of(place.seq * local, 128), local)
+        move = pltpu.make_async_copy(
+            source.at[rows, :], e_right.at[slot, pl.ds(0, local), column], local_sem.at[t]
+        )
+        move.start()
+        moves.append(move)
+
+    def share(index, sources, targets):
+        out = []
+        for k, (ours, theirs, target) in enumerate(zip(*sources, targets)):
+            here = pltpu.make_async_copy(ours, target.at[pl.ds(0, local), :], local_sem.at[3 + index + k])
+            there = remote(
+                theirs,
+                target.at[pl.ds(local, local), :],
+                core_send.at[index + k],
+                core_recv.at[index + k],
+                partner,
+            )
+            here.start()
+            there.start()
+            out += [here, there]
+        return out
+
+    def share_left(index, source, target):
+        columns = source.shape[1] // 4
+        ours = own_columns(source, place.core, columns)
+        theirs = own_columns(source, 1 - place.core, columns)
+        targets = [target.at[:, pl.ds(y * columns, columns)] for y in range(2)]
+        return share(index, (ours, theirs), targets)
+
+    ready = {}
+    ready["down"] = share_left(0, act_down, d_left) + share(2, ([g_down], [g_down]), [d_right])
+    ready["up"] = share_left(3, act_up, e_left.at[0])
+    for k in range(4):
+        part = g_up.at[:, pl.ds(k * BLOCK, BLOCK)]
+        ready["up"] += share(5 + k, ([part], [part]), [e_right.at[k]])
+    ready["out"] = share_left(9, act_out, e_left.at[1]) + share(11, ([g_out], [g_out]), [e_right.at[4]])
+    ready["in"] = share_left(12, act_in, e_left.at[2])
+
+    def write_down(p, value):
+        o_down[:, pl.ds(p * 256, 256)] = value
+
+    def write_rest(p, value):
+        if p < 4:
+            o_up[:, pl.ds(p * BLOCK, BLOCK)] = value
+        elif p == 4:
+            o_out[...] = value
+        else:
+            o_triple[:, pl.ds((p - 5) * BLOCK, BLOCK)] = value
+
+    down = Scatter(
+        place, (d_whole, d_first, d_second, d_near, d_far), (s_send, s_recv), 0,
+        lambda p: d_left, lambda p: d_right.at[:, pl.ds(p * 256, 256)], write_down,
+    )
+    rest = Scatter(
+        place, (e_whole, e_first, e_second, e_near, e_far), (s_send, s_recv), 4,
+        lambda p: e_left.at[0 if p < 4 else 1 if p == 4 else 2], lambda p: e_right.at[p], write_rest,
+    )
+    order = [(down, k) for k in range(4)] + [(rest, k) for k in (0, 1, 2, 3, 4, 7, 6, 5)]
+
+    def wait_all(copies):
+        for copy in copies:
+            copy.wait()
+
+    lag = 2
+    gain_s[...] = gains[...]
+
+    def step(t):
+        if t < len(order):
+            engine, p = order[t]
+            if t == 0:
+                wait_all(ready["down"])
+            if t == 4:
+                wait_all(ready["up"])
+            if t == 8:
+                wait_all(ready["out"])
+            engine.compute(p)
+        for stage in (1, 2, 3, 4):
+            at = t - stage * lag
+            if 0 <= at < len(order):
+                order[at][0].advance(order[at][1], stage)
+
+    for t in range(9):
+        step(t)
+
+    wait_all(moves)
+    back = [
+        remote(
+            e_right.at[5 + t, pl.ds(0, local), :],
+            e_right.at[5 + t, pl.ds(local, local), :],
+            core_send.at[14 + t],
+            core_recv.at[14 + t],
+            partner,
+        )
+        for t in range(3)
+    ]
+    for move in back:
+        move.start()
+
+    def columns_of(n, carry):
+        rows = pl.ds(pl.multiple_of(n * 256, 256), 256)
+        total = jnp.zeros((local, 256), jnp.float32)
+        for t in range(3):
+            total += nt(e_right[5 + t, pl.ds(0, local), :], triple[rows, pl.ds(t * width, width)])
+        grad_s[:, rows] = total
+        return carry
+
+    wait_all(ready["in"])
+    wait_all(back)
+    step(9)
+    step(10)
+    step(11)
+    lax.fori_loop(0, width // 256, columns_of, 0)
+    step(12)
+
+    def norm_rows(n, total):
+        rows = pl.ds(pl.multiple_of(n * 128, 128), 128)
+        values = tokens[rows, :].astype(jnp.float32)
+        center = values - jnp.mean(values, axis=-1, keepdims=True)
+        inverse = lax.rsqrt(jnp.mean(center * center, axis=-1, keepdims=True) + 1e-05)
+        unit = center * inverse
+        grad = grad_s[rows, :]
+        scaled = grad * gain[...]
+        pulled = inverse * (
+            scaled
+            - jnp.mean(scaled, axis=-1, keepdims=True)
+            - unit * jnp.mean(scaled * unit, axis=-1, keepdims=True)
+        )
+        o_tokens[rows, :] = (middle[rows, :] + pulled).astype(LOW)
+        return total + jnp.sum(grad * unit, axis=0, keepdims=True)
+
+    gain_s[0:1, :] = lax.fori_loop(0, local // 128, norm_rows, jnp.zeros((1, width), jnp.float32))
+
+    meets = (partner, place.y_partner(), place.x_partner(), place.near_partner(), place.far_partner())
+
+    def gain_step(k):
+        move = remote(gain_s, gain_r.at[k], gain_send.at[k], gain_recv.at[k], meets[k])
+        return move
+
+    for k in range(5):
+        move = gain_step(k)
+        move.start()
+        step(13 + k)
+        move.wait()
+        gain_s[...] = gain_s[...] + gain_r[k]
+        if k == 1:
+            o_gains[7:8, :] = gain_s[7:8, 0:128]
+    for t in range(18, len(order) + 4 * lag + 1):
+        step(t)
+    device = place.dp * 8 + place.seq
+    pick = (
+        lax.broadcasted_iota(jnp.int32, (width, 128), 0)
+        == device * 32 + lax.broadcasted_iota(jnp.int32, (width, 128), 1)
+    ).astype(jnp.float32)
+    o_gains[0:3, :] = jnp.dot(
+        gain_s[...], pick, preferred_element_type=jnp.float32, precision=lax.Precision.HIGHEST
+    )[0:3]
+    block = gain_s[:, pl.ds(pl.multiple_of((device % 8) * 128, 128), 128)]
+    row = lax.broadcasted_iota(jnp.int32, block.shape, 0)
+    o_gains[3:4, :] = jnp.sum(jnp.where(row == 3 + device // 8, block, 0.0), axis=0, keepdims=True)
+    o_gains[4:7, :] = jnp.zeros((3, 128), jnp.float32)
+    for engine, p in order:
+        engine.settle(p)
+
+
+def tail(dqkv, tokens, gain, middle, triple, acts, grads, gains):
+    local, width = tokens.shape
+    heads_width = dqkv[0].shape[1]
+    hidden = acts[0].shape[1]
+    any_spec = pl.BlockSpec(memory_space=pl.ANY)
+    vmem = pl.BlockSpec(memory_space=pltpu.VMEM)
+    wide = jnp.float32
+    dma = pltpu.SemaphoreType.DMA
+    return pl.pallas_call(
+        tail_kernel,
+        out_shape=(
+            jax.ShapeDtypeStruct((local, width), LOW),
+            jax.ShapeDtypeStruct((width // 32, 3 * width), wide),
+            jax.ShapeDtypeStruct((width // 32, width), wide),
+            jax.ShapeDtypeStruct((width // 32, hidden), wide),
+            jax.ShapeDtypeStruct((hidden // 32, width), wide),
+            jax.ShapeDtypeStruct((8, 128), wide),
+        ),
+        in_specs=[any_spec] * 3 + [vmem] * 4 + [any_spec] * 7 + [vmem],
+        out_specs=(vmem,) * 6,
+        scratch_shapes=[pltpu.VMEM((2 * local, hidden // 2), LOW), pltpu.VMEM((2 * local, width), LOW)]
+        + scatter_scratch(4, 128, 256)
+        + [pltpu.VMEM((3, 2 * local, width // 2), LOW), pltpu.VMEM((8, 2 * local, width), LOW)]
+        + scatter_scratch(8, 32, 1024)
+        + [
+            pltpu.VMEM((local, width), wide),
+            pltpu.VMEM((8, width), wide),
+            pltpu.VMEM((5, 8, width), wide),
+            dma((20,)),
+            dma((20,)),
+            dma((20,)),
+            dma((3, 7)),
+            dma((3, 7)),
+            dma((4, 12)),
+            dma((4, 12)),
+            dma((5,)),
+            dma((5,)),
+        ],
+        compiler_params=pltpu.CompilerParams(
+            collective_id=3, has_side_effects=True, vmem_limit_bytes=VMEM_BYTES
+        ),
+        name="tail",
+    )(*dqkv, tokens, gain.reshape(1, width), middle, triple, *acts, *grads, gains)
+
+
 def per_device(
     sizes,
     tokens,
@@ -422,6 +816,118 @@
     )
 
 
+def per_device_chips(
+    sizes,
+    tokens,
+    segment_ids,
+    first_gain,
+    triple_weight,
+    head_scale,
+    output_weight,
+    post_gain,
+    second_gain,
+    up_weight,
+    mid_gain,
+    down_weight,
+    cotangent,
+):
+    inputs = tokens[0].astype(jnp.float32)
+    width = inputs.shape[1]
+    doc_ids = lax.all_gather(segment_ids[0], "seq", axis=0, tiled=True)
+    triple_full, output_full = (
+        lax.all_gather(triple_weight, "dp", axis=0, tiled=True),
+        lax.all_gather(output_weight, "dp", axis=0, tiled=True),
+    )
+    normed = layer_norm(inputs, first_gain)
+    normed_low = normed.astype(jnp.bfloat16)
+    triple = jnp.dot(normed_low, triple_full, preferred_element_type=jnp.float32).astype(
+        jnp.bfloat16
+    )
+    queries, keys_all, values_all = (
+        lax.all_to_all(triple[:, :width], "seq", split_axis=1, concat_axis=0, tiled=True),
+        lax.all_to_all(
+            triple[:, width : 2 * width], "seq", split_axis=1, concat_axis=0, tiled=True
+        ),
+        lax.all_to_all(triple[:, 2 * width :], "seq", split_axis=1, concat_axis=0, tiled=True),
+    )
+    heads_here = queries.shape[1] // HEAD
+    own_scale = lax.dynamic_slice_in_dim(
+        head_scale, lax.axis_index("seq") * heads_here, heads_here, 0
+    )
+    scale_wide = jnp.repeat(own_scale, HEAD)[None]
+    bounds, starts = document_bounds(doc_ids)
+    attended, scaled, logsum = attend_forward(
+        queries, keys_all, values_all, bounds, starts, scale_wide
+    )
+    merged = lax.all_to_all(scaled, "seq", split_axis=0, concat_axis=1, tiled=True)
+    projected = jnp.dot(merged, output_full, preferred_element_type=jnp.float32)
+    post_normed, pull_post = jax.vjp(layer_norm, projected, post_gain)
+    middle = inputs + post_normed
+    second, pull_second = jax.vjp(layer_norm, middle, second_gain)
+    second_low = second.astype(jnp.bfloat16)
+    feed_up, feed_down = (
+        lax.all_gather(up_weight, "dp", axis=0, tiled=True),
+        lax.all_gather(down_weight, "dp", axis=0, tiled=True),
+    )
+    hidden = jnp.dot(second_low, feed_up, preferred_element_type=jnp.float32)
+    activated, pull_mid = jax.vjp(gelu_norm, hidden, mid_gain)
+    activated_low = activated.astype(jnp.bfloat16)
+    layer_out = (
+        middle + jnp.dot(activated_low, feed_down, preferred_element_type=jnp.float32)
+    ).astype(jnp.bfloat16)
+    upstream = cotangent[0]
+    grad_act = times_transposed(upstream, feed_down)
+    grad_hidden, grad_mid = pull_mid(grad_act)
+    grad_hidden_low = grad_hidden.astype(jnp.bfloat16)
+    grad_second_in = times_transposed(grad_hidden_low, feed_up)
+    grad_middle_part, grad_second = pull_second(grad_second_in)
+    grad_middle = upstream.astype(jnp.float32) + grad_middle_part
+    grad_projected, grad_post = pull_post(grad_middle)
+    grad_projected_low = grad_projected.astype(jnp.bfloat16)
+    grad_merged = times_transposed(grad_projected_low, output_full).astype(jnp.bfloat16)
+    grad_scaled = lax.all_to_all(
+        grad_merged, "seq", split_axis=1, concat_axis=0, tiled=True
+    )
+    grad_queries, grad_keys, grad_values, scale_lanes = attend_backward(
+        queries, keys_all, values_all, attended, grad_scaled, bounds, starts, scale_wide, logsum
+    )
+    grad_first_low = jnp.zeros((1, width), jnp.float32)
+    gains = jnp.concatenate(
+        (
+            grad_first_low,
+            grad_post[None],
+            grad_second[None],
+            grad_mid.reshape(-1, width),
+            jnp.pad(scale_lanes, ((0, 0), (0, width - scale_lanes.shape[1]))),
+        ),
+        axis=0,
+    )
+    grad_tokens, grad_triple, grad_output, grad_up, grad_down, sums = tail(
+        (grad_queries, grad_keys, grad_values),
+        tokens[0],
+        first_gain,
+        grad_middle,
+        triple_full,
+        (activated_low, second_low, merged, normed_low),
+        (upstream, grad_hidden_low, grad_projected_low),
+        gains,
+    )
+    own = width // 32
+    return (
+        layer_out[None],
+        grad_tokens[None],
+        sums[0, :own],
+        grad_triple,
+        jnp.sum(sums[7].reshape(heads_here, HEAD), axis=1),
+        grad_output,
+        sums[1, :own],
+        sums[2, :own],
+        grad_up,
+        sums[3],
+        grad_down,
+    )
+
+
 def solution(mesh):
     placed = (
         P("dp", "seq", None),
@@ -437,8 +943,10 @@
         P("dp", None),
         P("dp", "seq", None),
     )
+    sizes = (mesh.shape["dp"], mesh.shape["seq"])
+    program = per_device_chips if sizes == (4, 8) else per_device
     return jax.shard_map(
-        functools.partial(per_device, (mesh.shape["dp"], mesh.shape["seq"])),
+        functools.partial(program, sizes),
         mesh=mesh,
         in_specs=placed,
         out_specs=(

time: 634 us -> 477 us (0.75)
  Pallas kernels: 54.5 us -> 204 us
  waiting for transfers between devices: 250 us -> 111 us
  blocking collectives: 81.6 us -> 38.6 us
  starting transfers between devices: 52.7 us -> 20.8 us
  matrix products: 73.5 us -> 41.8 us
  other arithmetic: 53.4 us -> 22.9 us
  local copies, waits for them, and re-layouts: 49.6 us -> 23.1 us
    pallas_call x0 -> x1, Pallas kernels: none -> 152 us  [tail(): pl.pallas_call(tail_kernel, out_shape=(jax.ShapeDtypeStruct((local, width...]
    ppermute x20 -> x0, waiting for transfers between devices: 115 us -> none  [scatter_rows(): got = lax.ppermute(give, axis, [(i, i ^ 1 << bit) for i in range(size)])]
    psum x1 -> x0, blocking collectives: 43 us -> none  [per_device(): grad_scale = lax.psum(scale_terms, 'dp')]
    convert_element_type x21 -> x4, other arithmetic: 33.1 us -> 6.17 us  [the longest x1 4.56 us: per_device_chips(): grad_hidden_low = grad_hidden.astype(jnp.bfloat16)]
    dot_general x8 -> x4, matrix products: 51 us -> 24.3 us  [the longest x1 8.63 us: per_device_chips(): jnp.dot(activated_low, feed_down, preferred_element_type=jnp.float32)]
    all_to_all x8 -> x5, waiting for transfers between devices: 83.7 us -> 60.2 us  [the longest x1 19.5 us: per_device_chips(): lax.all_to_all(triple[:, :width], 'seq', split_axis=1, concat_axis=0, til...]
    ppermute x20 -> x0, starting transfers between devices: 19 us -> none  [scatter_rows(): got = lax.ppermute(give, axis, [(i, i ^ 1 << bit) for i in range(size)])]
    all_to_all x8 -> x5, starting transfers between devices: 33.5 us -> 20.6 us  [the longest x1 5.51 us: per_device_chips(): lax.all_to_all(triple[:, :width], 'seq', split_axis=1, concat_axis=0, til...]
  transfers between devices with their start and end apart: 32 -> 9, of which waited for: 14 -> 5; matrix products, arithmetic and copies ran while one was open for 20% -> 8% of each run, Pallas kernels for 4% -> 5%
where the time goes in v2:
time: 477 us; the launch traced here: 476 us
  Pallas kernels  204 us (43%)
  waiting for transfers between devices  111 us (23%)
  matrix products  41.8 us (9%)
  blocking collectives  38.6 us (8%)
  local copies, waits for them, and re-layouts  23.1 us (5%)
  other arithmetic  22.9 us (5%)
  starting transfers between devices  20.8 us (4%)
  between operations  14.2 us (3%)
    pallas_call x1, Pallas kernels, tail(): pl.pallas_call(tail_kernel, out_shape=(jax.ShapeDtypeStruct((local, width...  152 us
    all_gather x1, waiting for transfers between devices, per_device_chips(): lax.all_gather(triple_weight, 'dp', axis=0, tiled=True)  47.8 us
    all_gather x1, blocking collectives, per_device_chips(): doc_ids = lax.all_gather(segment_ids[0], 'seq', axis=0, tiled=True)  38.6 us
    pallas_call x1, Pallas kernels, attend_backward(): pl.pallas_call(functools.partial(backward_kernel, heads), out_shape=(jax....  27.1 us
    pallas_call x1, Pallas kernels, attend_forward(): pl.pallas_call(functools.partial(forward_kernel, heads), out_shape=(jax.S...  25.2 us
    all_to_all x1, waiting for transfers between devices, per_device_chips(): lax.all_to_all(triple[:, :width], 'seq', split_axis=1, concat_axis=0, til...  19.5 us
    all_to_all x1, waiting for transfers between devices, per_device_chips(): lax.all_to_all(triple[:, width:2 * width], 'seq', split_axis=1, concat_ax...  19.4 us
    dot_general x3, matrix products, times_transposed(): lax.dot_general(left, right, (((1,), (1,)), ((), ())), preferred_element_...  17.5 us
  transfers between devices with their start and end apart: 9, of which 5 were waited for; matrix products, arithmetic and copies ran while one was open for 8% of the time, Pallas kernels for 5%

profile of v2, /device:TPU:0, one launch (start us, length us, event | category | flops | bytes accessed | tf_op | source)
XLA Modules:
  0.0 476.2 jit_solution(5759847881699530008)
XLA Ops:
  7.2 0.7 all-gather.6.cloned.1.call-update
  8.0 0.7 all-gather.8.cloned.1.call-update
  8.7 0.7 all-gather.10.cloned.1.call-update
  9.5 0.5 all-gather.12.cloned.1.call-update
  10.0 0.2 convert_reduce_fusion
  10.2 0.4 fusion.9
  10.6 0.3 fusion.11.act_in
  10.9 47.8 %all-gather.6.cloned.1.call-done.triple = bf16[1024,3072]{1,0:T(8,128)(2,1)} async-done(((bf16[256,3072]{1,0:T(8,128)(2,1)}), bf16[1024,3072]{1,0:T(8,128)(2,1)}) %all-gather.6.cloned.1.call-update) | async-done | bytes 6291472 | tf_op jit(solution)/shard_map/all_gather | solution.py:838
  58.7 5.6 %convolution_convert_fusion = bf16[384,3072]{1,0:T(8,128)(2,1)S(1)} fusion(bf16[384,1024]{1,0:T(8,128)(2,1)S(1)} %fusion.11.act_in, bf16[1024,3072]{1,0:T(8,128)(2,1)} %all-gather.6.cloned.1.call-done.triple), kind=kOutput, calls=%fused_computation.15 | convolution fusion | flops 2417098752 | bytes 9437184 | tf_op jit(solution)/shard_map/dot_general | solution.py:843
  64.4 0.5 slice_bitcast_fusion
  64.9 1.0 copy.64
  65.9 5.5 %all-to-all-start = ((bf16[384,8,128]{2,0,1:T(8,128)(2,1)}), bf16[384,8,128]{2,0,1:T(8,128)(2,1)S(1)}, u32[]{:S(2)}, u32[]{:S(2)}) async-start(bf16[384,8,128]{2,0,1:T(8,128)(2,1)} %bitcast.85), calls=%async_computation | async-start | bytes 1572864 | tf_op jit(solution)/shard_map/all_to_all | solution.py:847
  71.4 1.0 copy.63
  72.4 19.5 %all-to-all-done = bf16[384,8,128]{2,0,1:T(8,128)(2,1)S(1)} async-done(((bf16[384,8,128]{2,0,1:T(8,128)(2,1)}), bf16[384,8,128]{2,0,1:T(8,128)(2,1)S(1)}, u32[]{:S(2)}, u32[]{:S(2)}) %all-to-all-start) | async-done | bytes 786464 | tf_op jit(solution)/shard_map/all_to_all | solution.py:847
  92.0 3.6 all-to-all-start.1
  95.6 1.0 copy.62
  96.6 19.4 %all-to-all-done.1 = bf16[384,8,128]{2,0,1:T(8,128)(2,1)S(1)} async-done(((bf16[384,8,128]{2,0,1:T(8,128)(2,1)}), bf16[384,8,128]{2,0,1:T(8,128)(2,1)S(1)}, u32[]{:S(2)}, u32[]{:S(2)}) %all-to-all-start.1) | async-done | bytes 786464 | tf_op jit(solution)/shard_map/all_to_all | solution.py:848
  116.0 3.5 all-to-all-start.2
  119.6 38.6 %all-gather = s32[1,3072]{1,0:T(1,128)S(1)} all-gather(s32[1,384]{1,0:T(1,128)S(1)} %copy-done.18), channel_id=2, replica_groups=mesh['dp'=4,'seq'=8] {'seq'}, dimensions={1}, use_global_device_ids=true | all-gather | bytes 13824 | tf_op jit(solution)/shard_map/all_gather | solution.py:836
  158.2 0.1 convert_reduce_fusion.1
  158.3 0.1 select_reduce_fusion
  158.6 0.6 broadcast_in_dim_reshape.3.scale_ref
  159.2 0.2 fusion.14
  159.4 0.5 and_select_fusion
  160.0 0.9 copy-done.12
  160.8 25.2 %attend_forward.1 = (f32[3072,128]{1,0:T(8,128)}, bf16[3072,128]{1,0:T(8,128)(2,1)}, f32[12,1,512]{2,1,0:T(1,128)}) custom-call(s32[12]{0:T(128)} %get-tuple-element.70.lo_ref, s32[12]{0:T(128)} %get-tuple-element.69.full_ref, bf16[3072,128]{1,0:T(8,128)(2,1)} %bitcast.89, bf16[3072,128]{1,0:T(8,128)(2,1)} %bitcast.91, bf16[3072,128]{1,0:T(8,128)(2,1)} %bitcast.93, ...), custom_call_target="tpu_custom_call" | custom-call | flops 1207959552 | bytes 6291456 | tf_op jit(solution)/shard_map/attend_forward/pallas_call | solution.py:97
  186.1 3.7 all-to-all-start.3
  189.8 1.3 convert_reduce_fusion.2.full_ref
  191.1 14.1 %all-to-all-done.3 = bf16[8,384,128]{2,1,0:T(8,128)(2,1)S(1)} async-done(((bf16[8,384,128]{2,1,0:T(8,128)(2,1)}), bf16[8,384,128]{2,1,0:T(8,128)(2,1)S(1)}, u32[]{:S(2)}, u32[]{:S(2)}) %all-to-all-start.3) | async-done | bytes 786464 | tf_op jit(solution)/shard_map/all_to_all | solution.py:862
  205.2 2.9 fusion.26
  208.1 0.3 multiply_reduce_fusion.8
  208.5 1.6 fusion.25
  210.1 0.3 multiply_reduce_fusion.7
  210.4 1.2 multiply_convert_fusion.1.act_up
  211.6 7.1 %fusion.21 = (f32[384]{0:T(512)S(1)}, f32[384,4096]{1,0:T(8,128)S(1)}) fusion(bf16[384,1024]{1,0:T(8,128)(2,1)} %multiply_convert_fusion.1.act_up, bf16[1024,4096]{1,0:T(8,128)(2,1)} %all-gather.10.cloned.1.call-done), kind=kOutput, calls=%fused_computation.91 | convolution fusion | flops 3235380736 | bytes 15468032 | tf_op jit(solution)/shard_map/dot_general | solution.py:872
  218.8 2.6 copy-done
  221.4 2.6 multiply_reduce_fusion.2
  224.0 9.0 %multiply_reduce_fusion = (f32[4096]{0:T(1024)S(1)}, f32[384]{0:T(512)S(1)}, f32[384,4096]{1,0:T(8,128)S(1)}) fusion(f32[384]{0:T(512)S(1)} %fusion.17, f32[384]{0:T(512)S(1)} %broadcast_multiply_fusion, f32[384,4096]{1,0:T(8,128)} %copy-done, f32[4096]{0:T(1024)S(1)} %copy-done.17, bf16[4096,1024]{1,0:T(8,128)(2,1)} %all-gather.12.cloned.1.call-done, ...), kind=kOutput, calls=%fused_computation.10 | convolution fusion | flops 3244813824 | bytes 21795328 | tf_op jit(solution)/shard_map/dot_general | solution.py:275
  233.1 5.8 %fusion.24 = (f32[384]{0:T(512)S(1)}, f32[384,4096]{1,0:T(8,128)S(1)}, bf16[384,4096]{1,0:T(8,128)(2,1)}) fusion(f32[384]{0:T(512)S(1)} %multiply_multiply_fusion.5, f32[384]{0:T(512)S(1)} %broadcast_multiply_fusion, f32[384,4096]{1,0:T(8,128)S(1)} %copy-done.1, f32[384]{0:T(512)S(1)} %fusion.17, f32[384,4096]{1,0:T(8,128)S(1)} %get-tuple-element.67, ...), kind=kLoop, calls=%fused_computation.94 | loop fusion | flops 28311168 | bytes 22042624 | tf_op jit(solution)/shard_map/transpose(jvp())/reduce_sum | solution.py:259
  238.9 4.6 fusion.6.g_up
  243.5 7.5 %multiply_reduce_fusion.3 = (f32[1024]{0:T(1024)S(1)}, f32[384]{0:T(512)S(1)}, f32[384,1024]{1,0:T(8,128)S(1)}) fusion(f32[384,1024]{1,0:T(8,128)S(1)} %get-tuple-element.53, f32[384]{0:T(512)S(1)} %fusion.16, f32[384]{0:T(512)S(1)} %broadcast_multiply_fusion.1, f32[1024]{0:T(1024)S(1)} %copy-done.16, bf16[384,4096]{1,0:T(8,128)(2,1)S(1)} %fusion.6.g_up, ...), kind=kOutput, calls=%fused_computation.26 | convolution fusion | flops 3223976448 | bytes 14692864 | tf_op jit(solution)/shard_map/dot_general | solution.py:275
  251.0 0.6 fusion.23
  251.6 0.8 multiply_reduce_fusion.4
  252.4 0.6 fusion.22
  253.0 0.1 add_convert_fusion.g_out
  253.2 1.0 fusion.13
  254.2 1.0 copy.61
  255.3 4.2 all-to-all-start.4
  259.5 0.6 convert_reduce_fusion.3.hi_ref
  260.1 1.0 copy_bitcast_fusion.act_out
  261.2 8.6 %fusion.12 = bf16[1,384,1024]{2,1,0:T(8,128)(2,1)} fusion(f32[384,1024]{1,0:T(8,128)S(1)} %get-tuple-element.53, bf16[384,4096]{1,0:T(8,128)(2,1)} %get-tuple-element.54.act_down, bf16[4096,1024]{1,0:T(8,128)(2,1)} %all-gather.12.cloned.1.call-done), kind=kOutput, calls=%fused_computation.37 | convolution fusion | flops 3222011904 | bytes 13893632 | tf_op jit(solution)/shard_map/dot_general | solution.py:876
  269.8 7.2 %all-to-all-done.4 = bf16[384,8,128]{2,0,1:T(8,128)(2,1)} async-done(((bf16[384,8,128]{2,0,1:T(8,128)(2,1)}), bf16[384,8,128]{2,0,1:T(8,128)(2,1)}, u32[]{:S(2)}, u32[]{:S(2)}) %all-to-all-start.4) | async-done | bytes 786464 | tf_op jit(solution)/shard_map/all_to_all | solution.py:888
  277.0 27.1 %attend_backward.1 = (bf16[3072,128]{1,0:T(8,128)(2,1)}, bf16[3072,128]{1,0:T(8,128)(2,1)}, bf16[3072,128]{1,0:T(8,128)(2,1)}, f32[1,128]{1,0:T(1,128)}) custom-call(s32[12]{0:T(128)} %convert_reduce_fusion.3.hi_ref, s32[12]{0:T(128)} %convert_reduce_fusion.2.full_ref, bf16[3072,128]{1,0:T(8,128)(2,1)} %bitcast.90, bf16[3072,128]{1,0:T(8,128)(2,1)} %bitcast.92, ...), custom_call_target="tpu_custom_call" | custom-call | flops 3623878656 | bytes 12582912 | tf_op jit(solution)/shard_map/attend_backward/pallas_call | solution.py:208
  304.1 0.7 pad.4
  304.7 0.7 concatenate.3.gains
  305.4 151.9 %tail.1 = (bf16[384,1024]{1,0:T(8,128)(2,1)}, f32[32,3072]{1,0:T(8,128)}, f32[32,1024]{1,0:T(8,128)}, f32[32,4096]{1,0:T(8,128)}, f32[128,1024]{1,0:T(8,128)}, /*index=5*/f32[8,128]{1,0:T(8,128)}) custom-call(bf16[3072,128]{1,0:T(8,128)(2,1)} %get-tuple-element.27.dq, bf16[3072,128]{1,0:T(8,128)(2,1)} %get-tuple-element.28.dk, ...), custom_call_target="tpu_custom_call" | custom-call | tf_op jit(solution)/shard_map/tail/pallas_call | solution.py:654
  457.3 1.3 slice_bitcast_fusion.3
  458.5 1.3 slice_bitcast_fusion.4
  459.9 0.6 reduce_sum.255
  460.6 2.1 copy.70
  462.6 1.8 copy.71
  464.4 1.6 copy.72
  466.0 1.9 copy.73
  467.8 1.9 copy.74
  (70 shorter events, 0.6 us)
Async XLA Ops:
  7.2 2.8 copy-start.2
  7.2 3.4 copy-start.15
  7.2 51.5 %all-gather.6.cloned.1.call-start = ((), (), s32[]{:S(2)}) async-start(), calls=%async_computation.5 | async-start | bytes 7864320 | tf_op jit(solution)/shard_map/all_gather | solution.py:838
  7.9 183.2 %all-gather.8.cloned.1.call-start = ((), (), s32[]{:S(2)}) async-start(), calls=%async_computation.6 | async-start | bytes 2621440 | tf_op jit(solution)/shard_map/all_gather | solution.py:839
  8.7 202.9 %all-gather.10.cloned.1.call-start = ((), (), s32[]{:S(2)}) async-start(), calls=%async_computation.7 | async-start | bytes 10485760 | tf_op jit(solution)/shard_map/all_gather | solution.py:869
  9.4 214.6 %all-gather.12.cloned.1.call-start = ((), (), s32[]{:S(2)}) async-start(), calls=%async_computation.8 | async-start | bytes 10485760 | tf_op jit(solution)/shard_map/all_gather | solution.py:870
  10.9 53.5 %copy-start.5 = (bf16[384,1024]{1,0:T(8,128)(2,1)}, bf16[384,1024]{1,0:T(8,128)(2,1)S(1)}, u32[]{:S(2)}) copy-start(bf16[384,1024]{1,0:T(8,128)(2,1)S(1)} %fusion.11.act_in) | copy-start | bytes 2359300
  64.3 55.2 %copy-start.18 = (s32[1,384]{1,0:T(1,128)S(1)}, s32[1,384]{1,0:T(1,128)}, u32[]{:S(2)}) copy-start(s32[1,384]{1,0:T(1,128)} %param.13) | copy-start | bytes 4612
  64.3 94.1 %copy-start.21 = (f32[16]{0:T(128)S(1)}, f32[16]{0:T(128)}, u32[]{:S(2)}) copy-start(f32[16]{0:T(128)} %param.16) | copy-start | bytes 196
  65.9 26.1 %all-to-all-start = ((bf16[384,8,128]{2,0,1:T(8,128)(2,1)}), bf16[384,8,128]{2,0,1:T(8,128)(2,1)S(1)}, u32[]{:S(2)}, u32[]{:S(2)}) async-start(bf16[384,8,128]{2,0,1:T(8,128)(2,1)} %bitcast.85), calls=%async_computation | async-start | bytes 1572864 | tf_op jit(solution)/shard_map/all_to_all | solution.py:847
  92.0 68.0 %copy-start.10 = (bf16[384,8,128]{2,0,1:T(8,128)(2,1)}, bf16[384,8,128]{2,0,1:T(8,128)(2,1)S(1)}, u32[]{:S(2)}) copy-start(bf16[384,8,128]{2,0,1:T(8,128)(2,1)S(1)} %all-to-all-done) | copy-start | bytes 2359300
  92.0 24.0 %all-to-all-start.1 = ((bf16[384,8,128]{2,0,1:T(8,128)(2,1)}), bf16[384,8,128]{2,0,1:T(8,128)(2,1)S(1)}, u32[]{:S(2)}, u32[]{:S(2)}) async-start(bf16[384,8,128]{2,0,1:T(8,128)(2,1)} %bitcast.84), calls=%async_computation.1 | async-start | bytes 1572864 | tf_op jit(solution)/shard_map/all_to_all | solution.py:848
  116.0 44.0 %copy-start.11 = (bf16[384,8,128]{2,0,1:T(8,128)(2,1)}, bf16[384,8,128]{2,0,1:T(8,128)(2,1)S(1)}, u32[]{:S(2)}) copy-start(bf16[384,8,128]{2,0,1:T(8,128)(2,1)S(1)} %all-to-all-done.1) | copy-start | bytes 2359300
  116.0 43.9 %all-to-all-start.2 = ((bf16[384,8,128]{2,0,1:T(8,128)(2,1)}), bf16[384,8,128]{2,0,1:T(8,128)(2,1)S(1)}, u32[]{:S(2)}, u32[]{:S(2)}) async-start(bf16[384,8,128]{2,0,1:T(8,128)(2,1)} %bitcast.83), calls=%async_computation.2 | async-start | bytes 1572864 | tf_op jit(solution)/shard_map/all_to_all | solution.py:851
  158.4 1.5 copy-start.13
  159.9 0.9 copy-start.12
  160.8 47.7 %copy-start.14 = (f32[1024]{0:T(1024)S(1)}, f32[1024]{0:T(1024)}, u32[]{:S(2)}) copy-start(f32[1024]{0:T(1024)} %param.18) | copy-start | bytes 12292
  186.1 19.1 %all-to-all-start.3 = ((bf16[8,384,128]{2,1,0:T(8,128)(2,1)}), bf16[8,384,128]{2,1,0:T(8,128)(2,1)S(1)}, u32[]{:S(2)}, u32[]{:S(2)}) async-start(bf16[8,384,128]{2,1,0:T(8,128)(2,1)} %bitcast.96), calls=%async_computation.3 | async-start | bytes 1572864 | tf_op jit(solution)/shard_map/all_to_all | solution.py:862
  189.8 20.6 %copy-start.16 = (f32[1024]{0:T(1024)S(1)}, f32[1024]{0:T(1024)}, u32[]{:S(2)}) copy-start(f32[1024]{0:T(1024)} %param.19) | copy-start | bytes 12292
  205.2 3.3 copy-start.8
  218.7 2.7 copy-start
  218.7 5.3 %copy-start.17 = (f32[4096]{0:T(1024)S(1)}, f32[4096]{0:T(1024)}, u32[]{:S(2)}) copy-start(f32[4096]{0:T(1024)} %param.21) | copy-start | bytes 49156
  224.0 9.0 %copy-start.1 = (f32[384,4096]{1,0:T(8,128)S(1)}, f32[384,4096]{1,0:T(8,128)}, u32[]{:S(2)}) copy-start(f32[384,4096]{1,0:T(8,128)} %copy-done) | copy-start | bytes 18874372
  243.4 7.5 %copy-start.4 = (bf16[384,4096]{1,0:T(8,128)(2,1)}, bf16[384,4096]{1,0:T(8,128)(2,1)S(1)}, u32[]{:S(2)}) copy-start(bf16[384,4096]{1,0:T(8,128)(2,1)S(1)} %fusion.6.g_up) | copy-start | bytes 9437188
  243.5 8.1 %copy-start.7 = (bf16[1,384,1024]{2,1,0:T(8,128)(2,1)S(1)}, bf16[1,384,1024]{2,1,0:T(8,128)(2,1)}, u32[]{:S(2)}) copy-start(bf16[1,384,1024]{2,1,0:T(8,128)(2,1)} %param.23) | copy-start | bytes 2359300
  251.6 1.6 copy-start.20
  252.4 2.9 copy-start.3
  253.0 6.5 %copy-start.19 = (s32[12]{0:T(128)S(1)}, s32[12]{0:T(128)}, u32[]{:S(2)}) copy-start(s32[12]{0:T(128)} %get-tuple-element.70.lo_ref) | copy-start | bytes 148
  253.0 7.1 %copy-start.9 = (bf16[8,384,128]{2,1,0:T(8,128)(2,1)S(1)}, bf16[8,384,128]{2,1,0:T(8,128)(2,1)}, u32[]{:S(2)}) copy-start(bf16[8,384,128]{2,1,0:T(8,128)(2,1)} %copy-done.8) | copy-start | bytes 2359300
  253.2 16.6 %copy-start.6 = (bf16[384,1024]{1,0:T(8,128)(2,1)}, bf16[384,1024]{1,0:T(8,128)(2,1)S(1)}, u32[]{:S(2)}) copy-start(bf16[384,1024]{1,0:T(8,128)(2,1)S(1)} %add_convert_fusion.g_out) | copy-start | bytes 2359300
  255.3 21.7 %all-to-all-start.4 = ((bf16[384,8,128]{2,0,1:T(8,128)(2,1)}), bf16[384,8,128]{2,0,1:T(8,128)(2,1)}, u32[]{:S(2)}, u32[]{:S(2)}) async-start(bf16[384,8,128]{2,0,1:T(8,128)(2,1)} %bitcast.88), calls=%async_computation.4 | async-start | bytes 1572864 | tf_op jit(solution)/shard_map/all_to_all | solution.py:888
Sparse Core Ops, SparseCore 0:
  9.6 49.0 all-gather.5
  60.3 22.5 all-gather.7
  84.5 58.2 all-gather.9
  144.2 58.2 all-gather.11

commit v3 on v2

--- a/solution.py
+++ b/solution.py
@@ -37,7 +37,7 @@
     )
 
 
-def forward_kernel(heads, lo_ref, full_ref, q_ref, k_ref, v_ref, start_ref, scale_ref,
+def forward_kernel(heads, first_ref, q_ref, k_ref, v_ref, start_ref, scale_ref,
                    o_ref, u_ref, lse_ref, m_s, l_s, acc_s):
     i = pl.program_id(0)
     rows = q_ref.shape[0]
@@ -69,7 +69,8 @@
         acc_s[...] = acc_s[...] * fade + tn(v_ref[at, :], weights.astype(jnp.bfloat16))
 
     step(i, False, True)
-    full = jnp.minimum(full_ref[i], i)
+    low = first_ref[i, 0, 0] // rows
+    full = jnp.minimum((first_ref[i, 0, rows - 1] + rows - 1) // rows, i)
 
     def plain(j, carry):
         step(j, False, False)
@@ -80,7 +81,7 @@
         return carry
 
     lax.fori_loop(full, i, plain, 0)
-    lax.fori_loop(lo_ref[i], full, edge, 0)
+    lax.fori_loop(low, full, edge, 0)
     total = l_s[...]
     out = unstack_heads(acc_s[...] / total, heads).T
     o_ref[...] = out
@@ -88,7 +89,7 @@
     lse_ref[0] = m_s[...] + jnp.log(total)
 
 
-def attend_forward(queries, keys, values, bounds, starts, scale_wide):
+def attend_forward(queries, keys, values, starts, scale_wide):
     length, width = queries.shape
     heads = width // HEAD
     blocks = length // BQ
@@ -102,7 +103,7 @@
             jax.ShapeDtypeStruct((blocks, 1, heads * BQ), jnp.float32),
         ),
         grid_spec=pltpu.PrefetchScalarGridSpec(
-            num_scalar_prefetch=2,
+            num_scalar_prefetch=1,
             grid=(blocks,),
             in_specs=[
                 mine,
@@ -122,10 +123,10 @@
             flops=length * length * width, bytes_accessed=16 * length * width, transcendentals=0
         ),
         name="attend_forward",
-    )(bounds[0], bounds[1], queries, keys, values, starts.reshape(blocks, 1, BQ), scale_wide)
-
-
-def backward_kernel(heads, hi_ref, full_ref, q_ref, k_ref, v_ref, o_ref, du_ref, start_ref, scale_ref, lse_ref,
+    )(starts, queries, keys, values, starts, scale_wide)
+
+
+def backward_kernel(heads, first_ref, q_ref, k_ref, v_ref, o_ref, du_ref, start_ref, scale_ref, lse_ref,
                     dq_ref, dk_ref, dv_ref, ds_ref, qs_s, dos_s, delta_s, dqt_s, dk_s, dv_s):
     j = pl.program_id(0)
     rows = k_ref.shape[0]
@@ -174,7 +175,11 @@
         dqt_s[i] += tn(keys, low)
 
     step(j, False, True)
-    full = jnp.maximum(full_ref[j], j + 1)
+    high, full = jnp.int32(0), jnp.int32(0)
+    for i in range(blocks):
+        high += (first_ref[i, 0, 0] // rows <= j).astype(jnp.int32)
+        full += ((first_ref[i, 0, rows - 1] + rows - 1) // rows <= j).astype(jnp.int32)
+    full = jnp.maximum(full, j + 1)
 
     def plain(i, carry):
         step(i, False, False)
@@ -185,7 +190,7 @@
         return carry
 
     lax.fori_loop(j + 1, full, plain, 0)
-    lax.fori_loop(full, hi_ref[j], edge, 0)
+    lax.fori_loop(full, high, edge, 0)
     dk_ref[...] = dk_s[...].astype(jnp.bfloat16)
     dv_ref[...] = dv_s[...].astype(jnp.bfloat16)
 
@@ -199,7 +204,7 @@
         lax.fori_loop(0, blocks, one, 0)
 
 
-def attend_backward(queries, keys, values, outs, grads, bounds, starts, scale_wide, logsum):
+def attend_backward(queries, keys, values, outs, grads, starts, scale_wide, logsum):
     length, width = queries.shape
     heads = width // HEAD
     blocks = length // BQ
@@ -210,7 +215,7 @@
         out_shape=(jax.ShapeDtypeStruct((length, width), jnp.bfloat16),) * 3
         + (jax.ShapeDtypeStruct((1, width), jnp.float32),),
         grid_spec=pltpu.PrefetchScalarGridSpec(
-            num_scalar_prefetch=2,
+            num_scalar_prefetch=1,
             grid=(blocks,),
             in_specs=[
                 whole,
@@ -236,23 +241,17 @@
             flops=3 * length * length * width, bytes_accessed=32 * length * width, transcendentals=0
         ),
         name="attend_backward",
-    )(bounds[2], bounds[3], queries, keys, values, outs, grads, starts.reshape(blocks, 1, BQ), scale_wide, logsum)
-
-
-def document_bounds(doc_ids):
+    )(starts, queries, keys, values, outs, grads, starts, scale_wide, logsum)
+
+
+def document_starts(doc_ids):
     length = doc_ids.shape[0]
-    blocks = length // BQ
-    counts = jnp.sum(doc_ids[None, :] < jnp.arange(8, dtype=jnp.int32)[:, None], axis=1, dtype=jnp.int32)
+    names = jnp.arange(8, dtype=jnp.int32)
+    counts = jnp.sum(doc_ids[None, :] < names[:, None], axis=1, dtype=jnp.int32)
     starts = jnp.sum(
-        jnp.where(doc_ids[:, None] == jnp.arange(8, dtype=jnp.int32)[None, :], counts[None, :], 0), axis=1, dtype=jnp.int32
-    )
-    by_block = starts.reshape(blocks, BQ)
-    low = by_block[:, 0] // BQ
-    full = (by_block[:, BQ - 1] + BQ - 1) // BQ
-    index = jnp.arange(blocks, dtype=jnp.int32)
-    high = jnp.sum(low[None, :] <= index[:, None], axis=1, dtype=jnp.int32)
-    full_high = jnp.sum(full[None, :] <= index[:, None], axis=1, dtype=jnp.int32)
-    return (low, full, high, full_high), starts
+        jnp.where(doc_ids[:, None] == names[None, :], counts[None, :], 0), axis=1, dtype=jnp.int32
+    )
+    return starts.reshape(length // BQ, 1, BQ)
 
 
 def layer_norm(values, gains):
@@ -341,6 +340,160 @@
     )
 
 
+def lanes_of(z, x, width):
+    return pl.ds(pl.multiple_of((z * 2 + x) * width, 128), width)
+
+
+def rows_of(z, x, local):
+    return pl.ds(pl.multiple_of((z * 2 + x) * local, 128), local)
+
+
+class ToHeads:
+    def __init__(self, place, part, target, relay, sems, keep_sem):
+        self.place, self.target, self.relay, self.sems = place, target, relay, sems
+        x_send, x_recv, z_send, z_recv = sems
+        local, width = relay.shape[-2:]
+        rows = rows_of(place.z, place.x, local)
+        self.moves, self.sends = [], []
+        for k in (2, 1, 3, 0):
+            source = part.at[:, lanes_of((place.z + k) % 4, 1 - place.x, width)]
+            landing = target.at[rows, :] if k == 0 else relay.at[k - 1]
+            move = remote(source, landing, x_send.at[k], x_recv.at[k], place.x_partner())
+            move.start()
+            (self.moves if k == 0 else self.sends).append(move)
+        for k in (2, 1, 3):
+            z = (place.z + k) % 4
+            source = part.at[:, lanes_of(z, place.x, width)]
+            move = remote(
+                source, target.at[rows, :], z_send.at[k - 1], z_recv.at[k - 1], (place.dp, z * 2 + place.x)
+            )
+            move.start()
+            self.moves.append(move)
+        source = part.at[:, lanes_of(place.z, place.x, width)]
+        move = pltpu.make_async_copy(source, target.at[rows, :], keep_sem)
+        move.start()
+        self.moves.append(move)
+
+    def pass_on(self):
+        place, local = self.place, self.relay.shape[-2]
+        x_send, x_recv, z_send, z_recv = self.sems
+        rows = rows_of(place.z, 1 - place.x, local)
+        for k in (2, 1, 3):
+            here = self.relay.at[k - 1]
+            remote(here, here, x_send.at[k], x_recv.at[k], place.x_partner()).wait_recv()
+            device = (place.dp, (place.z + k) % 4 * 2 + place.x)
+            move = remote(here, self.target.at[rows, :], z_send.at[k + 2], z_recv.at[k + 2], device)
+            move.start()
+            self.moves.append(move)
+
+    def finish(self):
+        for move in self.moves:
+            move.wait()
+        for move in self.sends:
+            move.wait_send()
+
+
+class ToTokens:
+    def __init__(self, place, source, target, relay, sems, keep_sem):
+        self.place, self.target, self.relay, self.sems = place, target, relay, sems
+        x_send, x_recv, z_send, z_recv = sems
+        local, width = relay.shape[-2:]
+        self.moves, self.sends = [], []
+        lanes = lanes_of(place.z, place.x, width)
+        for x, first in ((1 - place.x, 0), (place.x, 3)):
+            for k in (2, 1, 3):
+                z, index = (place.z + k) % 4, first + k - 1
+                landing = relay.at[k - 1] if first == 0 else target.at[:, lanes]
+                move = remote(
+                    source.at[rows_of(z, x, local), :],
+                    landing,
+                    z_send.at[index],
+                    z_recv.at[index],
+                    (place.dp, z * 2 + place.x),
+                )
+                move.start()
+                (self.sends if first == 0 else self.moves).append(move)
+        move = remote(
+            source.at[rows_of(place.z, 1 - place.x, local), :],
+            target.at[:, lanes],
+            x_send.at[0],
+            x_recv.at[0],
+            place.x_partner(),
+        )
+        move.start()
+        self.moves.append(move)
+        move = pltpu.make_async_copy(
+            source.at[rows_of(place.z, place.x, local), :], target.at[:, lanes], keep_sem
+        )
+        move.start()
+        self.moves.append(move)
+
+    def pass_on(self):
+        place, width = self.place, self.relay.shape[-1]
+        x_send, x_recv, z_send, z_recv = self.sems
+        for k in (2, 1, 3):
+            here = self.relay.at[k - 1]
+            remote(here, here, z_send.at[k - 1], z_recv.at[k - 1], place.near_partner()).wait_recv()
+            lanes = lanes_of((place.z + 4 - k) % 4, place.x, width)
+            move = remote(here, self.target.at[:, lanes], x_send.at[k], x_recv.at[k], place.x_partner())
+            move.start()
+            self.moves.append(move)
+
+    def finish(self):
+        for move in self.moves:
+            move.wait()
+        for move in self.sends:
+            move.wait_send()
+
+
+def exchange_sems(count):
+    dma = pltpu.SemaphoreType.DMA
+    return [dma((count, 4)), dma((count, 4)), dma((count, 6)), dma((count, 6))]
+
+
+def share(place, index, ours, theirs, target, local, here_sem, core_send, core_recv):
+    here = pltpu.make_async_copy(ours, target.at[pl.ds(0, local), :], here_sem.at[index])
+    there = remote(
+        theirs, target.at[pl.ds(local, local), :], core_send.at[index], core_recv.at[index], place.core_partner()
+    )
+    here.start()
+    there.start()
+    return [here, there]
+
+
+def share_left(place, index, source, target, local, *sems):
+    half = source.shape[1] // 2
+    columns = half // 2
+    out = []
+    for y in range(2):
+        ours, theirs = (
+            source.at[pl.ds(0, local), pl.ds(pl.multiple_of(y * half + core * columns, 128), columns)]
+            for core in (place.core, 1 - place.core)
+        )
+        out += share(place, index + y, ours, theirs, target.at[:, pl.ds(y * columns, columns)], local, *sems)
+    return out
+
+
+def wait_all(copies):
+    for copy in copies:
+        copy.wait()
+
+
+def norm_parts(values):
+    center = values - jnp.mean(values, axis=-1, keepdims=True)
+    inverse = lax.rsqrt(jnp.mean(center * center, axis=-1, keepdims=True) + 1e-05)
+    return center * inverse, inverse
+
+
+def norm_pull(grad, unit, inverse, gain):
+    scaled = grad * gain
+    return inverse * (
+        scaled
+        - jnp.mean(scaled, axis=-1, keepdims=True)
+        - unit * jnp.mean(scaled * unit, axis=-1, keepdims=True)
+    )
+
+
 class Scatter:
     def __init__(self, place, refs, sems, base, left, right, write):
         self.place, self.base, self.left, self.right, self.write = place, base, left, right, write
@@ -440,85 +593,544 @@
     ]
 
 
-def own_columns(source, core, columns):
-    half = source.shape[1] // 2
-    return [
-        source.at[:, pl.ds(pl.multiple_of(y * half + core * columns, 128), columns)] for y in range(2)
+class Gather:
+    def __init__(self, place, sems):
+        self.place = place
+        self.send, self.receive = sems
+
+    def copies(self, index, own, full, rows, shared):
+        place = self.place
+        across = place.dp + 2 - 4 * place.y
+        half = rows // 2
+
+        def move(kind, source, target, device):
+            return remote(source, target, self.send.at[kind, index], self.receive.at[kind, index], device)
+
+        out = [move(0, own, full(place.dp, 0, rows), place.core_partner())]
+        if shared:
+            first = place.x * half
+            out.append(
+                move(1, own.at[pl.ds(pl.multiple_of(first, half), half), :],
+                     full(place.dp, first, half), place.y_partner())
+            )
+            landed = full(across, first, half)
+            out.append(move(2, landed, landed, place.x_partner()))
+        else:
+            out.append(move(1, own, full(place.dp, 0, rows), place.y_partner()))
+            out.append(None)
+        landed = full(across, 0, rows)
+        out.append(move(3, landed, landed, place.core_partner()))
+        return out
+
+
+def front_kernel(
+    tokens, gain, ids, w_triple, w_out, w_up,
+    o_v, o_k, o_q, o_normed, o_starts, o_triple, o_out, o_up,
+    triple_s, part_s, ids_s, bounce, relay, send, receive, x_send, x_recv, z_send, z_recv, ids_send, ids_recv, local_sem,
+):
+    place = Place()
+    exchange_sem = (x_send, x_recv, z_send, z_recv)
+    local, width = tokens.shape
+    heads_width = o_v.shape[1]
+    meet([(place.dp, (place.seq + k) % 8) for k in range(1, 8)] + [place.core_partner(), place.y_partner()])
+    gather = Gather(place, (send, receive))
+
+    def columns(weight, rows, column):
+        at = pl.ds(column * width, width)
+
+        def full(d, first, count):
+            return weight.at[pl.ds(pl.multiple_of(d * rows + first, 128), count), at]
+
+        return full
+
+    plans = []
+    for n, t in enumerate((2, 1, 0)):
+        plans.append((w_triple.at[:, pl.ds(t * width, width)], columns(triple_s, 256, t)))
+    plans.append((w_out, columns(o_out, 256, 0)))
+    for k in range(w_up.shape[1] // width):
+        plans.append((w_up.at[:, pl.ds(k * width, width)], columns(o_up, 256, k)))
+    alone = (3,)
+    chunks = [
+        gather.copies(n, own, full, 256, n not in alone) for n, (own, full) in enumerate(plans)
     ]
+    mine = []
+    for n, (own, full) in enumerate(plans):
+        chunks[n][1].start()
+        chunks[n][0].start()
+        target = full(place.dp, 0, 256) if n < 3 else bounce.at[n - 3]
+        copy = pltpu.make_async_copy(own, target, local_sem.at[n])
+        copy.start()
+        mine.append(copy)
+        if n == 0:
+            news = []
+            for k in range(1, 8):
+                peer = (place.dp, (place.seq + k) % 8)
+                move = remote(ids, ids_s.at[place.seq], ids_send.at[k - 1], ids_recv.at[k - 1], peer)
+                move.start()
+                news.append(move)
+            ids_s[pl.ds(place.seq, 1)] = ids[...].reshape(1, 1, local)
+
+    def norm_rows(n, carry):
+        rows = pl.ds(pl.multiple_of(n * 128, 128), 128)
+        values = tokens[rows, :].astype(jnp.float32)
+        o_normed[rows, :] = (norm_parts(values)[0] * gain[...]).astype(LOW)
+        return carry
+
+    lax.fori_loop(0, local // 128, norm_rows, 0)
+    moves = []
+    exchanges = []
+
+    def project(n):
+        t, target = (2, 1, 0)[n], (o_v, o_k, o_q)[n]
+
+        def one(c, carry):
+            at = pl.ds(pl.multiple_of(c * 256, 256), 256)
+            from_at = pl.ds(pl.multiple_of(t * width + c * 256, 256), 256)
+            part_s[n, :, at] = jnp.dot(
+                o_normed[...], triple_s[:, from_at], preferred_element_type=jnp.float32
+            ).astype(LOW)
+            return carry
+
+        lax.fori_loop(0, width // 256, one, 0)
+        exchange = ToHeads(
+            place, part_s.at[n], target, relay.at[n], [sem.at[n] for sem in exchange_sem], local_sem.at[12 + n]
+        )
+        exchanges.append(exchange)
+        save = pltpu.make_async_copy(
+            triple_s.at[:, pl.ds(t * width, width)], o_triple.at[:, pl.ds(t * width, width)], local_sem.at[15 + n]
+        )
+        save.start()
+        moves.append(save)
+
+    def forward(n):
+        if chunks[n][2] is not None:
+            chunks[n][1].wait_recv()
+            chunks[n][2].start()
+
+    def across(n):
+        (chunks[n][1] if chunks[n][2] is None else chunks[n][2]).wait_recv()
+        chunks[n][3].start()
+
+    def finish(n):
+        chunks[n][0].wait_recv()
+        chunks[n][3].wait_recv()
+        if n < 3:
+            mine[n].wait()
+            project(n)
+
+    def put_back(n):
+        mine[n].wait()
+        copy = pltpu.make_async_copy(bounce.at[n - 3], plans[n][1](place.dp, 0, 256), local_sem.at[n])
+        copy.start()
+        moves.append(copy)
+
+    count = len(chunks)
+    forward(0)
+    for n in range(count):
+        if n + 1 < count:
+            forward(n + 1)
+        across(n)
+        if n < 3:
+            finish(n)
+        else:
+            put_back(n)
+        if 0 < n < 4:
+            exchanges[n - 1].pass_on()
+        if n == 4:
+            for move in news:
+                move.wait()
+            every = ids_s[...]
+            starts = jnp.zeros_like(every)
+            for d in range(1, 8):
+                before = jnp.sum((every < d).astype(jnp.int32), axis=2, keepdims=True)
+                before = jnp.sum(before, axis=0, keepdims=True)
+                starts = jnp.where(every == d, before, starts)
+            for b in range(o_starts.shape[0]):
+                for piece in range(BQ // 128):
+                    at = b * BQ + piece * 128
+                    o_starts[b, :, pl.ds(piece * 128, 128)] = starts[
+                        at // local, :, at % local : at % local + 128
+                    ]
+    for n in range(3, count):
+        finish(n)
+    for move in moves:
+        move.wait()
+    for exchange in exchanges:
+        exchange.finish()
+    for chunk in chunks:
+        for copy in chunk:
+            if copy is not None:
+                copy.wait_send()
+
+
+def front(tokens, gain, ids, w_triple, w_out, w_up):
+    local, width = tokens.shape
+    heads_width = width // 8
+    length = local * 8
+    hidden = w_up.shape[1]
+    any_spec = pl.BlockSpec(memory_space=pl.ANY)
+    vmem = pl.BlockSpec(memory_space=pltpu.VMEM)
+    dma = pltpu.SemaphoreType.DMA
+    one = jax.ShapeDtypeStruct((length, heads_width), LOW)
+    return pl.pallas_call(
+        front_kernel,
+        out_shape=(
+            one, one, one,
+            jax.ShapeDtypeStruct((local, width), LOW),
+            jax.ShapeDtypeStruct((length // BQ, 1, BQ), jnp.int32),
+            jax.ShapeDtypeStruct((width, 3 * width), LOW),
+            jax.ShapeDtypeStruct((width, width), LOW),
+            jax.ShapeDtypeStruct((width, hidden), LOW),
+        ),
+        in_specs=[vmem] * 3 + [any_spec] * 3,
+        out_specs=(any_spec,) * 3 + (vmem,) * 2 + (any_spec,) * 3,
+        scratch_shapes=[
+            pltpu.VMEM((width, 3 * width), LOW),
+            pltpu.VMEM((3, local, width), LOW),
+            pltpu.VMEM((8, 1, local), jnp.int32),
+            pltpu.VMEM((1 + hidden // width, 256, width), LOW),
+            pltpu.VMEM((3, 3, local, heads_width), LOW),
+            dma((4, 8)),
+            dma((4, 8)),
+            *exchange_sems(3),
+            dma((7,)),
+            dma((7,)),
+            dma((20,)),
+        ],
+        compiler_params=pltpu.CompilerParams(
+            collective_id=1, has_side_effects=True, vmem_limit_bytes=VMEM_BYTES
+        ),
+        name="front",
+    )(tokens, gain.reshape(1, width), ids, w_triple, w_out, w_up)
+
+
+def middle_kernel(
+    u, tokens, cotangent, post_gain, second_gain, mid_gain, w_out, w_up, w_down,
+    o_layer, o_middle, o_heads, o_merged, o_second, o_hidden, o_projected, o_gains, o_down,
+    out_s, up_s, down_s, merged_s, second_s, unit_s, slope_s, act_s, hidden_s, projected_s, middle_s, far_s,
+    inverse_s, inner_s, relay, grad_s,
+    d_left, d_right, d_whole, d_first, d_second, d_near, d_far,
+    local_sem, g_send, g_recv, core_send, core_recv, x_send, x_recv, z_send, z_recv, s_send, s_recv,
+):
+    place = Place()
+    local, width = tokens.shape
+    hidden = mid_gain.shape[1]
+    wide = jnp.float32
+    column_peers = [(place.dp, (place.z + k) % 4 * 2 + place.x) for k in range(1, 4)]
+    meet(column_peers + [place.x_partner(), place.core_partner(), place.y_partner()])
+    exchange_sem = (x_send, x_recv, z_send, z_recv)
+
+    inbound = ToTokens(place, u, merged_s, relay.at[0], [sem.at[0] for sem in exchange_sem], local_sem.at[0])
+    gather = Gather(place, (g_send, g_recv))
+    alone = (0, 1)
+    chunks, mine = [], []
+    for k in range(4):
+
+        def full(d, first, count, k=k):
+            return down_s.at[pl.ds(pl.multiple_of(d * 1024 + k * 256 + first, 128), count), :]
+
+        own = w_down.at[pl.ds(k * 256, 256), :]
+        chunks.append(gather.copies(k, own, full, 256, k not in alone))
+        chunks[k][1].start()
+        chunks[k][0].start()
+        mine.append(pltpu.make_async_copy(own, full(place.dp, 0, 256), local_sem.at[1 + k]))
+        mine[k].start()
+    loads = [
+        pltpu.make_async_copy(w_out, out_s, local_sem.at[5]),
+        pltpu.make_async_copy(w_up, up_s, local_sem.at[6]),
+    ]
+    for load in loads:
+        load.start()
+    sems = (local_sem, core_send, core_recv)
+    right = share(place, 7, cotangent, cotangent, d_right, local, *sems)
+    saves = []
+
+    def save(source, target, index):
+        copy = pltpu.make_async_copy(source, target, local_sem.at[index])
+        copy.start()
+        saves.append(copy)
+
+    def across(k):
+        (chunks[k][1] if chunks[k][2] is None else chunks[k][2]).wait_recv()
+        chunks[k][3].start()
+
+    def forward(k):
+        chunks[k][1].wait_recv()
+        chunks[k][2].start()
+
+    gain = mid_gain[...]
+    part_one = gain.astype(LOW)
+    left_over = gain - part_one.astype(wide)
+    part_two = left_over.astype(LOW)
+    part_three = (left_over - part_two.astype(wide)).astype(LOW)
+    row = lax.broadcasted_iota(jnp.int32, (16, hidden), 0)
+    parts = jnp.where(row == 0, part_one.astype(wide), jnp.where(row == 1, part_two.astype(wide), part_three.astype(wide)))
+    act_s[pl.ds(local, 16), :] = jnp.where(row < 3, parts, 0.0).astype(LOW)
+
+    inbound.pass_on()
+    across(0)
+    forward(2)
+    inbound.finish()
+    wait_all(loads)
+    save(merged_s, o_merged, 8)
+
+    def blocks(count, body):
+        def one(n, carry):
+            body(n)
+            return carry
+
+        lax.fori_loop(0, count, one, 0)
+
+    def span(n, size):
+        return pl.ds(pl.multiple_of(n * size, size), size)
+
+    def project(n):
+        at = span(n, 256)
+        far_s[:, at] = jnp.dot(merged_s[...], out_s[:, at], preferred_element_type=wide)
+
+    blocks(width // 256, project)
+
+    def norms(n):
+        rows = span(n, 128)
+        unit, inverse = norm_parts(far_s[rows, :])
+        far_s[rows, :] = unit
+        inverse_s[rows, :] = jnp.broadcast_to(inverse, (128, 128))
+        middle = tokens[rows, :].astype(wide) + unit * post_gain[...]
+        middle_s[rows, :] = middle
+        second_s[rows, :] = (norm_parts(middle)[0] * second_gain[...]).astype(LOW)
+
+    blocks(local // 128, norms)
+    save(second_s, o_second, 9)
+
+    def grow(n):
+        at = span(n, 256)
+        z = jnp.dot(second_s[...], up_s[:, at], preferred_element_type=wide)
+        root = 0.7978845608028654
+        square = z * z
+        bent = jnp.tanh(root * z * (1.0 + 0.044715 * square))
+        half = 0.5 * (1.0 + bent)
+        unit_s[:, at] = z * half
+        slope_s[:, at] = half + 0.5 * root * z * (1.0 - bent * bent) * (1.0 + 3.0 * 0.044715 * square)
+
+    half_way = hidden // 512
+
+    def grow_from(first):
+        def body(n):
+            grow(n + first)
+
+        return body
+
+    blocks(half_way, grow_from(0))
+    across(1)
+    across(2)
+    forward(3)
+    blocks(half_way, grow_from(half_way))
+
+    def hidden_norm(n):
+        rows = span(n, 32)
+        unit, inverse = norm_parts(unit_s[rows, :])
+        unit_s[rows, :] = unit
+        inner_s[rows, :] = jnp.broadcast_to(inverse, (32, 128))
+        act_s[rows, :] = (unit * gain).astype(LOW)
+
+    blocks(local // 32, hidden_norm)
+    left = share_left(place, 10, act_s, d_left, local, *sems)
+    across(3)
+    for k in range(4):
+        chunks[k][0].wait_recv()
+        chunks[k][3].wait_recv()
+        mine[k].wait()
+
+    def shrink(n):
+        at = span(n, 256)
+        total = jnp.dot(act_s[...], down_s[:, at], preferred_element_type=wide)
+        low = cotangent[:, at].astype(wide)
+        value = total[:local]
+        o_layer[:, at] = (middle_s[:, at] + value).astype(LOW)
+        weight = jnp.sum(total[local:], axis=0, keepdims=True)
+        first = jnp.sum(low * weight, axis=1, keepdims=True) * (1.0 / hidden)
+        second = jnp.sum(low * value, axis=1, keepdims=True) * (1.0 / hidden)
+        grad_s[0] = grad_s[0] + jnp.broadcast_to(first, (local, 128))
+        grad_s[1] = grad_s[1] + jnp.broadcast_to(second, (local, 128))
+
+    grad_s[...] = jnp.zeros_like(grad_s)
+    blocks(width // 256, shrink)
+
+    def write_down(p, value):
+        o_down[:, pl.ds(p * 256, 256)] = value
+
+    down = Scatter(
+        place, (d_whole, d_first, d_second, d_near, d_far), (s_send, s_recv), 0,
+        lambda p: d_left, lambda p: d_right.at[:, pl.ds(p * 256, 256)], write_down,
+    )
+    wait_all(right)
+    wait_all(left)
+    for p in range(4):
+        down.compute(p)
+
+    def pull_hidden(n):
+        at = span(n, 256)
+        grad = nt(cotangent[...], down_s[at, :])
+        unit = unit_s[:, at]
+        o_gains[3:4, at] = jnp.sum(grad * unit, axis=0, keepdims=True)
+        pulled = grad * mid_gain[:, at] - grad_s[0][:, 0:1] - unit * grad_s[1][:, 0:1]
+        hidden_s[:, at] = (inner_s[:, 0:1] * pulled * slope_s[:, at]).astype(LOW)
+
+    blocks(hidden // 256, pull_hidden)
+    save(hidden_s, o_hidden, 15)
+    for p in range(2):
+        down.advance(p, 1)
+
+    def pull_second(n):
+        at = span(n, 256)
+        o_middle[:, at] = nt(hidden_s[...], up_s[at, :])
+
+    blocks(width // 256, pull_second)
+
+    def pull_norms(n, totals):
+        rows = span(n, 128)
+        grad = o_middle[rows, :]
+        unit, inverse = norm_parts(middle_s[rows, :])
+        grad_middle = cotangent[rows, :].astype(wide) + norm_pull(grad, unit, inverse, second_gain[...])
+        o_middle[rows, :] = grad_middle
+        outer = far_s[rows, :]
+        projected_s[rows, :] = norm_pull(grad_middle, outer, inverse_s[rows, 0:1], post_gain[...]).astype(LOW)
+        return (
+            totals[0] + jnp.sum(grad_middle * outer, axis=0, keepdims=True),
+            totals[1] + jnp.sum(grad * unit, axis=0, keepdims=True),
+        )
+
+    nothing = jnp.zeros((1, width), wide)
+    post, second = lax.fori_loop(0, local // 128, pull_norms, (nothing, nothing))
+    o_gains[1:2, 0:width] = post
+    o_gains[2:3, 0:width] = second
+    save(projected_s, o_projected, 16)
+
+    def pull_merged(n):
+        at = span(n, 256)
+        merged_s[:, at] = nt(projected_s[...], out_s[at, :]).astype(LOW)
+
+    saves[0].wait()
+    blocks(width // 256, pull_merged)
+    outbound = ToHeads(
+        place, merged_s, o_heads, relay.at[1], [sem.at[1] for sem in exchange_sem], local_sem.at[17]
+    )
+    down.advance(2, 1)
+    down.advance(0, 2)
+    down.advance(1, 2)
+    outbound.pass_on()
+    down.advance(3, 1)
+    down.advance(2, 2)
+    down.advance(0, 3)
+    down.advance(1, 3)
+    down.advance(3, 2)
+    for p in range(4):
+        if p > 1:
+            down.advance(p, 3)
+    for p in range(4):
+        down.advance(p, 4)
+    outbound.finish()
+    wait_all(saves[1:])
+    for p in range(4):
+        down.settle(p)
+    for chunk in chunks:
+        for copy in chunk:
+            if copy is not None:
+                copy.wait_send()
+
+
+def middle(u, tokens, cotangent, post_gain, second_gain, mid_gain, w_out, w_up, w_down):
+    local, width = tokens.shape
+    hidden = w_up.shape[1]
+    any_spec = pl.BlockSpec(memory_space=pl.ANY)
+    vmem = pl.BlockSpec(memory_space=pltpu.VMEM)
+    dma = pltpu.SemaphoreType.DMA
+    wide = jnp.float32
+    act = jax.ShapeDtypeStruct((local, width), LOW)
+    return pl.pallas_call(
+        middle_kernel,
+        out_shape=(
+            act,
+            jax.ShapeDtypeStruct((local, width), wide),
+            jax.ShapeDtypeStruct((local * 8, width // 8), LOW),
+            act,
+            act,
+            jax.ShapeDtypeStruct((local, hidden), LOW),
+            act,
+            jax.ShapeDtypeStruct((8, hidden), wide),
+            jax.ShapeDtypeStruct((hidden // 32, width), wide),
+        ),
+        in_specs=[any_spec] + [vmem] * 5 + [any_spec] * 3,
+        out_specs=(vmem,) * 2 + (any_spec,) * 5 + (vmem,) * 2,
+        scratch_shapes=[
+            pltpu.VMEM((width, width), LOW),
+            pltpu.VMEM((width, hidden), LOW),
+            pltpu.VMEM((hidden, width), LOW),
+            pltpu.VMEM((local, width), LOW),
+            pltpu.VMEM((local, width), LOW),
+            pltpu.VMEM((local, hidden), wide),
+            pltpu.VMEM((local, hidden), wide),
+            pltpu.VMEM((local + 16, hidden), LOW),
+            pltpu.VMEM((local, hidden), LOW),
+            pltpu.VMEM((local, width), LOW),
+            pltpu.VMEM((local, width), wide),
+            pltpu.VMEM((local, width), wide),
+            pltpu.VMEM((local, 128), wide),
+            pltpu.VMEM((local, 128), wide),
+            pltpu.VMEM((2, 3, local, width // 8), LOW),
+            pltpu.VMEM((2, local, 128), wide),
+            pltpu.VMEM((2 * local, hidden // 2), LOW),
+            pltpu.VMEM((2 * local, width), LOW),
+            *scatter_scratch(4, 128, 256),
+            dma((20,)),
+            dma((4, 4)),
+            dma((4, 4)),
+            dma((20,)),
+            dma((20,)),
+            *exchange_sems(2),
+            dma((4, 4)),
+            dma((4, 4)),
+        ],
+        compiler_params=pltpu.CompilerParams(
+            collective_id=2, has_side_effects=True, vmem_limit_bytes=VMEM_BYTES
+        ),
+        name="middle",
+    )(
+        u, tokens, cotangent, post_gain.reshape(1, width), second_gain.reshape(1, width),
+        mid_gain.reshape(1, hidden), w_out, w_up, w_down,
+    )
 
 
 def tail_kernel(
-    dq, dk, dv, tokens, gain, middle, triple, act_down, act_up, act_out, act_in, g_down, g_up, g_out, gains,
-    o_tokens, o_triple, o_out, o_up, o_down, o_gains,
-    d_left, d_right, d_whole, d_first, d_second, d_near, d_far,
+    dq, dk, dv, tokens, gain, middle, triple, act_up, act_out, act_in, g_up, g_out, gains, scales,
+    o_tokens, o_triple, o_out, o_up, o_gains,
     e_left, e_right, e_whole, e_first, e_second, e_near, e_far,
-    grad_s, gain_s, gain_r,
-    local_sem, core_send, core_recv, a2a_send, a2a_recv, s_send, s_recv, gain_send, gain_recv,
+    grad_s, gain_s, gain_r, relay,
+    local_sem, core_send, core_recv, x_send, x_recv, z_send, z_recv, s_send, s_recv, gain_send, gain_recv,
 ):
     place = Place()
     partner = place.core_partner()
-    peers = [(place.dp, (place.seq + k) % 8) for k in range(1, 8)]
+    column_peers = [(place.dp, (place.z + k) % 4 * 2 + place.x) for k in range(1, 4)]
     local, width = tokens.shape
     heads_width = dq.shape[1]
-    meet(peers + [partner, place.y_partner()])
-
-    moves = []
-    column = pl.ds(pl.multiple_of(place.seq * heads_width, 128), heads_width)
-    for t, source in enumerate((dv, dk, dq)):
-        slot = 5 + (2 - t)
-        for k in range(1, 8):
-            peer = (place.seq + k) % 8
-            rows = pl.ds(pl.multiple_of(peer * local, 128), local)
-            move = remote(
-                source.at[rows, :],
-                e_right.at[slot, pl.ds(0, local), column],
-                a2a_send.at[t, k - 1],
-                a2a_recv.at[t, k - 1],
-                (place.dp, peer),
-            )
-            move.start()
-            moves.append(move)
-        rows = pl.ds(pl.multiple_of(place.seq * local, 128), local)
-        move = pltpu.make_async_copy(
-            source.at[rows, :], e_right.at[slot, pl.ds(0, local), column], local_sem.at[t]
+    meet(column_peers + [place.x_partner(), partner, place.y_partner()])
+
+    def start_exchange(t):
+        return ToTokens(
+            place, (dv, dk, dq)[t], e_right.at[7 - t, pl.ds(0, local), :], relay.at[t],
+            [sem.at[t] for sem in (x_send, x_recv, z_send, z_recv)], local_sem.at[13 + t],
         )
-        move.start()
-        moves.append(move)
-
-    def share(index, sources, targets):
-        out = []
-        for k, (ours, theirs, target) in enumerate(zip(*sources, targets)):
-            here = pltpu.make_async_copy(ours, target.at[pl.ds(0, local), :], local_sem.at[3 + index + k])
-            there = remote(
-                theirs,
-                target.at[pl.ds(local, local), :],
-                core_send.at[index + k],
-                core_recv.at[index + k],
-                partner,
-            )
-            here.start()
-            there.start()
-            out += [here, there]
-        return out
-
-    def share_left(index, source, target):
-        columns = source.shape[1] // 4
-        ours = own_columns(source, place.core, columns)
-        theirs = own_columns(source, 1 - place.core, columns)
-        targets = [target.at[:, pl.ds(y * columns, columns)] for y in range(2)]
-        return share(index, (ours, theirs), targets)
-
-    ready = {}
-    ready["down"] = share_left(0, act_down, d_left) + share(2, ([g_down], [g_down]), [d_right])
-    ready["up"] = share_left(3, act_up, e_left.at[0])
+
+    exchanges = [start_exchange(0), start_exchange(1)]
+
+    sems = (local_sem, core_send, core_recv)
+    ready = {"up": share_left(place, 0, act_up, e_left.at[0], local, *sems)}
     for k in range(4):
         part = g_up.at[:, pl.ds(k * BLOCK, BLOCK)]
-        ready["up"] += share(5 + k, ([part], [part]), [e_right.at[k]])
-    ready["out"] = share_left(9, act_out, e_left.at[1]) + share(11, ([g_out], [g_out]), [e_right.at[4]])
-    ready["in"] = share_left(12, act_in, e_left.at[2])
-
-    def write_down(p, value):
-        o_down[:, pl.ds(p * 256, 256)] = value
+        ready["up"] += share(place, 2 + k, part, part, e_right.at[k], local, *sems)
+    ready["out"] = share_left(place, 6, act_out, e_left.at[1], local, *sems)
+    ready["out"] += share(place, 8, g_out, g_out, e_right.at[4], local, *sems)
+    ready["in"] = share_left(place, 9, act_in, e_left.at[2], local, *sems)
 
     def write_rest(p, value):
         if p < 4:
@@ -528,49 +1140,44 @@
         else:
             o_triple[:, pl.ds((p - 5) * BLOCK, BLOCK)] = value
 
-    down = Scatter(
-        place, (d_whole, d_first, d_second, d_near, d_far), (s_send, s_recv), 0,
-        lambda p: d_left, lambda p: d_right.at[:, pl.ds(p * 256, 256)], write_down,
-    )
     rest = Scatter(
-        place, (e_whole, e_first, e_second, e_near, e_far), (s_send, s_recv), 4,
+        place, (e_whole, e_first, e_second, e_near, e_far), (s_send, s_recv), 0,
         lambda p: e_left.at[0 if p < 4 else 1 if p == 4 else 2], lambda p: e_right.at[p], write_rest,
     )
-    order = [(down, k) for k in range(4)] + [(rest, k) for k in (0, 1, 2, 3, 4, 7, 6, 5)]
-
-    def wait_all(copies):
-        for copy in copies:
-            copy.wait()
-
-    lag = 2
+    order = [(rest, k) for k in (0, 1, 2, 3, 4, 7, 6, 5)]
     gain_s[...] = gains[...]
-
-    def step(t):
-        if t < len(order):
-            engine, p = order[t]
-            if t == 0:
-                wait_all(ready["down"])
-            if t == 4:
-                wait_all(ready["up"])
-            if t == 8:
-                wait_all(ready["out"])
-            engine.compute(p)
-        for stage in (1, 2, 3, 4):
-            at = t - stage * lag
-            if 0 <= at < len(order):
-                order[at][0].advance(order[at][1], stage)
-
-    for t in range(9):
-        step(t)
-
-    wait_all(moves)
+    gain_s[7:8, 0:128] = scales[...]
+    marks = {"compute": 0, 1: 0, 2: 0, 3: 0, 4: 0}
+
+    def advance(stage, upto):
+        while marks[stage] < min(upto, len(order)):
+            engine, p = order[marks[stage]]
+            engine.advance(p, stage) if stage != "compute" else engine.compute(p)
+            marks[stage] += 1
+
+    wait_all(ready["up"])
+    advance("compute", 2)
+    advance(1, 1)
+    exchanges[0].pass_on()
+    advance("compute", 3)
+    advance(1, 2)
+    advance(2, 1)
+    exchanges.append(start_exchange(2))
+    wait_all(ready["out"])
+    advance("compute", 4)
+    advance(1, 3)
+    exchanges[1].pass_on()
+    advance("compute", 5)
+    advance(1, 4)
+    advance(2, 2)
+    exchanges[2].pass_on()
+
+    for exchange in exchanges:
+        exchange.finish()
     back = [
         remote(
-            e_right.at[5 + t, pl.ds(0, local), :],
-            e_right.at[5 + t, pl.ds(local, local), :],
-            core_send.at[14 + t],
-            core_recv.at[14 + t],
-            partner,
+            e_right.at[5 + t, pl.ds(0, local), :], e_right.at[5 + t, pl.ds(local, local), :],
+            core_send.at[11 + t], core_recv.at[11 + t], partner,
         )
         for t in range(3)
     ]
@@ -587,25 +1194,18 @@
 
     wait_all(ready["in"])
     wait_all(back)
-    step(9)
-    step(10)
-    step(11)
+    advance("compute", 8)
+    advance(1, 5)
+    advance(2, 4)
     lax.fori_loop(0, width // 256, columns_of, 0)
-    step(12)
+    advance(3, 2)
+    advance(1, 6)
 
     def norm_rows(n, total):
         rows = pl.ds(pl.multiple_of(n * 128, 128), 128)
-        values = tokens[rows, :].astype(jnp.float32)
-        center = values - jnp.mean(values, axis=-1, keepdims=True)
-        inverse = lax.rsqrt(jnp.mean(center * center, axis=-1, keepdims=True) + 1e-05)
-        unit = center * inverse
+        unit, inverse = norm_parts(tokens[rows, :].astype(jnp.float32))
         grad = grad_s[rows, :]
-        scaled = grad * gain[...]
-        pulled = inverse * (
-            scaled
-            - jnp.mean(scaled, axis=-1, keepdims=True)
-            - unit * jnp.mean(scaled * unit, axis=-1, keepdims=True)
-        )
+        pulled = norm_pull(grad, unit, inverse, gain[...])
         o_tokens[rows, :] = (middle[rows, :] + pulled).astype(LOW)
         return total + jnp.sum(grad * unit, axis=0, keepdims=True)
 
@@ -613,20 +1213,23 @@
 
     meets = (partner, place.y_partner(), place.x_partner(), place.near_partner(), place.far_partner())
 
-    def gain_step(k):
+    for k in range(5):
         move = remote(gain_s, gain_r.at[k], gain_send.at[k], gain_recv.at[k], meets[k])
-        return move
-
-    for k in range(5):
-        move = gain_step(k)
         move.start()
-        step(13 + k)
+        advance(1, 7 + k // 2)
+        advance(2, 5 + k // 2)
+        advance(3, 3 + k // 2)
+        advance(4, 1 + k // 2)
         move.wait()
         gain_s[...] = gain_s[...] + gain_r[k]
         if k == 1:
             o_gains[7:8, :] = gain_s[7:8, 0:128]
-    for t in range(18, len(order) + 4 * lag + 1):
-        step(t)
+    for n in range(8):
+        advance(2, n + 1)
+        advance(3, n)
+        advance(4, n - 1)
+    advance(3, 8)
+    advance(4, 8)
     device = place.dp * 8 + place.seq
     pick = (
         lax.broadcasted_iota(jnp.int32, (width, 128), 0)
@@ -643,10 +1246,10 @@
         engine.settle(p)
 
 
-def tail(dqkv, tokens, gain, middle, triple, acts, grads, gains):
+def tail(dqkv, tokens, gain, middle, triple, acts, grads, gains, scales):
     local, width = tokens.shape
     heads_width = dqkv[0].shape[1]
-    hidden = acts[0].shape[1]
+    hidden = grads[0].shape[1]
     any_spec = pl.BlockSpec(memory_space=pl.ANY)
     vmem = pl.BlockSpec(memory_space=pltpu.VMEM)
     wide = jnp.float32
@@ -658,26 +1261,23 @@
             jax.ShapeDtypeStruct((width // 32, 3 * width), wide),
             jax.ShapeDtypeStruct((width // 32, width), wide),
             jax.ShapeDtypeStruct((width // 32, hidden), wide),
-            jax.ShapeDtypeStruct((hidden // 32, width), wide),
             jax.ShapeDtypeStruct((8, 128), wide),
         ),
-        in_specs=[any_spec] * 3 + [vmem] * 4 + [any_spec] * 7 + [vmem],
-        out_specs=(vmem,) * 6,
-        scratch_shapes=[pltpu.VMEM((2 * local, hidden // 2), LOW), pltpu.VMEM((2 * local, width), LOW)]
-        + scatter_scratch(4, 128, 256)
-        + [pltpu.VMEM((3, 2 * local, width // 2), LOW), pltpu.VMEM((8, 2 * local, width), LOW)]
+        in_specs=[any_spec] * 3 + [vmem] * 4 + [any_spec] * 5 + [vmem] * 2,
+        out_specs=(vmem,) * 5,
+        scratch_shapes=[pltpu.VMEM((3, 2 * local, width // 2), LOW), pltpu.VMEM((8, 2 * local, width), LOW)]
         + scatter_scratch(8, 32, 1024)
         + [
             pltpu.VMEM((local, width), wide),
             pltpu.VMEM((8, width), wide),
             pltpu.VMEM((5, 8, width), wide),
+            pltpu.VMEM((3, 3, local, heads_width), LOW),
             dma((20,)),
             dma((20,)),
             dma((20,)),
-            dma((3, 7)),
-            dma((3, 7)),
-            dma((4, 12)),
-            dma((4, 12)),
+            *exchange_sems(3),
+            dma((4, 8)),
+            dma((4, 8)),
             dma((5,)),
             dma((5,)),
         ],
@@ -685,7 +1285,7 @@
             collective_id=3, has_side_effects=True, vmem_limit_bytes=VMEM_BYTES
         ),
         name="tail",
-    )(*dqkv, tokens, gain.reshape(1, width), middle, triple, *acts, *grads, gains)
+    )(*dqkv, tokens, gain.reshape(1, width), middle, triple, *acts, *grads, gains, scales)
 
 
 def per_device(
@@ -727,9 +1327,9 @@
         head_scale, lax.axis_index("seq") * heads_here, heads_here, 0
     )
     scale_wide = jnp.repeat(own_scale, HEAD)[None]
-    bounds, starts = document_bounds(doc_ids)
+    starts = document_starts(doc_ids)
     attended, scaled, logsum = attend_forward(
-        queries, keys_all, values_all, bounds, starts, scale_wide
+        queries, keys_all, values_all, starts, scale_wide
     )
     merged = lax.all_to_all(scaled, "seq", split_axis=0, concat_axis=1, tiled=True)
     projected = jnp.dot(merged, output_full, preferred_element_type=jnp.float32)
@@ -761,7 +1361,7 @@
         grad_merged, "seq", split_axis=1, concat_axis=0, tiled=True
     )
     grad_queries, grad_keys, grad_values, scale_lanes = attend_backward(
-        queries, keys_all, values_all, attended, grad_scaled, bounds, starts, scale_wide, logsum
+        queries, keys_all, values_all, attended, grad_scaled, starts, scale_wide, logsum
     )
     scale_terms = jnp.sum(scale_lanes.reshape(heads_here, HEAD), axis=1)
     back_queries, back_keys, back_values = (
@@ -831,86 +1431,35 @@
     down_weight,
     cotangent,
 ):
-    inputs = tokens[0].astype(jnp.float32)
-    width = inputs.shape[1]
-    doc_ids = lax.all_gather(segment_ids[0], "seq", axis=0, tiled=True)
-    triple_full, output_full = (
-        lax.all_gather(triple_weight, "dp", axis=0, tiled=True),
-        lax.all_gather(output_weight, "dp", axis=0, tiled=True),
-    )
-    normed = layer_norm(inputs, first_gain)
-    normed_low = normed.astype(jnp.bfloat16)
-    triple = jnp.dot(normed_low, triple_full, preferred_element_type=jnp.float32).astype(
-        jnp.bfloat16
-    )
-    queries, keys_all, values_all = (
-        lax.all_to_all(triple[:, :width], "seq", split_axis=1, concat_axis=0, tiled=True),
-        lax.all_to_all(
-            triple[:, width : 2 * width], "seq", split_axis=1, concat_axis=0, tiled=True
-        ),
-        lax.all_to_all(triple[:, 2 * width :], "seq", split_axis=1, concat_axis=0, tiled=True),
-    )
-    heads_here = queries.shape[1] // HEAD
+    width, hidden = tokens.shape[2], up_weight.shape[1]
+    heads_here = width // HEAD // sizes[1]
     own_scale = lax.dynamic_slice_in_dim(
         head_scale, lax.axis_index("seq") * heads_here, heads_here, 0
     )
     scale_wide = jnp.repeat(own_scale, HEAD)[None]
-    bounds, starts = document_bounds(doc_ids)
-    attended, scaled, logsum = attend_forward(
-        queries, keys_all, values_all, bounds, starts, scale_wide
-    )
-    merged = lax.all_to_all(scaled, "seq", split_axis=0, concat_axis=1, tiled=True)
-    projected = jnp.dot(merged, output_full, preferred_element_type=jnp.float32)
-    post_normed, pull_post = jax.vjp(layer_norm, projected, post_gain)
-    middle = inputs + post_normed
-    second, pull_second = jax.vjp(layer_norm, middle, second_gain)
-    second_low = second.astype(jnp.bfloat16)
-    feed_up, feed_down = (
-        lax.all_gather(up_weight, "dp", axis=0, tiled=True),
-        lax.all_gather(down_weight, "dp", axis=0, tiled=True),
-    )
-    hidden = jnp.dot(second_low, feed_up, preferred_element_type=jnp.float32)
-    activated, pull_mid = jax.vjp(gelu_norm, hidden, mid_gain)
-    activated_low = activated.astype(jnp.bfloat16)
-    layer_out = (
-        middle + jnp.dot(activated_low, feed_down, preferred_element_type=jnp.float32)
-    ).astype(jnp.bfloat16)
-    upstream = cotangent[0]
-    grad_act = times_transposed(upstream, feed_down)
-    grad_hidden, grad_mid = pull_mid(grad_act)
-    grad_hidden_low = grad_hidden.astype(jnp.bfloat16)
-    grad_second_in = times_transposed(grad_hidden_low, feed_up)
-    grad_middle_part, grad_second = pull_second(grad_second_in)
-    grad_middle = upstream.astype(jnp.float32) + grad_middle_part
-    grad_projected, grad_post = pull_post(grad_middle)
-    grad_projected_low = grad_projected.astype(jnp.bfloat16)
-    grad_merged = times_transposed(grad_projected_low, output_full).astype(jnp.bfloat16)
-    grad_scaled = lax.all_to_all(
-        grad_merged, "seq", split_axis=1, concat_axis=0, tiled=True
+    values, keys, queries, normed, starts, triple_full, output_full, up_full = front(
+        tokens[0], first_gain, segment_ids, triple_weight, output_weight, up_weight
+    )
+    attended, scaled, logsum = attend_forward(queries, keys, values, starts, scale_wide)
+    layer_out, grad_middle, grad_scaled, merged, second, grad_hidden, grad_projected, gains, grad_down = middle(
+        scaled, tokens[0], cotangent[0], post_gain, second_gain, mid_gain, output_full, up_full, down_weight
     )
     grad_queries, grad_keys, grad_values, scale_lanes = attend_backward(
-        queries, keys_all, values_all, attended, grad_scaled, bounds, starts, scale_wide, logsum
-    )
-    grad_first_low = jnp.zeros((1, width), jnp.float32)
+        queries, keys, values, attended, grad_scaled, starts, scale_wide, logsum
+    )
     gains = jnp.concatenate(
-        (
-            grad_first_low,
-            grad_post[None],
-            grad_second[None],
-            grad_mid.reshape(-1, width),
-            jnp.pad(scale_lanes, ((0, 0), (0, width - scale_lanes.shape[1]))),
-        ),
-        axis=0,
-    )
-    grad_tokens, grad_triple, grad_output, grad_up, grad_down, sums = tail(
+        (gains[:3, :width], gains[3].reshape(-1, width), jnp.zeros((1, width), jnp.float32)), axis=0
+    )
+    grad_tokens, grad_triple, grad_output, grad_up, sums = tail(
         (grad_queries, grad_keys, grad_values),
         tokens[0],
         first_gain,
         grad_middle,
         triple_full,
-        (activated_low, second_low, merged, normed_low),
-        (upstream, grad_hidden_low, grad_projected_low),
+        (second, merged, normed),
+        (grad_hidden, grad_projected),
         gains,
+        scale_lanes,
     )
     own = width // 32
     return (

time: 477 us -> 406 us (0.85)
  Pallas kernels: 204 us -> 392 us
  waiting for transfers between devices: 111 us -> 0 us
  matrix products: 41.8 us -> 0 us
  blocking collectives: 38.6 us -> 0 us
  other arithmetic: 22.9 us -> 1.32 us
  starting transfers between devices: 20.8 us -> 0 us
  between operations: 14.2 us -> 0.74 us
  local copies, waits for them, and re-layouts: 23.1 us -> 10 us
    pallas_call x0 -> x2, Pallas kernels: none -> 204 us  [the longest x1 120 us: middle(): pl.pallas_call(middle_kernel, out_shape=(act, jax.ShapeDtypeStruct((local...]
    all_to_all x5 -> x0, waiting for transfers between devices: 60.2 us -> none  [the longest x1 19.5 us: per_device_chips(): lax.all_to_all(triple[:, :width], 'seq', split_axis=1, concat_axis=0, til...]
    all_gather x4 -> x0, waiting for transfers between devices: 47.9 us -> none  [the longest x1 47.8 us: per_device_chips(): lax.all_gather(triple_weight, 'dp', axis=0, tiled=True)]
    dot_general x7 -> x0, matrix products: 41.8 us -> none  [the longest x3 17.5 us: times_transposed(): lax.dot_general(left, right, (((1,), (1,)), ((), ())), preferred_element_...]
    all_gather x1 -> x0, blocking collectives: 38.6 us -> none  [per_device_chips(): doc_ids = lax.all_gather(segment_ids[0], 'seq', axis=0, tiled=True)]
    all_to_all x5 -> x0, starting transfers between devices: 20.6 us -> none  [the longest x1 5.51 us: per_device_chips(): lax.all_to_all(triple[:, :width], 'seq', split_axis=1, concat_axis=0, til...]
    reduce_sum x14 -> x0, other arithmetic: 15.3 us -> none  [the longest x5 8.75 us: layer_norm(): center = values - jnp.mean(values, axis=-1, keepdims=True)]
    pallas_call x1, Pallas kernels: 152 us -> 139 us  [tail(): pl.pallas_call(tail_kernel, out_shape=(jax.ShapeDtypeStruct((local, width...]
  transfers between devices with their start and end apart: 9 -> 0, of which waited for: 5 -> 0; matrix products, arithmetic and copies ran while one was open for 8% -> 0% of each run, Pallas kernels for 5% -> 0%
where the time goes in v3:
time: 406 us; the launch traced here: 404 us
  Pallas kernels  392 us (97%)
  local copies, waits for them, and re-layouts  10 us (2%)
    pallas_call x1, Pallas kernels, tail(): pl.pallas_call(tail_kernel, out_shape=(jax.ShapeDtypeStruct((local, width...  139 us
    pallas_call x1, Pallas kernels, middle(): pl.pallas_call(middle_kernel, out_shape=(act, jax.ShapeDtypeStruct((local...  120 us
    pallas_call x1, Pallas kernels, front(): pl.pallas_call(front_kernel, out_shape=(one, one, one, jax.ShapeDtypeStru...  84.1 us
    pallas_call x1, Pallas kernels, attend_backward(): pl.pallas_call(functools.partial(backward_kernel, heads), out_shape=(jax....  26.1 us
    pallas_call x1, Pallas kernels, attend_forward(): pl.pallas_call(functools.partial(forward_kernel, heads), out_shape=(jax.S...  22.3 us

profile of v3, /device:TPU:0, one launch (start us, length us, event | category | flops | bytes accessed | tf_op | source)
XLA Modules:
  0.0 403.9 jit_solution(4891105754719093576)
XLA Ops:
  0.6 0.0 copy-start.6
  0.7 84.1 %front.1 = (bf16[3072,128]{1,0:T(8,128)(2,1)}, bf16[3072,128]{1,0:T(8,128)(2,1)}, bf16[3072,128]{1,0:T(8,128)(2,1)}, bf16[384,1024]{1,0:T(8,128)(2,1)}, s32[12,1...) custom-call(bf16[384,1024]{1,0:T(8,128)(2,1)} %bitcast.17, ...), custom_call_target="tpu_custom_call" | custom-call | tf_op jit(solution)/shard_map/front/pallas_call | solution.py:775
  84.8 0.0 copy-done.6
  84.8 0.1 dynamic_slice.3
  84.9 0.1 broadcast_in_dim.12
  84.9 0.6 broadcast_in_dim_reshape.3.scale_ref
  85.5 22.3 %attend_forward.1 = (f32[3072,128]{1,0:T(8,128)}, bf16[3072,128]{1,0:T(8,128)(2,1)}, f32[12,1,512]{2,1,0:T(1,128)}) custom-call(s32[12,1,256]{2,1,0:T(1,128)} %get-tuple-element.40.first_ref.start_ref, bf16[3072,128]{1,0:T(8,128)(2,1)} %get-tuple-element.41.q_ref, bf16[3072,128]{1,0:T(8,128)(2,1)} %get-tuple-element.42.k_ref, ...), custom_call_target="tpu_custom_call" | custom-call | flops 1207959552 | bytes 6291456 | tf_op jit(solution)/shard_map/attend_forward/pallas_call | solution.py:98
  107.8 119.9 %middle.1 = (bf16[384,1024]{1,0:T(8,128)(2,1)}, f32[384,1024]{1,0:T(8,128)}, bf16[3072,128]{1,0:T(8,128)(2,1)}, bf16[384,1024]{1,0:T(8,128)(2,1)}, bf16[384,1024...) custom-call(bf16[3072,128]{1,0:T(8,128)(2,1)} %get-tuple-element.44., ...), custom_call_target="tpu_custom_call" | custom-call | tf_op jit(solution)/shard_map/middle/pallas_call | solution.py:1050
  227.7 1.0 slice_reduce_fusion
  228.7 0.8 slice.21
  229.4 0.1 pad.2.clone
  229.5 0.7 maximum_maximum_fusion.gains
  230.2 26.1 %attend_backward.1 = (bf16[3072,128]{1,0:T(8,128)(2,1)}, bf16[3072,128]{1,0:T(8,128)(2,1)}, bf16[3072,128]{1,0:T(8,128)(2,1)}, f32[1,128]{1,0:T(1,128)}) custom-call(s32[12,1,256]{2,1,0:T(1,128)} %get-tuple-element.40.first_ref.start_ref, bf16[3072,128]{1,0:T(8,128)(2,1)} %get-tuple-element.41.q_ref, bf16[3072,128]{1,0:T(8,128)(2,1)} %get-tuple-element.42.k_ref, ...), custom_call_target="tpu_custom_call" | custom-call | flops 3623878656 | bytes 12582912 | tf_op jit(solution)/shard_map/attend_backward/pallas_call | solution.py:213
  256.3 0.0 copy-start
  256.3 139.5 %tail.1 = (bf16[384,1024]{1,0:T(8,128)(2,1)}, f32[32,3072]{1,0:T(8,128)}, f32[32,1024]{1,0:T(8,128)}, f32[32,4096]{1,0:T(8,128)}, f32[8,128]{1,0:T(8,128)}) custom-call(bf16[3072,128]{1,0:T(8,128)(2,1)} %get-tuple-element.51.dq, bf16[3072,128]{1,0:T(8,128)(2,1)} %get-tuple-element.52.dk, bf16[3072,128]{1,0:T(8,128)(2,1)} %get-tuple-element.53.dv, ...), custom_call_target="tpu_custom_call" | custom-call | tf_op jit(solution)/shard_map/tail/pallas_call | solution.py:1257
  395.8 0.0 copy-start.1
  395.8 0.0 copy-start.4
  395.8 0.0 copy-start.5
  395.8 1.3 slice_bitcast_fusion
  397.1 0.1 reshape_squeeze.7
  397.2 0.6 reduce_sum.9
  397.8 1.3 slice_bitcast_fusion.1
  399.1 0.0 copy-done
  399.1 0.0 copy-start.3
  399.1 0.9 copy.29
  400.0 0.0 copy-done.1
  400.0 0.0 copy-start.2
  400.0 0.9 copy.30
  400.9 0.0 copy-done.4
  400.9 0.7 copy.31
  401.6 0.0 copy-done.5
  401.7 0.7 copy.32
  402.3 0.0 copy-done.3
  402.3 0.8 copy.33
  403.1 0.0 copy-done.2
  403.1 0.8 copy.34
  (1 shorter events, 0.0 us)
Async XLA Ops:
  0.6 84.1 %copy-start.6 = (f32[16]{0:T(128)S(1)}, f32[16]{0:T(128)}, u32[]{:S(2)}) copy-start(f32[16]{0:T(128)} %param.16) | copy-start | bytes 196
  256.3 142.8 %copy-start = (bf16[384,1024]{1,0:T(8,128)(2,1)S(1)}, bf16[384,1024]{1,0:T(8,128)(2,1)}, u32[]{:S(2)}) copy-start(bf16[384,1024]{1,0:T(8,128)(2,1)} %get-tuple-element.47) | copy-start | bytes 2359300
  395.8 4.2 %copy-start.1 = (bf16[384,1024]{1,0:T(8,128)(2,1)S(1)}, bf16[384,1024]{1,0:T(8,128)(2,1)}, u32[]{:S(2)}) copy-start(bf16[384,1024]{1,0:T(8,128)(2,1)} %get-tuple-element.63) | copy-start | bytes 2359300
  395.8 5.1 %copy-start.4 = (f32[32,3072]{1,0:T(8,128)S(1)}, f32[32,3072]{1,0:T(8,128)}, u32[]{:S(2)}) copy-start(f32[32,3072]{1,0:T(8,128)} %get-tuple-element.88) | copy-start | bytes 1179652
  395.8 5.8 %copy-start.5 = (f32[32,1024]{1,0:T(8,128)S(1)}, f32[32,1024]{1,0:T(8,128)}, u32[]{:S(2)}) copy-start(f32[32,1024]{1,0:T(8,128)} %get-tuple-element.90) | copy-start | bytes 393220
  399.1 3.2 copy-start.3
  400.0 3.1 copy-start.2

commit v4 on v3

--- a/solution.py
+++ b/solution.py
@@ -9,6 +9,9 @@
 HEAD = 64
 NEG = -1e30
 BQ = 256
+QB = 512
+KB = 512
+WIDE = 1
 
 
 def nt(a, b):
@@ -39,62 +42,80 @@
 
 def forward_kernel(heads, first_ref, q_ref, k_ref, v_ref, start_ref, scale_ref,
                    o_ref, u_ref, lse_ref, m_s, l_s, acc_s):
-    i = pl.program_id(0)
-    rows = q_ref.shape[0]
-    wide = heads * rows
-    queries = stack_heads(q_ref[...] * jnp.bfloat16(HEAD ** -0.5), heads)
-    starts = jnp.concatenate([start_ref[0]] * heads, axis=1)
-    m_s[...] = jnp.full_like(m_s, NEG)
-    l_s[...] = jnp.zeros_like(l_s)
-    acc_s[...] = jnp.zeros_like(acc_s)
-
-    def step(j, masked, diagonal):
-        at = pl.ds(pl.multiple_of(j * rows, rows), rows)
-        scores = nt(k_ref[at, :], queries)
-        if masked or diagonal:
-            key = j * rows + lax.broadcasted_iota(jnp.int32, scores.shape, 0)
-            allowed = key >= starts
+    rows, step_rows = QB, KB
+    ratio = rows // step_rows
+
+    def one(i, carry):
+        mine = pl.ds(pl.multiple_of(i * rows, rows), rows)
+        queries = stack_heads(q_ref[mine, :] * jnp.bfloat16(HEAD ** -0.5), heads)
+        starts = jnp.concatenate([start_ref[i * (rows // BQ) + k] for k in range(rows // BQ)] * heads, axis=1)
+
+        def step(j, count, masked, diagonal):
+            at = pl.ds(pl.multiple_of(j * step_rows, step_rows), count * step_rows)
+            scores = nt(k_ref[at, :], queries)
+            if masked or diagonal:
+                key = j * step_rows + lax.broadcasted_iota(jnp.int32, scores.shape, 0)
+                allowed = key >= starts
+                if diagonal:
+                    lane = lax.broadcasted_iota(jnp.int32, scores.shape, 1) & (rows - 1)
+                    allowed = allowed & (key <= i * rows + lane)
+                scores = jnp.where(allowed, scores, NEG)
+            highest = jnp.max(scores, axis=0, keepdims=True)
+            if not diagonal:
+                before = m_s[...]
+                highest = jnp.maximum(before, highest)
+                fade = jnp.exp(before - highest)
+            weights = jnp.exp(scores - highest)
+            total = jnp.sum(weights, axis=0, keepdims=True)
+            part = tn(v_ref[at, :], weights.astype(jnp.bfloat16))
+            m_s[...] = highest
             if diagonal:
-                lane = lax.broadcasted_iota(jnp.int32, scores.shape, 1) & (rows - 1)
-                allowed = allowed & (key <= i * rows + lane)
-            scores = jnp.where(allowed, scores, NEG)
-        before = m_s[...]
-        highest = jnp.maximum(before, jnp.max(scores, axis=0, keepdims=True))
-        weights = jnp.exp(scores - highest)
-        fade = jnp.exp(before - highest)
-        if masked:
-            weights = jnp.where(scores > 0.5 * NEG, weights, 0.0)
-        m_s[...] = highest
-        l_s[...] = l_s[...] * fade + jnp.sum(weights, axis=0, keepdims=True)
-        acc_s[...] = acc_s[...] * fade + tn(v_ref[at, :], weights.astype(jnp.bfloat16))
-
-    step(i, False, True)
-    low = first_ref[i, 0, 0] // rows
-    full = jnp.minimum((first_ref[i, 0, rows - 1] + rows - 1) // rows, i)
-
-    def plain(j, carry):
-        step(j, False, False)
+                l_s[...] = total
+                acc_s[...] = part
+            else:
+                l_s[...] = l_s[...] * fade + total
+                acc_s[...] = acc_s[...] * fade + part
+
+        step(i * ratio, ratio, False, True)
+        low = first_ref[i * (rows // BQ), 0, 0] // step_rows
+        last = first_ref[i * (rows // BQ) + rows // BQ - 1, 0, BQ - 1]
+        full = jnp.minimum((last + step_rows - 1) // step_rows, i * ratio)
+        pairs = (i * ratio - full) // WIDE
+
+        def wide(n, carry):
+            step(i * ratio - WIDE * (n + 1), WIDE, False, False)
+            return carry
+
+        def plain(j, carry):
+            step(j, 1, False, False)
+            return carry
+
+        def edge(j, carry):
+            step(j, 1, True, False)
+            return carry
+
+        lax.fori_loop(0, pairs, wide, 0)
+        lax.fori_loop(full, i * ratio - WIDE * pairs, plain, 0)
+        lax.fori_loop(low, full, edge, 0)
+        total = l_s[...]
+        out = unstack_heads(acc_s[...] * (1.0 / total), heads).T
+        o_ref[mine, :] = out
+        u_ref[mine, :] = (out * scale_ref[...]).astype(jnp.bfloat16)
+        logsum = m_s[...] + jnp.log(total)
+        for k in range(rows // BQ):
+            lse_ref[i * (rows // BQ) + k] = jnp.concatenate(
+                [logsum[:, h * rows + k * BQ : h * rows + (k + 1) * BQ] for h in range(heads)], axis=1
+            )
         return carry
 
-    def edge(j, carry):
-        step(j, True, False)
-        return carry
-
-    lax.fori_loop(full, i, plain, 0)
-    lax.fori_loop(low, full, edge, 0)
-    total = l_s[...]
-    out = unstack_heads(acc_s[...] / total, heads).T
-    o_ref[...] = out
-    u_ref[...] = (out * scale_ref[...]).astype(jnp.bfloat16)
-    lse_ref[0] = m_s[...] + jnp.log(total)
+    lax.fori_loop(0, q_ref.shape[0] // rows, one, 0)
 
 
 def attend_forward(queries, keys, values, starts, scale_wide):
     length, width = queries.shape
     heads = width // HEAD
     blocks = length // BQ
-    whole = pl.BlockSpec((length, width), lambda i, *_: (0, 0))
-    mine = pl.BlockSpec((BQ, width), lambda i, *_: (i, 0))
+    vmem = pl.BlockSpec(memory_space=pltpu.VMEM)
     return pl.pallas_call(
         functools.partial(forward_kernel, heads),
         out_shape=(
@@ -102,23 +123,13 @@
             jax.ShapeDtypeStruct((length, width), jnp.bfloat16),
             jax.ShapeDtypeStruct((blocks, 1, heads * BQ), jnp.float32),
         ),
-        grid_spec=pltpu.PrefetchScalarGridSpec(
-            num_scalar_prefetch=1,
-            grid=(blocks,),
-            in_specs=[
-                mine,
-                whole,
-                whole,
-                pl.BlockSpec((1, 1, BQ), lambda i, *_: (i, 0, 0)),
-                pl.BlockSpec((1, width), lambda i, *_: (0, 0)),
-            ],
-            out_specs=(mine, mine, pl.BlockSpec((1, 1, heads * BQ), lambda i, *_: (i, 0, 0))),
-            scratch_shapes=[
-                pltpu.VMEM((1, heads * BQ), jnp.float32),
-                pltpu.VMEM((1, heads * BQ), jnp.float32),
-                pltpu.VMEM((width, heads * BQ), jnp.float32),
-            ],
-        ),
+        in_specs=[pl.BlockSpec(memory_space=pltpu.SMEM)] + [vmem] * 5,
+        out_specs=(vmem,) * 3,
+        scratch_shapes=[
+            pltpu.VMEM((1, heads * QB), jnp.float32),
+            pltpu.VMEM((1, heads * QB), jnp.float32),
+            pltpu.VMEM((width, heads * QB), jnp.float32),
+        ],
         cost_estimate=pl.CostEstimate(
             flops=length * length * width, bytes_accessed=16 * length * width, transcendentals=0
         ),
@@ -128,115 +139,104 @@
 
 def backward_kernel(heads, first_ref, q_ref, k_ref, v_ref, o_ref, du_ref, start_ref, scale_ref, lse_ref,
                     dq_ref, dk_ref, dv_ref, ds_ref, qs_s, dos_s, delta_s, dqt_s, dk_s, dv_s):
-    j = pl.program_id(0)
-    rows = k_ref.shape[0]
+    rows = BQ
     blocks = qs_s.shape[0]
-    wide = heads * rows
-
-    @pl.when(j == 0)
-    def prepare():
-        def one(i, total):
-            at = pl.ds(pl.multiple_of(i * rows, rows), rows)
-            qs_s[i] = stack_heads(q_ref[at, :] * jnp.bfloat16(HEAD ** -0.5), heads)
-            grad = du_ref[at, :].astype(jnp.float32)
-            out = o_ref[at, :]
-            low = (grad * scale_ref[...]).astype(jnp.bfloat16)
-            dos_s[i] = stack_heads(low, heads)
-            inner = (low.astype(jnp.float32) * out).T
-            delta_s[i] = jnp.concatenate(
-                [jnp.sum(inner[h * HEAD : (h + 1) * HEAD], axis=0, keepdims=True) for h in range(heads)],
-                axis=1,
-            )
-            return total + jnp.sum(grad * out, axis=0, keepdims=True)
-
-        ds_ref[...] = lax.fori_loop(0, blocks, one, jnp.zeros(ds_ref.shape, jnp.float32))
-        dqt_s[...] = jnp.zeros_like(dqt_s)
-
-    keys, values = k_ref[...], v_ref[...]
-    dk_s[...] = jnp.zeros_like(dk_s)
-    dv_s[...] = jnp.zeros_like(dv_s)
-
-    def step(i, masked, diagonal):
-        queries, grads = qs_s[i], dos_s[i]
-        scores = nt(keys, queries)
-        if masked or diagonal:
-            key = j * rows + lax.broadcasted_iota(jnp.int32, scores.shape, 0)
-            starts = jnp.concatenate([start_ref[i]] * heads, axis=1)
-            allowed = key >= starts
+
+    def prepare(i, total):
+        at = pl.ds(pl.multiple_of(i * rows, rows), rows)
+        qs_s[i] = stack_heads(q_ref[at, :] * jnp.bfloat16(HEAD ** -0.5), heads)
+        grad = du_ref[at, :].astype(jnp.float32)
+        out = o_ref[at, :]
+        low = (grad * scale_ref[...]).astype(jnp.bfloat16)
+        dos_s[i] = stack_heads(low, heads)
+        inner = (low.astype(jnp.float32) * out).T
+        delta_s[i] = jnp.concatenate(
+            [jnp.sum(inner[h * HEAD : (h + 1) * HEAD], axis=0, keepdims=True) for h in range(heads)],
+            axis=1,
+        )
+        return total + jnp.sum(grad * out, axis=0, keepdims=True)
+
+    ds_ref[...] = lax.fori_loop(0, blocks, prepare, jnp.zeros(ds_ref.shape, jnp.float32))
+
+    def one(j, carry):
+        mine = pl.ds(pl.multiple_of(j * rows, rows), rows)
+        keys, values = k_ref[mine, :], v_ref[mine, :]
+
+        def step(i, masked, diagonal):
+            queries, grads = qs_s[i], dos_s[i]
+            scores = nt(keys, queries)
+            if masked or diagonal:
+                key = j * rows + lax.broadcasted_iota(jnp.int32, scores.shape, 0)
+                starts = jnp.concatenate([start_ref[i]] * heads, axis=1)
+                allowed = key >= starts
+                if diagonal:
+                    lane = lax.broadcasted_iota(jnp.int32, scores.shape, 1) & (rows - 1)
+                    allowed = allowed & (key <= i * rows + lane)
+                scores = jnp.where(allowed, scores, NEG)
+            weights = jnp.exp(scores - lse_ref[i])
+            pulls = nt(values, grads)
+            low = (weights * (pulls - delta_s[i])).astype(jnp.bfloat16)
+            part_v = jnp.dot(weights.astype(jnp.bfloat16), grads, preferred_element_type=jnp.float32)
+            part_k = jnp.dot(low, queries, preferred_element_type=jnp.float32)
+            part_q = tn(keys, low)
             if diagonal:
-                lane = lax.broadcasted_iota(jnp.int32, scores.shape, 1) & (rows - 1)
-                allowed = allowed & (key <= i * rows + lane)
-            scores = jnp.where(allowed, scores, NEG)
-        weights = jnp.exp(scores - lse_ref[i])
-        pulls = nt(values, grads)
-        low = (weights * (pulls - delta_s[i])).astype(jnp.bfloat16)
-        dv_s[...] += jnp.dot(weights.astype(jnp.bfloat16), grads, preferred_element_type=jnp.float32)
-        dk_s[...] += jnp.dot(low, queries, preferred_element_type=jnp.float32)
-        dqt_s[i] += tn(keys, low)
-
-    step(j, False, True)
-    high, full = jnp.int32(0), jnp.int32(0)
-    for i in range(blocks):
-        high += (first_ref[i, 0, 0] // rows <= j).astype(jnp.int32)
-        full += ((first_ref[i, 0, rows - 1] + rows - 1) // rows <= j).astype(jnp.int32)
-    full = jnp.maximum(full, j + 1)
-
-    def plain(i, carry):
-        step(i, False, False)
+                dv_s[...] = part_v
+                dk_s[...] = part_k
+            else:
+                dv_s[...] += part_v
+                dk_s[...] += part_k
+            return part_q
+
+        high, full = jnp.int32(0), jnp.int32(0)
+        for i in range(blocks):
+            high += (first_ref[i, 0, 0] // rows <= j).astype(jnp.int32)
+            full += ((first_ref[i, 0, rows - 1] + rows - 1) // rows <= j).astype(jnp.int32)
+        full = jnp.maximum(full, j + 1)
+
+        def plain(i, carry):
+            dqt_s[i] += step(i, False, False)
+            return carry
+
+        def edge(i, carry):
+            dqt_s[i] += step(i, True, False)
+            return carry
+
+        dqt_s[j] = step(j, False, True)
+        lax.fori_loop(j + 1, full, plain, 0)
+        lax.fori_loop(full, high, edge, 0)
+        dk_ref[mine, :] = dk_s[...].astype(jnp.bfloat16)
+        dv_ref[mine, :] = dv_s[...].astype(jnp.bfloat16)
         return carry
 
-    def edge(i, carry):
-        step(i, True, False)
+    lax.fori_loop(0, blocks, lambda n, carry: one(blocks - 1 - n, carry), 0)
+
+    def finish(i, carry):
+        at = pl.ds(pl.multiple_of(i * rows, rows), rows)
+        dq_ref[at, :] = (unstack_heads(dqt_s[i], heads).T * HEAD ** -0.5).astype(jnp.bfloat16)
         return carry
 
-    lax.fori_loop(j + 1, full, plain, 0)
-    lax.fori_loop(full, high, edge, 0)
-    dk_ref[...] = dk_s[...].astype(jnp.bfloat16)
-    dv_ref[...] = dv_s[...].astype(jnp.bfloat16)
-
-    @pl.when(j == blocks - 1)
-    def finish():
-        def one(i, carry):
-            at = pl.ds(pl.multiple_of(i * rows, rows), rows)
-            dq_ref[at, :] = (unstack_heads(dqt_s[i], heads).T * HEAD ** -0.5).astype(jnp.bfloat16)
-            return carry
-
-        lax.fori_loop(0, blocks, one, 0)
+    lax.fori_loop(0, blocks, finish, 0)
 
 
 def attend_backward(queries, keys, values, outs, grads, starts, scale_wide, logsum):
     length, width = queries.shape
     heads = width // HEAD
     blocks = length // BQ
-    whole = pl.BlockSpec((length, width), lambda i, *_: (0, 0))
-    mine = pl.BlockSpec((BQ, width), lambda i, *_: (i, 0))
+    vmem = pl.BlockSpec(memory_space=pltpu.VMEM)
     return pl.pallas_call(
         functools.partial(backward_kernel, heads),
         out_shape=(jax.ShapeDtypeStruct((length, width), jnp.bfloat16),) * 3
         + (jax.ShapeDtypeStruct((1, width), jnp.float32),),
-        grid_spec=pltpu.PrefetchScalarGridSpec(
-            num_scalar_prefetch=1,
-            grid=(blocks,),
-            in_specs=[
-                whole,
-                mine,
-                mine,
-                whole,
-                whole,
-                pl.BlockSpec((blocks, 1, BQ), lambda i, *_: (0, 0, 0)),
-                pl.BlockSpec((1, width), lambda i, *_: (0, 0)),
-                pl.BlockSpec((blocks, 1, heads * BQ), lambda i, *_: (0, 0, 0)),
-            ],
-            out_specs=(whole, mine, mine, pl.BlockSpec((1, width), lambda i, *_: (0, 0))),
-            scratch_shapes=[
-                pltpu.VMEM((blocks, heads * BQ, width), jnp.bfloat16),
-                pltpu.VMEM((blocks, heads * BQ, width), jnp.bfloat16),
-                pltpu.VMEM((blocks, 1, heads * BQ), jnp.float32),
-                pltpu.VMEM((blocks, width, heads * BQ), jnp.float32),
-                pltpu.VMEM((BQ, width), jnp.float32),
-                pltpu.VMEM((BQ, width), jnp.float32),
-            ],
-        ),
+        in_specs=[pl.BlockSpec(memory_space=pltpu.SMEM)] + [vmem] * 8,
+        out_specs=(vmem,) * 4,
+        scratch_shapes=[
+            pltpu.VMEM((blocks, heads * BQ, width), jnp.bfloat16),
+            pltpu.VMEM((blocks, heads * BQ, width), jnp.bfloat16),
+            pltpu.VMEM((blocks, 1, heads * BQ), jnp.float32),
+            pltpu.VMEM((blocks, width, heads * BQ), jnp.float32),
+            pltpu.VMEM((BQ, width), jnp.float32),
+            pltpu.VMEM((BQ, width), jnp.float32),
+        ],
         cost_estimate=pl.CostEstimate(
             flops=3 * length * length * width, bytes_accessed=32 * length * width, transcendentals=0
         ),
@@ -495,15 +495,15 @@
 
 
 class Scatter:
-    def __init__(self, place, refs, sems, base, left, right, write):
-        self.place, self.base, self.left, self.right, self.write = place, base, left, right, write
+    def __init__(self, place, refs, sems, x_first, left, right, write):
+        self.place, self.x_first, self.left, self.right, self.write = place, x_first, left, right, write
         self.whole, self.first, self.second, self.near, self.far = refs
         self.send, self.receive = sems
         self.rows, self.columns = self.whole.shape[-2:]
 
     def axes(self, p):
         place = self.place
-        if p % 2 == 0:
+        if p not in self.x_first:
             return place.y, place.x, place.y_partner(), place.x_partner()
         return place.x, place.y, place.x_partner(), place.y_partner()
 
@@ -518,7 +518,7 @@
             source, target, device = self.second.at[p, :, 1 - place.z0], self.near.at[p], place.near_partner()
         else:
             source, target, device = self.near.at[p, 1 - place.z1], self.far.at[p], place.far_partner()
-        index = self.base + p
+        index = p
         return remote(source, target, self.send.at[stage, index], self.receive.at[stage, index], device)
 
     def compute(self, p):
@@ -533,7 +533,7 @@
                 for k in range(4):
                     x = k % 2
                     part = block[k * rows : (k + 1) * rows]
-                    if p % 2 == 0:
+                    if p not in self.x_first:
                         self.whole[p, y, half, k // 2, x] = part
                     else:
                         self.whole[p, x, half, k // 2, y] = part
@@ -804,6 +804,15 @@
     )(tokens, gain.reshape(1, width), ids, w_triple, w_out, w_up)
 
 
+MIDDLE_ALONE = (0, 2, 3)
+MIDDLE_X_FIRST = (1, 3)
+MIDDLE_ORDER = (
+    1100, 600, 1200, 1300, 1400, 700, 701, 702, 602, 501, 703, 1500, 601, 3, 603, 0, 800, 801,
+    1, 802, 900, 901, 103, 100, 2, 902, 903, 203, 1000, 1001, 101, 303, 1600, 200, 1700, 102,
+    300, 403, 201, 1800, 400, 202, 301, 302, 1900, 401, 402,
+)
+
+
 def middle_kernel(
     u, tokens, cotangent, post_gain, second_gain, mid_gain, w_out, w_up, w_down,
     o_layer, o_middle, o_heads, o_merged, o_second, o_hidden, o_projected, o_gains, o_down,
@@ -822,7 +831,7 @@
 
     inbound = ToTokens(place, u, merged_s, relay.at[0], [sem.at[0] for sem in exchange_sem], local_sem.at[0])
     gather = Gather(place, (g_send, g_recv))
-    alone = (0, 1)
+    alone = MIDDLE_ALONE
     chunks, mine = [], []
     for k in range(4):
 
@@ -867,28 +876,26 @@
     parts = jnp.where(row == 0, part_one.astype(wide), jnp.where(row == 1, part_two.astype(wide), part_three.astype(wide)))
     act_s[pl.ds(local, 16), :] = jnp.where(row < 3, parts, 0.0).astype(LOW)
 
-    inbound.pass_on()
-    across(0)
-    forward(2)
-    inbound.finish()
-    wait_all(loads)
-    save(merged_s, o_merged, 8)
-
-    def blocks(count, body):
+    def blocks(first, count, body):
         def one(n, carry):
-            body(n)
+            body(n + first)
             return carry
 
         lax.fori_loop(0, count, one, 0)
 
     def span(n, size):
         return pl.ds(pl.multiple_of(n * size, size), size)
+
+    later = {}
+
+    def arrive(_):
+        inbound.finish()
+        wait_all(loads)
+        save(merged_s, o_merged, 8)
 
     def project(n):
         at = span(n, 256)
         far_s[:, at] = jnp.dot(merged_s[...], out_s[:, at], preferred_element_type=wide)
-
-    blocks(width // 256, project)
 
     def norms(n):
         rows = span(n, 128)
@@ -898,9 +905,6 @@
         middle = tokens[rows, :].astype(wide) + unit * post_gain[...]
         middle_s[rows, :] = middle
         second_s[rows, :] = (norm_parts(middle)[0] * second_gain[...]).astype(LOW)
-
-    blocks(local // 128, norms)
-    save(second_s, o_second, 9)
 
     def grow(n):
         at = span(n, 256)
@@ -912,20 +916,6 @@
         unit_s[:, at] = z * half
         slope_s[:, at] = half + 0.5 * root * z * (1.0 - bent * bent) * (1.0 + 3.0 * 0.044715 * square)
 
-    half_way = hidden // 512
-
-    def grow_from(first):
-        def body(n):
-            grow(n + first)
-
-        return body
-
-    blocks(half_way, grow_from(0))
-    across(1)
-    across(2)
-    forward(3)
-    blocks(half_way, grow_from(half_way))
-
     def hidden_norm(n):
         rows = span(n, 32)
         unit, inverse = norm_parts(unit_s[rows, :])
@@ -933,13 +923,12 @@
         inner_s[rows, :] = jnp.broadcast_to(inverse, (32, 128))
         act_s[rows, :] = (unit * gain).astype(LOW)
 
-    blocks(local // 32, hidden_norm)
-    left = share_left(place, 10, act_s, d_left, local, *sems)
-    across(3)
-    for k in range(4):
-        chunks[k][0].wait_recv()
-        chunks[k][3].wait_recv()
-        mine[k].wait()
+    def settle_weights():
+        for k in range(4):
+            chunks[k][0].wait_recv()
+            chunks[k][3].wait_recv()
+            mine[k].wait()
+        grad_s[...] = jnp.zeros_like(grad_s)
 
     def shrink(n):
         at = span(n, 256)
@@ -953,20 +942,13 @@
         grad_s[0] = grad_s[0] + jnp.broadcast_to(first, (local, 128))
         grad_s[1] = grad_s[1] + jnp.broadcast_to(second, (local, 128))
 
-    grad_s[...] = jnp.zeros_like(grad_s)
-    blocks(width // 256, shrink)
-
     def write_down(p, value):
         o_down[:, pl.ds(p * 256, 256)] = value
 
     down = Scatter(
-        place, (d_whole, d_first, d_second, d_near, d_far), (s_send, s_recv), 0,
+        place, (d_whole, d_first, d_second, d_near, d_far), (s_send, s_recv), MIDDLE_X_FIRST,
         lambda p: d_left, lambda p: d_right.at[:, pl.ds(p * 256, 256)], write_down,
     )
-    wait_all(right)
-    wait_all(left)
-    for p in range(4):
-        down.compute(p)
 
     def pull_hidden(n):
         at = span(n, 256)
@@ -976,16 +958,9 @@
         pulled = grad * mid_gain[:, at] - grad_s[0][:, 0:1] - unit * grad_s[1][:, 0:1]
         hidden_s[:, at] = (inner_s[:, 0:1] * pulled * slope_s[:, at]).astype(LOW)
 
-    blocks(hidden // 256, pull_hidden)
-    save(hidden_s, o_hidden, 15)
-    for p in range(2):
-        down.advance(p, 1)
-
     def pull_second(n):
         at = span(n, 256)
         o_middle[:, at] = nt(hidden_s[...], up_s[at, :])
-
-    blocks(width // 256, pull_second)
 
     def pull_norms(n, totals):
         rows = span(n, 128)
@@ -1000,36 +975,73 @@
             totals[1] + jnp.sum(grad * unit, axis=0, keepdims=True),
         )
 
-    nothing = jnp.zeros((1, width), wide)
-    post, second = lax.fori_loop(0, local // 128, pull_norms, (nothing, nothing))
-    o_gains[1:2, 0:width] = post
-    o_gains[2:3, 0:width] = second
-    save(projected_s, o_projected, 16)
-
     def pull_merged(n):
         at = span(n, 256)
         merged_s[:, at] = nt(projected_s[...], out_s[at, :]).astype(LOW)
 
-    saves[0].wait()
-    blocks(width // 256, pull_merged)
-    outbound = ToHeads(
-        place, merged_s, o_heads, relay.at[1], [sem.at[1] for sem in exchange_sem], local_sem.at[17]
-    )
-    down.advance(2, 1)
-    down.advance(0, 2)
-    down.advance(1, 2)
-    outbound.pass_on()
-    down.advance(3, 1)
-    down.advance(2, 2)
-    down.advance(0, 3)
-    down.advance(1, 3)
-    down.advance(3, 2)
-    for p in range(4):
-        if p > 1:
-            down.advance(p, 3)
-    for p in range(4):
-        down.advance(p, 4)
-    outbound.finish()
+    def compute(p):
+        if later.get("left"):
+            wait_all(right)
+            wait_all(later.pop("left"))
+        down.compute(p)
+
+    def do_norms(_):
+        blocks(0, local // 128, norms)
+        save(second_s, o_second, 9)
+
+    def do_hidden_norm(_):
+        blocks(0, local // 32, hidden_norm)
+        later["left"] = share_left(place, 10, act_s, d_left, local, *sems)
+
+    def do_shrink(n):
+        if n == 0:
+            settle_weights()
+        else:
+            blocks((n - 1) * 2, 2, shrink)
+
+    def do_pull_hidden(n):
+        blocks(n * (hidden // 1024), hidden // 1024, pull_hidden)
+        if n == 3:
+            save(hidden_s, o_hidden, 15)
+
+    def do_pull_norms(_):
+        nothing = jnp.zeros((1, width), wide)
+        post, second = lax.fori_loop(0, local // 128, pull_norms, (nothing, nothing))
+        o_gains[1:2, 0:width] = post
+        o_gains[2:3, 0:width] = second
+        save(projected_s, o_projected, 16)
+
+    def do_pull_merged(_):
+        saves[0].wait()
+        blocks(0, width // 256, pull_merged)
+        later["out"] = ToHeads(
+            place, merged_s, o_heads, relay.at[1], [sem.at[1] for sem in exchange_sem], local_sem.at[17]
+        )
+
+    act = (
+        compute,
+        lambda p: down.advance(p, 1),
+        lambda p: down.advance(p, 2),
+        lambda p: down.advance(p, 3),
+        lambda p: down.advance(p, 4),
+        forward,
+        across,
+        lambda n: blocks(n * (hidden // 1024), hidden // 1024, grow),
+        do_shrink,
+        do_pull_hidden,
+        lambda n: blocks(n * 2, 2, pull_second),
+        lambda n: inbound.pass_on(),
+        arrive,
+        lambda n: blocks(0, width // 256, project),
+        do_norms,
+        do_hidden_norm,
+        do_pull_norms,
+        do_pull_merged,
+        lambda n: later["out"].pass_on(),
+        lambda n: later["out"].finish(),
+    )
+    for code in MIDDLE_ORDER:
+        act[code // 100](code % 100)
     wait_all(saves[1:])
     for p in range(4):
         down.settle(p)
@@ -1101,6 +1113,17 @@
     )
 
 
+HALF = 512
+X_FIRST = (1, 3, 5, 12, 13)
+TAIL_ORDER = (
+    0, 3, 7, 9, 500, 1, 100, 2, 103, 4, 5, 600, 700, 15, 101, 501, 200, 107, 102, 109,
+    8, 203, 6, 105, 14, 601, 303, 502, 701, 12, 104, 115, 201, 207, 300, 202, 13, 209, 108, 602,
+    702, 800, 900, 302, 106, 205, 309, 112, 301, 11, 204, 305, 402, 400, 901, 215, 304, 401, 307, 405,
+    212, 403, 114, 10, 409, 113, 315, 208, 111, 404, 312, 206, 902, 415, 308, 407, 306, 412, 214, 110,
+    408, 213, 211, 406, 314, 313, 210, 311, 310, 414, 413, 411, 410,
+)
+
+
 def tail_kernel(
     dq, dk, dv, tokens, gain, middle, triple, act_up, act_out, act_in, g_up, g_out, gains, scales,
     o_tokens, o_triple, o_out, o_up, o_gains,
@@ -1110,10 +1133,11 @@
 ):
     place = Place()
     partner = place.core_partner()
-    column_peers = [(place.dp, (place.z + k) % 4 * 2 + place.x) for k in range(1, 4)]
     local, width = tokens.shape
     heads_width = dq.shape[1]
-    meet(column_peers + [place.x_partner(), partner, place.y_partner()])
+    seq_peers = [(place.dp, (place.seq + k) % 8) for k in range(1, 8)]
+    dp_peers = [((place.dp + k) % 4, place.seq) for k in range(1, 4)]
+    meet(seq_peers + dp_peers)
 
     def start_exchange(t):
         return ToTokens(
@@ -1121,85 +1145,51 @@
             [sem.at[t] for sem in (x_send, x_recv, z_send, z_recv)], local_sem.at[13 + t],
         )
 
-    exchanges = [start_exchange(0), start_exchange(1)]
+    exchanges = [start_exchange(t) for t in range(3)]
 
     sems = (local_sem, core_send, core_recv)
     ready = {"up": share_left(place, 0, act_up, e_left.at[0], local, *sems)}
     for k in range(4):
         part = g_up.at[:, pl.ds(k * BLOCK, BLOCK)]
-        ready["up"] += share(place, 2 + k, part, part, e_right.at[k], local, *sems)
+        ready[k] = share(place, 2 + k, part, part, e_right.at[k], local, *sems)
     ready["out"] = share_left(place, 6, act_out, e_left.at[1], local, *sems)
     ready["out"] += share(place, 8, g_out, g_out, e_right.at[4], local, *sems)
     ready["in"] = share_left(place, 9, act_in, e_left.at[2], local, *sems)
 
-    def write_rest(p, value):
-        if p < 4:
-            o_up[:, pl.ds(p * BLOCK, BLOCK)] = value
-        elif p == 4:
-            o_out[...] = value
+    def write(p, value):
+        at = pl.ds(p % 2 * HALF, HALF)
+        if p < 8:
+            o_up[:, pl.ds(p * HALF, HALF)] = value
+        elif p < 10:
+            o_out[:, at] = value
         else:
-            o_triple[:, pl.ds((p - 5) * BLOCK, BLOCK)] = value
-
-    rest = Scatter(
-        place, (e_whole, e_first, e_second, e_near, e_far), (s_send, s_recv), 0,
-        lambda p: e_left.at[0 if p < 4 else 1 if p == 4 else 2], lambda p: e_right.at[p], write_rest,
-    )
-    order = [(rest, k) for k in (0, 1, 2, 3, 4, 7, 6, 5)]
+            o_triple[:, pl.ds((p - 10) * HALF, HALF)] = value
+
+    engine = Scatter(
+        place, (e_whole, e_first, e_second, e_near, e_far), (s_send, s_recv), X_FIRST,
+        lambda p: e_left.at[0 if p < 8 else 1 if p < 10 else 2],
+        lambda p: e_right.at[p // 2, :, pl.ds(p % 2 * HALF, HALF)], write,
+    )
     gain_s[...] = gains[...]
     gain_s[7:8, 0:128] = scales[...]
-    marks = {"compute": 0, 1: 0, 2: 0, 3: 0, 4: 0}
-
-    def advance(stage, upto):
-        while marks[stage] < min(upto, len(order)):
-            engine, p = order[marks[stage]]
-            engine.advance(p, stage) if stage != "compute" else engine.compute(p)
-            marks[stage] += 1
-
-    wait_all(ready["up"])
-    advance("compute", 2)
-    advance(1, 1)
-    exchanges[0].pass_on()
-    advance("compute", 3)
-    advance(1, 2)
-    advance(2, 1)
-    exchanges.append(start_exchange(2))
-    wait_all(ready["out"])
-    advance("compute", 4)
-    advance(1, 3)
-    exchanges[1].pass_on()
-    advance("compute", 5)
-    advance(1, 4)
-    advance(2, 2)
-    exchanges[2].pass_on()
-
-    for exchange in exchanges:
-        exchange.finish()
-    back = [
-        remote(
-            e_right.at[5 + t, pl.ds(0, local), :], e_right.at[5 + t, pl.ds(local, local), :],
+    def bring_back(t):
+        exchanges[t].finish()
+        slot = e_right.at[7 - t]
+        move = remote(
+            slot.at[pl.ds(0, local), :], slot.at[pl.ds(local, local), :],
             core_send.at[11 + t], core_recv.at[11 + t], partner,
         )
-        for t in range(3)
-    ]
-    for move in back:
         move.start()
-
-    def columns_of(n, carry):
-        rows = pl.ds(pl.multiple_of(n * 256, 256), 256)
-        total = jnp.zeros((local, 256), jnp.float32)
-        for t in range(3):
-            total += nt(e_right[5 + t, pl.ds(0, local), :], triple[rows, pl.ds(t * width, width)])
-        grad_s[:, rows] = total
-        return carry
-
-    wait_all(ready["in"])
-    wait_all(back)
-    advance("compute", 8)
-    advance(1, 5)
-    advance(2, 4)
-    lax.fori_loop(0, width // 256, columns_of, 0)
-    advance(3, 2)
-    advance(1, 6)
+        return move
+
+    def pull_normed(t):
+        def one(n, carry):
+            rows = pl.ds(pl.multiple_of(n * 256, 256), 256)
+            part = nt(e_right[7 - t, pl.ds(0, local), :], triple[rows, pl.ds((2 - t) * width, width)])
+            grad_s[:, rows] = part if t == 0 else grad_s[:, rows] + part
+            return carry
+
+        lax.fori_loop(0, width // 256, one, 0)
 
     def norm_rows(n, total):
         rows = pl.ds(pl.multiple_of(n * 128, 128), 128)
@@ -1209,27 +1199,67 @@
         o_tokens[rows, :] = (middle[rows, :] + pulled).astype(LOW)
         return total + jnp.sum(grad * unit, axis=0, keepdims=True)
 
-    gain_s[0:1, :] = lax.fori_loop(0, local // 128, norm_rows, jnp.zeros((1, width), jnp.float32))
-
-    meets = (partner, place.y_partner(), place.x_partner(), place.near_partner(), place.far_partner())
-
-    for k in range(5):
-        move = remote(gain_s, gain_r.at[k], gain_send.at[k], gain_recv.at[k], meets[k])
-        move.start()
-        advance(1, 7 + k // 2)
-        advance(2, 5 + k // 2)
-        advance(3, 3 + k // 2)
-        advance(4, 1 + k // 2)
-        move.wait()
-        gain_s[...] = gain_s[...] + gain_r[k]
-        if k == 1:
+    def pull_norm(_):
+        gain_s[0:1, :] = lax.fori_loop(0, local // 128, norm_rows, jnp.zeros((1, width), jnp.float32))
+
+    def gain_moves(peers, first):
+        out = [
+            remote(gain_s, gain_r.at[first + k], gain_send.at[first + k], gain_recv.at[first + k], peer)
+            for k, peer in enumerate(peers)
+        ]
+        for move in out:
+            move.start()
+        return out
+
+    gain_steps = {}
+
+    def sum_gains(step):
+        if step == 0:
+            gain_steps[0] = gain_moves(dp_peers, 0)
+        elif step == 1:
+            wait_all(gain_steps[0])
+            gain_s[...] = gain_s[...] + gain_r[0] + gain_r[1] + gain_r[2]
             o_gains[7:8, :] = gain_s[7:8, 0:128]
-    for n in range(8):
-        advance(2, n + 1)
-        advance(3, n)
-        advance(4, n - 1)
-    advance(3, 8)
-    advance(4, 8)
+            gain_steps[1] = gain_moves(seq_peers, 3)
+        else:
+            wait_all(gain_steps[1])
+            total = gain_s[...]
+            for k in range(7):
+                total = total + gain_r[3 + k]
+            gain_s[...] = total
+
+    backs, waited = {}, set()
+
+    def need(key):
+        if key not in waited:
+            wait_all(ready[key])
+            waited.add(key)
+
+    def compute(p):
+        need("up" if p < 8 else "out" if p < 10 else "in")
+        if p < 8:
+            need(p // 2)
+        elif p >= 10 and 7 - p // 2 in backs:
+            backs.pop(7 - p // 2).wait()
+        engine.compute(p)
+
+    def bring(t):
+        backs[t] = bring_back(t)
+
+    act = (
+        compute,
+        lambda p: engine.advance(p, 1),
+        lambda p: engine.advance(p, 2),
+        lambda p: engine.advance(p, 3),
+        lambda p: engine.advance(p, 4),
+        lambda t: exchanges[t].pass_on(),
+        bring,
+        pull_normed,
+        pull_norm,
+        sum_gains,
+    )
+    for code in TAIL_ORDER:
+        act[code // 100](code % 100)
     device = place.dp * 8 + place.seq
     pick = (
         lax.broadcasted_iota(jnp.int32, (width, 128), 0)
@@ -1242,7 +1272,7 @@
     row = lax.broadcasted_iota(jnp.int32, block.shape, 0)
     o_gains[3:4, :] = jnp.sum(jnp.where(row == 3 + device // 8, block, 0.0), axis=0, keepdims=True)
     o_gains[4:7, :] = jnp.zeros((3, 128), jnp.float32)
-    for engine, p in order:
+    for p in range(16):
         engine.settle(p)
 
 
@@ -1266,20 +1296,20 @@
         in_specs=[any_spec] * 3 + [vmem] * 4 + [any_spec] * 5 + [vmem] * 2,
         out_specs=(vmem,) * 5,
         scratch_shapes=[pltpu.VMEM((3, 2 * local, width // 2), LOW), pltpu.VMEM((8, 2 * local, width), LOW)]
-        + scatter_scratch(8, 32, 1024)
+        + scatter_scratch(16, 32, HALF)
         + [
             pltpu.VMEM((local, width), wide),
             pltpu.VMEM((8, width), wide),
-            pltpu.VMEM((5, 8, width), wide),
+            pltpu.VMEM((10, 8, width), wide),
             pltpu.VMEM((3, 3, local, heads_width), LOW),
             dma((20,)),
             dma((20,)),
             dma((20,)),
             *exchange_sems(3),
-            dma((4, 8)),
-            dma((4, 8)),
-            dma((5,)),
-            dma((5,)),
+            dma((4, 16)),
+            dma((4, 16)),
+            dma((10,)),
+            dma((10,)),
         ],
         compiler_params=pltpu.CompilerParams(
             collective_id=3, has_side_effects=True, vmem_limit_bytes=VMEM_BYTES

time: 406 us -> 360 us (0.89)
  Pallas kernels: 392 us -> 347 us
    pallas_call x1, Pallas kernels: 139 us -> 111 us  [tail(): pl.pallas_call(tail_kernel, out_shape=(jax.ShapeDtypeStruct((local, width...]
    pallas_call x1, Pallas kernels: 120 us -> 111 us  [middle(): pl.pallas_call(middle_kernel, out_shape=(act, jax.ShapeDtypeStruct((local...]
    pallas_call x1, Pallas kernels: 22.3 us -> 16.4 us  [attend_forward(): pl.pallas_call(functools.partial(forward_kernel, heads), out_shape=(jax.S...]
where the time goes in v4:
time: 360 us
  Pallas kernels  347 us (96%)
  local copies, waits for them, and re-layouts  10 us (3%)
    pallas_call x1, Pallas kernels, tail(): pl.pallas_call(tail_kernel, out_shape=(jax.ShapeDtypeStruct((local, width...  111 us
    pallas_call x1, Pallas kernels, middle(): pl.pallas_call(middle_kernel, out_shape=(act, jax.ShapeDtypeStruct((local...  111 us
    pallas_call x1, Pallas kernels, front(): pl.pallas_call(front_kernel, out_shape=(one, one, one, jax.ShapeDtypeStru...  84.1 us
    pallas_call x1, Pallas kernels, attend_backward(): pl.pallas_call(functools.partial(backward_kernel, heads), out_shape=(jax....  25 us
    pallas_call x1, Pallas kernels, attend_forward(): pl.pallas_call(functools.partial(forward_kernel, heads), out_shape=(jax.S...  16.4 us

profile of v4, /device:TPU:0, one launch (start us, length us, event | category | flops | bytes accessed | tf_op | source)
XLA Modules:
  0.0 359.6 jit_solution(14942078819311128890)
XLA Ops:
  0.6 0.0 copy-start.6
  0.7 84.1 %front.1 = (bf16[3072,128]{1,0:T(8,128)(2,1)}, bf16[3072,128]{1,0:T(8,128)(2,1)}, bf16[3072,128]{1,0:T(8,128)(2,1)}, bf16[384,1024]{1,0:T(8,128)(2,1)}, s32[12,1...) custom-call(bf16[384,1024]{1,0:T(8,128)(2,1)} %bitcast.17, ...), custom_call_target="tpu_custom_call" | custom-call | tf_op jit(solution)/shard_map/front/pallas_call | solution.py:775
  84.8 0.0 copy-done.6
  84.8 0.1 dynamic_slice.3
  84.9 0.1 broadcast_in_dim.12
  84.9 0.6 broadcast_in_dim_reshape.3.scale_ref
  85.5 16.4 %attend_forward.1 = (f32[3072,128]{1,0:T(8,128)}, bf16[3072,128]{1,0:T(8,128)(2,1)}, f32[12,1,512]{2,1,0:T(1,128)}) custom-call(s32[12,1,256]{2,1,0:T(1,128)} %get-tuple-element.40.first_ref.start_ref, bf16[3072,128]{1,0:T(8,128)(2,1)} %get-tuple-element.41.q_ref, bf16[3072,128]{1,0:T(8,128)(2,1)} %get-tuple-element.42.k_ref, ...), custom_call_target="tpu_custom_call" | custom-call | flops 1207959552 | bytes 6291456 | tf_op jit(solution)/shard_map/attend_forward/pallas_call | solution.py:119
  101.9 110.8 %middle.1 = (bf16[384,1024]{1,0:T(8,128)(2,1)}, f32[384,1024]{1,0:T(8,128)}, bf16[3072,128]{1,0:T(8,128)(2,1)}, bf16[384,1024]{1,0:T(8,128)(2,1)}, bf16[384,1024...) custom-call(bf16[3072,128]{1,0:T(8,128)(2,1)} %get-tuple-element.44., ...), custom_call_target="tpu_custom_call" | custom-call | tf_op jit(solution)/shard_map/middle/pallas_call | solution.py:1062
  212.8 1.0 slice_reduce_fusion
  213.7 0.8 slice.21
  214.5 0.1 pad.2.clone
  214.6 0.7 maximum_maximum_fusion.gains
  215.3 25.0 %attend_backward.1 = (bf16[3072,128]{1,0:T(8,128)(2,1)}, bf16[3072,128]{1,0:T(8,128)(2,1)}, bf16[3072,128]{1,0:T(8,128)(2,1)}, f32[1,128]{1,0:T(1,128)}) custom-call(s32[12,1,256]{2,1,0:T(1,128)} %get-tuple-element.40.first_ref.start_ref, bf16[3072,128]{1,0:T(8,128)(2,1)} %get-tuple-element.41.q_ref, bf16[3072,128]{1,0:T(8,128)(2,1)} %get-tuple-element.42.k_ref, ...), custom_call_target="tpu_custom_call" | custom-call | flops 3623878656 | bytes 12582912 | tf_op jit(solution)/shard_map/attend_backward/pallas_call | solution.py:226
  240.3 0.0 copy-start
  240.3 111.2 %tail.1 = (bf16[384,1024]{1,0:T(8,128)(2,1)}, f32[32,3072]{1,0:T(8,128)}, f32[32,1024]{1,0:T(8,128)}, f32[32,4096]{1,0:T(8,128)}, f32[8,128]{1,0:T(8,128)}) custom-call(bf16[3072,128]{1,0:T(8,128)(2,1)} %get-tuple-element.51.dq, bf16[3072,128]{1,0:T(8,128)(2,1)} %get-tuple-element.52.dk, bf16[3072,128]{1,0:T(8,128)(2,1)} %get-tuple-element.53.dv, ...), custom_call_target="tpu_custom_call" | custom-call | tf_op jit(solution)/shard_map/tail/pallas_call | solution.py:1287
  351.4 0.0 copy-start.1
  351.4 0.0 copy-start.4
  351.5 0.0 copy-start.5
  351.5 1.3 slice_bitcast_fusion
  352.8 0.1 reshape_squeeze.7
  352.8 0.6 reduce_sum.9
  353.5 1.3 slice_bitcast_fusion.1
  354.8 0.0 copy-done
  354.8 0.0 copy-start.3
  354.8 0.9 copy.29
  355.7 0.0 copy-done.1
  355.7 0.0 copy-start.2
  355.7 0.9 copy.30
  356.5 0.0 copy-done.4
  356.6 0.7 copy.31
  357.3 0.0 copy-done.5
  357.3 0.7 copy.32
  358.0 0.0 copy-done.3
  358.0 0.8 copy.33
  358.8 0.0 copy-done.2
  358.8 0.8 copy.34
  (1 shorter events, 0.0 us)
Async XLA Ops:
  0.6 84.1 %copy-start.6 = (f32[16]{0:T(128)S(1)}, f32[16]{0:T(128)}, u32[]{:S(2)}) copy-start(f32[16]{0:T(128)} %param.16) | copy-start | bytes 196
  240.3 114.5 %copy-start = (bf16[384,1024]{1,0:T(8,128)(2,1)S(1)}, bf16[384,1024]{1,0:T(8,128)(2,1)}, u32[]{:S(2)}) copy-start(bf16[384,1024]{1,0:T(8,128)(2,1)} %get-tuple-element.47) | copy-start | bytes 2359300
  351.4 4.2 %copy-start.1 = (bf16[384,1024]{1,0:T(8,128)(2,1)S(1)}, bf16[384,1024]{1,0:T(8,128)(2,1)}, u32[]{:S(2)}) copy-start(bf16[384,1024]{1,0:T(8,128)(2,1)} %get-tuple-element.63) | copy-start | bytes 2359300
  351.4 5.1 %copy-start.4 = (f32[32,3072]{1,0:T(8,128)S(1)}, f32[32,3072]{1,0:T(8,128)}, u32[]{:S(2)}) copy-start(f32[32,3072]{1,0:T(8,128)} %get-tuple-element.88) | copy-start | bytes 1179652
  351.5 5.8 %copy-start.5 = (f32[32,1024]{1,0:T(8,128)S(1)}, f32[32,1024]{1,0:T(8,128)}, u32[]{:S(2)}) copy-start(f32[32,1024]{1,0:T(8,128)} %get-tuple-element.90) | copy-start | bytes 393220
  354.8 3.2 copy-start.3
  355.7 3.1 copy-start.2

commit v5 on v4

--- a/solution.py
+++ b/solution.py
@@ -9,9 +9,8 @@
 HEAD = 64
 NEG = -1e30
 BQ = 256
-QB = 512
+QB = 1024
 KB = 512
-WIDE = 1
 
 
 def nt(a, b):
@@ -40,9 +39,20 @@
     )
 
 
+def scale_row(scale_ref, width):
+    heads = width // HEAD
+    first = lax.axis_index("seq") * heads
+    lane = lax.broadcasted_iota(jnp.int32, (1, width), 1)
+    row = jnp.full((1, width), scale_ref[first], jnp.float32)
+    for h in range(1, heads):
+        row = jnp.where(lane >= h * HEAD, scale_ref[first + h], row)
+    return row
+
+
 def forward_kernel(heads, first_ref, q_ref, k_ref, v_ref, start_ref, scale_ref,
                    o_ref, u_ref, lse_ref, m_s, l_s, acc_s):
     rows, step_rows = QB, KB
+    scale = scale_row(scale_ref, q_ref.shape[1])
     ratio = rows // step_rows
 
     def one(i, carry):
@@ -50,57 +60,65 @@
         queries = stack_heads(q_ref[mine, :] * jnp.bfloat16(HEAD ** -0.5), heads)
         starts = jnp.concatenate([start_ref[i * (rows // BQ) + k] for k in range(rows // BQ)] * heads, axis=1)
 
-        def step(j, count, masked, diagonal):
-            at = pl.ds(pl.multiple_of(j * step_rows, step_rows), count * step_rows)
+        def scores_of(j, count, queries, starts):
+            at = pl.ds(pl.multiple_of(j * BQ, BQ), count)
             scores = nt(k_ref[at, :], queries)
-            if masked or diagonal:
-                key = j * step_rows + lax.broadcasted_iota(jnp.int32, scores.shape, 0)
-                allowed = key >= starts
-                if diagonal:
-                    lane = lax.broadcasted_iota(jnp.int32, scores.shape, 1) & (rows - 1)
-                    allowed = allowed & (key <= i * rows + lane)
-                scores = jnp.where(allowed, scores, NEG)
-            highest = jnp.max(scores, axis=0, keepdims=True)
-            if not diagonal:
-                before = m_s[...]
-                highest = jnp.maximum(before, highest)
-                fade = jnp.exp(before - highest)
+            if starts is not None:
+                key = j * BQ + lax.broadcasted_iota(jnp.int32, scores.shape, 0)
+                scores = jnp.where(key >= starts, scores, NEG)
+            return at, scores
+
+        def fold(at, scores, columns):
+            before = m_s[:, columns]
+            highest = jnp.maximum(before, jnp.max(scores, axis=0, keepdims=True))
+            fade = jnp.exp(before - highest)
             weights = jnp.exp(scores - highest)
-            total = jnp.sum(weights, axis=0, keepdims=True)
-            part = tn(v_ref[at, :], weights.astype(jnp.bfloat16))
-            m_s[...] = highest
-            if diagonal:
-                l_s[...] = total
-                acc_s[...] = part
-            else:
-                l_s[...] = l_s[...] * fade + total
-                acc_s[...] = acc_s[...] * fade + part
-
-        step(i * ratio, ratio, False, True)
+            m_s[:, columns] = highest
+            l_s[:, columns] = l_s[:, columns] * fade + jnp.sum(weights, axis=0, keepdims=True)
+            acc_s[:, columns] = acc_s[:, columns] * fade + tn(v_ref[at, :], weights.astype(jnp.bfloat16))
+
+        def step(j, masked):
+            at, scores = scores_of(j * (step_rows // BQ), step_rows, queries, starts if masked else None)
+            fold(at, scores, slice(None))
+
+        for k in range(rows // BQ):
+            wide = rows - k * BQ
+            late = [slice(h * rows + k * BQ, (h + 1) * rows) for h in range(heads)]
+            some = queries if k == 0 else jnp.concatenate([queries[c] for c in late], axis=0)
+            start = starts if k == 0 else jnp.concatenate([starts[:, c] for c in late], axis=1)
+            at, scores = scores_of(i * (rows // BQ) + k, BQ, some, start)
+            key = lax.broadcasted_iota(jnp.int32, scores.shape, 0)
+            for h in range(heads):
+                part = scores[:, h * wide : (h + 1) * wide]
+                lane = lax.broadcasted_iota(jnp.int32, part.shape, 1)
+                part = jnp.where(key[:, :wide] <= lane, part, NEG)
+                if k == 0:
+                    highest = jnp.max(part, axis=0, keepdims=True)
+                    weights = jnp.exp(part - highest)
+                    m_s[:, late[h]] = highest
+                    l_s[:, late[h]] = jnp.sum(weights, axis=0, keepdims=True)
+                    acc_s[:, late[h]] = tn(v_ref[at, :], weights.astype(jnp.bfloat16))
+                else:
+                    fold(at, part, late[h])
+
         low = first_ref[i * (rows // BQ), 0, 0] // step_rows
         last = first_ref[i * (rows // BQ) + rows // BQ - 1, 0, BQ - 1]
         full = jnp.minimum((last + step_rows - 1) // step_rows, i * ratio)
-        pairs = (i * ratio - full) // WIDE
-
-        def wide(n, carry):
-            step(i * ratio - WIDE * (n + 1), WIDE, False, False)
+
+        def plain(j, carry):
+            step(j, False)
             return carry
 
-        def plain(j, carry):
-            step(j, 1, False, False)
+        def edge(j, carry):
+            step(j, True)
             return carry
 
-        def edge(j, carry):
-            step(j, 1, True, False)
-            return carry
-
-        lax.fori_loop(0, pairs, wide, 0)
-        lax.fori_loop(full, i * ratio - WIDE * pairs, plain, 0)
+        lax.fori_loop(full, i * ratio, plain, 0)
         lax.fori_loop(low, full, edge, 0)
         total = l_s[...]
         out = unstack_heads(acc_s[...] * (1.0 / total), heads).T
         o_ref[mine, :] = out
-        u_ref[mine, :] = (out * scale_ref[...]).astype(jnp.bfloat16)
+        u_ref[mine, :] = (out * scale).astype(jnp.bfloat16)
         logsum = m_s[...] + jnp.log(total)
         for k in range(rows // BQ):
             lse_ref[i * (rows // BQ) + k] = jnp.concatenate(
@@ -111,19 +129,18 @@
     lax.fori_loop(0, q_ref.shape[0] // rows, one, 0)
 
 
-def attend_forward(queries, keys, values, starts, scale_wide):
+def attend_forward(queries, keys, values, starts, scales):
     length, width = queries.shape
     heads = width // HEAD
-    blocks = length // BQ
     vmem = pl.BlockSpec(memory_space=pltpu.VMEM)
     return pl.pallas_call(
         functools.partial(forward_kernel, heads),
         out_shape=(
             jax.ShapeDtypeStruct((length, width), jnp.float32),
             jax.ShapeDtypeStruct((length, width), jnp.bfloat16),
-            jax.ShapeDtypeStruct((blocks, 1, heads * BQ), jnp.float32),
+            jax.ShapeDtypeStruct((length // BQ, 1, heads * BQ), jnp.float32),
         ),
-        in_specs=[pl.BlockSpec(memory_space=pltpu.SMEM)] + [vmem] * 5,
+        in_specs=[pl.BlockSpec(memory_space=pltpu.SMEM)] + [vmem] * 4 + [pl.BlockSpec(memory_space=pltpu.SMEM)],
         out_specs=(vmem,) * 3,
         scratch_shapes=[
             pltpu.VMEM((1, heads * QB), jnp.float32),
@@ -134,40 +151,42 @@
             flops=length * length * width, bytes_accessed=16 * length * width, transcendentals=0
         ),
         name="attend_forward",
-    )(starts, queries, keys, values, starts, scale_wide)
+    )(starts, queries, keys, values, starts, scales)
 
 
 def backward_kernel(heads, first_ref, q_ref, k_ref, v_ref, o_ref, du_ref, start_ref, scale_ref, lse_ref,
                     dq_ref, dk_ref, dv_ref, ds_ref, qs_s, dos_s, delta_s, dqt_s, dk_s, dv_s):
-    rows = BQ
+    rows, group = BQ, 1
     blocks = qs_s.shape[0]
+    scale = scale_row(scale_ref, q_ref.shape[1])
 
     def prepare(i, total):
         at = pl.ds(pl.multiple_of(i * rows, rows), rows)
         qs_s[i] = stack_heads(q_ref[at, :] * jnp.bfloat16(HEAD ** -0.5), heads)
         grad = du_ref[at, :].astype(jnp.float32)
         out = o_ref[at, :]
-        low = (grad * scale_ref[...]).astype(jnp.bfloat16)
+        low = (grad * scale).astype(jnp.bfloat16)
         dos_s[i] = stack_heads(low, heads)
         inner = (low.astype(jnp.float32) * out).T
         delta_s[i] = jnp.concatenate(
             [jnp.sum(inner[h * HEAD : (h + 1) * HEAD], axis=0, keepdims=True) for h in range(heads)],
             axis=1,
         )
+        dqt_s[i] = jnp.zeros(dqt_s.shape[1:], jnp.float32)
         return total + jnp.sum(grad * out, axis=0, keepdims=True)
 
     ds_ref[...] = lax.fori_loop(0, blocks, prepare, jnp.zeros(ds_ref.shape, jnp.float32))
 
     def one(j, carry):
-        mine = pl.ds(pl.multiple_of(j * rows, rows), rows)
+        mine = pl.ds(pl.multiple_of(j * BQ, BQ), BQ)
         keys, values = k_ref[mine, :], v_ref[mine, :]
 
         def step(i, masked, diagonal):
             queries, grads = qs_s[i], dos_s[i]
             scores = nt(keys, queries)
             if masked or diagonal:
-                key = j * rows + lax.broadcasted_iota(jnp.int32, scores.shape, 0)
-                starts = jnp.concatenate([start_ref[i]] * heads, axis=1)
+                key = j * BQ + lax.broadcasted_iota(jnp.int32, scores.shape, 0)
+                starts = jnp.concatenate([start_ref[i * group + k] for k in range(group)] * heads, axis=1)
                 allowed = key >= starts
                 if diagonal:
                     lane = lax.broadcasted_iota(jnp.int32, scores.shape, 1) & (rows - 1)
@@ -189,9 +208,10 @@
 
         high, full = jnp.int32(0), jnp.int32(0)
         for i in range(blocks):
-            high += (first_ref[i, 0, 0] // rows <= j).astype(jnp.int32)
-            full += ((first_ref[i, 0, rows - 1] + rows - 1) // rows <= j).astype(jnp.int32)
-        full = jnp.maximum(full, j + 1)
+            high += (first_ref[i * group, 0, 0] // BQ <= j).astype(jnp.int32)
+            full += (first_ref[i * group + group - 1, 0, BQ - 1] <= j * BQ).astype(jnp.int32)
+        own = j // group
+        full = jnp.maximum(full, own + 1)
 
         def plain(i, carry):
             dqt_s[i] += step(i, False, False)
@@ -201,14 +221,14 @@
             dqt_s[i] += step(i, True, False)
             return carry
 
-        dqt_s[j] = step(j, False, True)
-        lax.fori_loop(j + 1, full, plain, 0)
+        dqt_s[own] += step(own, False, True)
+        lax.fori_loop(own + 1, full, plain, 0)
         lax.fori_loop(full, high, edge, 0)
         dk_ref[mine, :] = dk_s[...].astype(jnp.bfloat16)
         dv_ref[mine, :] = dv_s[...].astype(jnp.bfloat16)
         return carry
 
-    lax.fori_loop(0, blocks, lambda n, carry: one(blocks - 1 - n, carry), 0)
+    lax.fori_loop(0, blocks * group, one, 0)
 
     def finish(i, carry):
         at = pl.ds(pl.multiple_of(i * rows, rows), rows)
@@ -218,7 +238,7 @@
     lax.fori_loop(0, blocks, finish, 0)
 
 
-def attend_backward(queries, keys, values, outs, grads, starts, scale_wide, logsum):
+def attend_backward(queries, keys, values, outs, grads, starts, scales, logsum):
     length, width = queries.shape
     heads = width // HEAD
     blocks = length // BQ
@@ -227,7 +247,7 @@
         functools.partial(backward_kernel, heads),
         out_shape=(jax.ShapeDtypeStruct((length, width), jnp.bfloat16),) * 3
         + (jax.ShapeDtypeStruct((1, width), jnp.float32),),
-        in_specs=[pl.BlockSpec(memory_space=pltpu.SMEM)] + [vmem] * 8,
+        in_specs=[pl.BlockSpec(memory_space=pltpu.SMEM)] + [vmem] * 6 + [pl.BlockSpec(memory_space=pltpu.SMEM), vmem],
         out_specs=(vmem,) * 4,
         scratch_shapes=[
             pltpu.VMEM((blocks, heads * BQ, width), jnp.bfloat16),
@@ -241,7 +261,7 @@
             flops=3 * length * length * width, bytes_accessed=32 * length * width, transcendentals=0
         ),
         name="attend_backward",
-    )(starts, queries, keys, values, outs, grads, starts, scale_wide, logsum)
+    )(starts, queries, keys, values, outs, grads, starts, scales, logsum)
 
 
 def document_starts(doc_ids):
@@ -623,6 +643,13 @@
         return out
 
 
+FRONT_ALONE = (0, 2, 5, 7)
+FRONT_ORDER = (
+    500, 200, 0, 101, 300, 600, 202, 2, 201, 1, 103, 104, 302, 301, 205, 203, 106, 204,
+    206, 207, 405, 403, 404, 406, 407,
+)
+
+
 def front_kernel(
     tokens, gain, ids, w_triple, w_out, w_up,
     o_v, o_k, o_q, o_normed, o_starts, o_triple, o_out, o_up,
@@ -649,7 +676,7 @@
     plans.append((w_out, columns(o_out, 256, 0)))
     for k in range(w_up.shape[1] // width):
         plans.append((w_up.at[:, pl.ds(k * width, width)], columns(o_up, 256, k)))
-    alone = (3,)
+    alone = FRONT_ALONE
     chunks = [
         gather.copies(n, own, full, 256, n not in alone) for n, (own, full) in enumerate(plans)
     ]
@@ -676,9 +703,8 @@
         o_normed[rows, :] = (norm_parts(values)[0] * gain[...]).astype(LOW)
         return carry
 
-    lax.fori_loop(0, local // 128, norm_rows, 0)
     moves = []
-    exchanges = []
+    exchanges = {}
 
     def project(n):
         t, target = (2, 1, 0)[n], (o_v, o_k, o_q)[n]
@@ -695,7 +721,7 @@
         exchange = ToHeads(
             place, part_s.at[n], target, relay.at[n], [sem.at[n] for sem in exchange_sem], local_sem.at[12 + n]
         )
-        exchanges.append(exchange)
+        exchanges[n] = exchange
         save = pltpu.make_async_copy(
             triple_s.at[:, pl.ds(t * width, width)], o_triple.at[:, pl.ds(t * width, width)], local_sem.at[15 + n]
         )
@@ -714,48 +740,42 @@
     def finish(n):
         chunks[n][0].wait_recv()
         chunks[n][3].wait_recv()
-        if n < 3:
-            mine[n].wait()
-            project(n)
+        mine[n].wait()
+        project(n)
 
     def put_back(n):
+        chunks[n][0].wait_recv()
+        chunks[n][3].wait_recv()
         mine[n].wait()
         copy = pltpu.make_async_copy(bounce.at[n - 3], plans[n][1](place.dp, 0, 256), local_sem.at[n])
         copy.start()
         moves.append(copy)
 
-    count = len(chunks)
-    forward(0)
-    for n in range(count):
-        if n + 1 < count:
-            forward(n + 1)
-        across(n)
-        if n < 3:
-            finish(n)
-        else:
-            put_back(n)
-        if 0 < n < 4:
-            exchanges[n - 1].pass_on()
-        if n == 4:
-            for move in news:
-                move.wait()
-            every = ids_s[...]
-            starts = jnp.zeros_like(every)
-            for d in range(1, 8):
-                before = jnp.sum((every < d).astype(jnp.int32), axis=2, keepdims=True)
-                before = jnp.sum(before, axis=0, keepdims=True)
-                starts = jnp.where(every == d, before, starts)
-            for b in range(o_starts.shape[0]):
-                for piece in range(BQ // 128):
-                    at = b * BQ + piece * 128
-                    o_starts[b, :, pl.ds(piece * 128, 128)] = starts[
-                        at // local, :, at % local : at % local + 128
-                    ]
-    for n in range(3, count):
-        finish(n)
+    def document_starts_here(_):
+        for move in news:
+            move.wait()
+        every = ids_s[...]
+        starts = jnp.zeros_like(every)
+        for d in range(1, 8):
+            before = jnp.sum((every < d).astype(jnp.int32), axis=2, keepdims=True)
+            before = jnp.sum(before, axis=0, keepdims=True)
+            starts = jnp.where(every == d, before, starts)
+        for b in range(o_starts.shape[0]):
+            for piece in range(BQ // 128):
+                at = b * BQ + piece * 128
+                o_starts[b, :, pl.ds(piece * 128, 128)] = starts[
+                    at // local, :, at % local : at % local + 128
+                ]
+
+    act = (
+        finish, forward, across, lambda n: exchanges[n].pass_on(), put_back,
+        lambda n: lax.fori_loop(0, local // 128, norm_rows, 0), document_starts_here,
+    )
+    for code in FRONT_ORDER:
+        act[code // 100](code % 100)
     for move in moves:
         move.wait()
-    for exchange in exchanges:
+    for exchange in exchanges.values():
         exchange.finish()
     for chunk in chunks:
         for copy in chunk:
@@ -804,20 +824,20 @@
     )(tokens, gain.reshape(1, width), ids, w_triple, w_out, w_up)
 
 
-MIDDLE_ALONE = (0, 2, 3)
-MIDDLE_X_FIRST = (1, 3)
+MIDDLE_ALONE = (3,)
+MIDDLE_X_FIRST = (0, 2)
 MIDDLE_ORDER = (
-    1100, 600, 1200, 1300, 1400, 700, 701, 702, 602, 501, 703, 1500, 601, 3, 603, 0, 800, 801,
-    1, 802, 900, 901, 103, 100, 2, 902, 903, 203, 1000, 1001, 101, 303, 1600, 200, 1700, 102,
-    300, 403, 201, 1800, 400, 202, 301, 302, 1900, 401, 402,
+    1100, 500, 501, 502, 1200, 1300, 1400, 700, 701, 702, 703, 1500, 603, 601, 600, 2, 602, 0,
+    1, 800, 801, 802, 900, 901, 902, 102, 903, 1000, 101, 3, 1001, 202, 1600, 1700, 100, 302,
+    201, 103, 1800, 200, 301, 402, 203, 1900, 300, 303, 401, 400, 403,
 )
 
 
 def middle_kernel(
     u, tokens, cotangent, post_gain, second_gain, mid_gain, w_out, w_up, w_down,
-    o_layer, o_middle, o_heads, o_merged, o_second, o_hidden, o_projected, o_gains, o_down,
+    o_layer, o_grad, o_heads, o_merged, o_second, o_hidden, o_projected, o_gains, o_down,
     out_s, up_s, down_s, merged_s, second_s, unit_s, slope_s, act_s, hidden_s, projected_s, middle_s, far_s,
-    inverse_s, inner_s, relay, grad_s,
+    layer_s, o_middle, inverse_s, inner_s, relay, grad_s,
     d_left, d_right, d_whole, d_first, d_second, d_near, d_far,
     local_sem, g_send, g_recv, core_send, core_recv, x_send, x_recv, z_send, z_recv, s_send, s_recv,
 ):
@@ -894,7 +914,7 @@
         save(merged_s, o_merged, 8)
 
     def project(n):
-        at = span(n, 256)
+        at = span(n, 512)
         far_s[:, at] = jnp.dot(merged_s[...], out_s[:, at], preferred_element_type=wide)
 
     def norms(n):
@@ -907,20 +927,20 @@
         second_s[rows, :] = (norm_parts(middle)[0] * second_gain[...]).astype(LOW)
 
     def grow(n):
-        at = span(n, 256)
+        at = span(n, 512)
         z = jnp.dot(second_s[...], up_s[:, at], preferred_element_type=wide)
         root = 0.7978845608028654
         square = z * z
-        bent = jnp.tanh(root * z * (1.0 + 0.044715 * square))
-        half = 0.5 * (1.0 + bent)
-        unit_s[:, at] = z * half
-        slope_s[:, at] = half + 0.5 * root * z * (1.0 - bent * bent) * (1.0 + 3.0 * 0.044715 * square)
+        half = 0.5 + 0.5 * jnp.tanh(z * (root + (root * 0.044715) * square))
+        value = z * half
+        unit_s[:, at] = value
+        slope_s[:, at] = half + (value - value * half) * (2.0 * root + (6.0 * root * 0.044715) * square)
 
     def hidden_norm(n):
-        rows = span(n, 32)
+        rows = span(n, 64)
         unit, inverse = norm_parts(unit_s[rows, :])
         unit_s[rows, :] = unit
-        inner_s[rows, :] = jnp.broadcast_to(inverse, (32, 128))
+        inner_s[rows, :] = jnp.broadcast_to(inverse, (64, 128))
         act_s[rows, :] = (unit * gain).astype(LOW)
 
     def settle_weights():
@@ -931,11 +951,11 @@
         grad_s[...] = jnp.zeros_like(grad_s)
 
     def shrink(n):
-        at = span(n, 256)
+        at = span(n, 512)
         total = jnp.dot(act_s[...], down_s[:, at], preferred_element_type=wide)
         low = cotangent[:, at].astype(wide)
         value = total[:local]
-        o_layer[:, at] = (middle_s[:, at] + value).astype(LOW)
+        layer_s[:, at] = (middle_s[:, at] + value).astype(LOW)
         weight = jnp.sum(total[local:], axis=0, keepdims=True)
         first = jnp.sum(low * weight, axis=1, keepdims=True) * (1.0 / hidden)
         second = jnp.sum(low * value, axis=1, keepdims=True) * (1.0 / hidden)
@@ -951,7 +971,7 @@
     )
 
     def pull_hidden(n):
-        at = span(n, 256)
+        at = span(n, 512)
         grad = nt(cotangent[...], down_s[at, :])
         unit = unit_s[:, at]
         o_gains[3:4, at] = jnp.sum(grad * unit, axis=0, keepdims=True)
@@ -959,7 +979,7 @@
         hidden_s[:, at] = (inner_s[:, 0:1] * pulled * slope_s[:, at]).astype(LOW)
 
     def pull_second(n):
-        at = span(n, 256)
+        at = span(n, 512)
         o_middle[:, at] = nt(hidden_s[...], up_s[at, :])
 
     def pull_norms(n, totals):
@@ -976,7 +996,7 @@
         )
 
     def pull_merged(n):
-        at = span(n, 256)
+        at = span(n, 512)
         merged_s[:, at] = nt(projected_s[...], out_s[at, :]).astype(LOW)
 
     def compute(p):
@@ -990,17 +1010,19 @@
         save(second_s, o_second, 9)
 
     def do_hidden_norm(_):
-        blocks(0, local // 32, hidden_norm)
+        blocks(0, local // 64, hidden_norm)
         later["left"] = share_left(place, 10, act_s, d_left, local, *sems)
 
     def do_shrink(n):
         if n == 0:
             settle_weights()
         else:
-            blocks((n - 1) * 2, 2, shrink)
+            blocks(n - 1, 1, shrink)
+        if n == 2:
+            save(layer_s, o_layer, 18)
 
     def do_pull_hidden(n):
-        blocks(n * (hidden // 1024), hidden // 1024, pull_hidden)
+        blocks(n * (hidden // 2048), hidden // 2048, pull_hidden)
         if n == 3:
             save(hidden_s, o_hidden, 15)
 
@@ -1010,10 +1032,11 @@
         o_gains[1:2, 0:width] = post
         o_gains[2:3, 0:width] = second
         save(projected_s, o_projected, 16)
+        save(o_middle, o_grad, 19)
 
     def do_pull_merged(_):
         saves[0].wait()
-        blocks(0, width // 256, pull_merged)
+        blocks(0, width // 512, pull_merged)
         later["out"] = ToHeads(
             place, merged_s, o_heads, relay.at[1], [sem.at[1] for sem in exchange_sem], local_sem.at[17]
         )
@@ -1026,13 +1049,13 @@
         lambda p: down.advance(p, 4),
         forward,
         across,
-        lambda n: blocks(n * (hidden // 1024), hidden // 1024, grow),
+        lambda n: blocks(n * (hidden // 2048), hidden // 2048, grow),
         do_shrink,
         do_pull_hidden,
-        lambda n: blocks(n * 2, 2, pull_second),
+        lambda n: blocks(n, 1, pull_second),
         lambda n: inbound.pass_on(),
         arrive,
-        lambda n: blocks(0, width // 256, project),
+        lambda n: blocks(0, width // 512, project),
         do_norms,
         do_hidden_norm,
         do_pull_norms,
@@ -1073,7 +1096,7 @@
             jax.ShapeDtypeStruct((hidden // 32, width), wide),
         ),
         in_specs=[any_spec] + [vmem] * 5 + [any_spec] * 3,
-        out_specs=(vmem,) * 2 + (any_spec,) * 5 + (vmem,) * 2,
+        out_specs=(any_spec,) * 7 + (vmem,) * 2,
         scratch_shapes=[
             pltpu.VMEM((width, width), LOW),
             pltpu.VMEM((width, hidden), LOW),
@@ -1086,6 +1109,8 @@
             pltpu.VMEM((local, hidden), LOW),
             pltpu.VMEM((local, width), LOW),
             pltpu.VMEM((local, width), wide),
+            pltpu.VMEM((local, width), wide),
+            pltpu.VMEM((local, width), LOW),
             pltpu.VMEM((local, width), wide),
             pltpu.VMEM((local, 128), wide),
             pltpu.VMEM((local, 128), wide),
@@ -1114,21 +1139,21 @@
 
 
 HALF = 512
-X_FIRST = (1, 3, 5, 12, 13)
+X_FIRST = (0, 3, 8, 13)
 TAIL_ORDER = (
-    0, 3, 7, 9, 500, 1, 100, 2, 103, 4, 5, 600, 700, 15, 101, 501, 200, 107, 102, 109,
-    8, 203, 6, 105, 14, 601, 303, 502, 701, 12, 104, 115, 201, 207, 300, 202, 13, 209, 108, 602,
-    702, 800, 900, 302, 106, 205, 309, 112, 301, 11, 204, 305, 402, 400, 901, 215, 304, 401, 307, 405,
-    212, 403, 114, 10, 409, 113, 315, 208, 111, 404, 312, 206, 902, 415, 308, 407, 306, 412, 214, 110,
-    408, 213, 211, 406, 314, 313, 210, 311, 310, 414, 413, 411, 410,
+    1, 2, 0, 4, 500, 6, 7, 9, 101, 8, 5, 100, 3, 102, 600, 700, 15, 501, 201, 14,
+    104, 108, 106, 103, 107, 202, 109, 302, 601, 502, 701, 301, 105, 12, 13, 200, 206, 204, 207, 402,
+    300, 209, 115, 307, 306, 304, 309, 400, 602, 702, 208, 114, 800, 900, 205, 308, 11, 10, 203, 305,
+    901, 303, 215, 409, 405, 112, 404, 406, 408, 407, 113, 214, 111, 212, 902, 314, 315, 403, 211, 110,
+    312, 414, 213, 311, 415, 210, 412, 313, 401, 310, 411, 413, 410,
 )
 
 
 def tail_kernel(
-    dq, dk, dv, tokens, gain, middle, triple, act_up, act_out, act_in, g_up, g_out, gains, scales,
+    dq, dk, dv, tokens, gain, middle_in, triple_in, act_up, act_out, act_in, g_up, g_out, gains, scales,
     o_tokens, o_triple, o_out, o_up, o_gains,
     e_left, e_right, e_whole, e_first, e_second, e_near, e_far,
-    grad_s, gain_s, gain_r, relay,
+    triple, middle, tokens_s, grad_s, gain_s, gain_r, relay,
     local_sem, core_send, core_recv, x_send, x_recv, z_send, z_recv, s_send, s_recv, gain_send, gain_recv,
 ):
     place = Place()
@@ -1147,6 +1172,9 @@
 
     exchanges = [start_exchange(t) for t in range(3)]
 
+    load_triple = pltpu.make_async_copy(triple_in, triple, local_sem.at[16])
+    load_middle = pltpu.make_async_copy(middle_in, middle, local_sem.at[17])
+
     sems = (local_sem, core_send, core_recv)
     ready = {"up": share_left(place, 0, act_up, e_left.at[0], local, *sems)}
     for k in range(4):
@@ -1155,6 +1183,8 @@
     ready["out"] = share_left(place, 6, act_out, e_left.at[1], local, *sems)
     ready["out"] += share(place, 8, g_out, g_out, e_right.at[4], local, *sems)
     ready["in"] = share_left(place, 9, act_in, e_left.at[2], local, *sems)
+    load_triple.start()
+    load_middle.start()
 
     def write(p, value):
         at = pl.ds(p % 2 * HALF, HALF)
@@ -1170,7 +1200,10 @@
         lambda p: e_left.at[0 if p < 8 else 1 if p < 10 else 2],
         lambda p: e_right.at[p // 2, :, pl.ds(p % 2 * HALF, HALF)], write,
     )
-    gain_s[...] = gains[...]
+    gain_s[0:3, :] = gains[0:3, 0:width]
+    for k in range(gains.shape[1] // width):
+        gain_s[3 + k : 4 + k, :] = gains[3:4, pl.ds(k * width, width)]
+    gain_s[7:8, :] = jnp.zeros((1, width), jnp.float32)
     gain_s[7:8, 0:128] = scales[...]
     def bring_back(t):
         exchanges[t].finish()
@@ -1183,6 +1216,9 @@
         return move
 
     def pull_normed(t):
+        if t == 0:
+            load_triple.wait()
+
         def one(n, carry):
             rows = pl.ds(pl.multiple_of(n * 256, 256), 256)
             part = nt(e_right[7 - t, pl.ds(0, local), :], triple[rows, pl.ds((2 - t) * width, width)])
@@ -1196,11 +1232,15 @@
         unit, inverse = norm_parts(tokens[rows, :].astype(jnp.float32))
         grad = grad_s[rows, :]
         pulled = norm_pull(grad, unit, inverse, gain[...])
-        o_tokens[rows, :] = (middle[rows, :] + pulled).astype(LOW)
+        tokens_s[rows, :] = (middle[rows, :] + pulled).astype(LOW)
         return total + jnp.sum(grad * unit, axis=0, keepdims=True)
 
+    save_tokens = pltpu.make_async_copy(tokens_s, o_tokens, local_sem.at[18])
+
     def pull_norm(_):
+        load_middle.wait()
         gain_s[0:1, :] = lax.fori_loop(0, local // 128, norm_rows, jnp.zeros((1, width), jnp.float32))
+        save_tokens.start()
 
     def gain_moves(peers, first):
         out = [
@@ -1227,6 +1267,17 @@
             for k in range(7):
                 total = total + gain_r[3 + k]
             gain_s[...] = total
+            device = place.dp * 8 + place.seq
+            pick = (
+                lax.broadcasted_iota(jnp.int32, (width, 128), 0)
+                == device * 32 + lax.broadcasted_iota(jnp.int32, (width, 128), 1)
+            ).astype(jnp.float32)
+            o_gains[0:3, :] = jnp.dot(
+                gain_s[...], pick, preferred_element_type=jnp.float32, precision=lax.Precision.HIGHEST
+            )[0:3]
+            block = gain_s[:, pl.ds(pl.multiple_of((device % 8) * 128, 128), 128)]
+            row = lax.broadcasted_iota(jnp.int32, block.shape, 0)
+            o_gains[3:4, :] = jnp.sum(jnp.where(row == 3 + device // 8, block, 0.0), axis=0, keepdims=True)
 
     backs, waited = {}, set()
 
@@ -1260,18 +1311,8 @@
     )
     for code in TAIL_ORDER:
         act[code // 100](code % 100)
-    device = place.dp * 8 + place.seq
-    pick = (
-        lax.broadcasted_iota(jnp.int32, (width, 128), 0)
-        == device * 32 + lax.broadcasted_iota(jnp.int32, (width, 128), 1)
-    ).astype(jnp.float32)
-    o_gains[0:3, :] = jnp.dot(
-        gain_s[...], pick, preferred_element_type=jnp.float32, precision=lax.Precision.HIGHEST
-    )[0:3]
-    block = gain_s[:, pl.ds(pl.multiple_of((device % 8) * 128, 128), 128)]
-    row = lax.broadcasted_iota(jnp.int32, block.shape, 0)
-    o_gains[3:4, :] = jnp.sum(jnp.where(row == 3 + device // 8, block, 0.0), axis=0, keepdims=True)
     o_gains[4:7, :] = jnp.zeros((3, 128), jnp.float32)
+    save_tokens.wait()
     for p in range(16):
         engine.settle(p)
 
@@ -1293,11 +1334,14 @@
             jax.ShapeDtypeStruct((width // 32, hidden), wide),
             jax.ShapeDtypeStruct((8, 128), wide),
         ),
-        in_specs=[any_spec] * 3 + [vmem] * 4 + [any_spec] * 5 + [vmem] * 2,
-        out_specs=(vmem,) * 5,
+        in_specs=[any_spec] * 3 + [vmem] * 2 + [any_spec] * 7 + [vmem] * 2,
+        out_specs=(any_spec,) + (vmem,) * 4,
         scratch_shapes=[pltpu.VMEM((3, 2 * local, width // 2), LOW), pltpu.VMEM((8, 2 * local, width), LOW)]
         + scatter_scratch(16, 32, HALF)
         + [
+            pltpu.VMEM((width, 3 * width), LOW),
+            pltpu.VMEM((local, width), wide),
+            pltpu.VMEM((local, width), LOW),
             pltpu.VMEM((local, width), wide),
             pltpu.VMEM((8, width), wide),
             pltpu.VMEM((10, 8, width), wide),
@@ -1316,6 +1360,36 @@
         ),
         name="tail",
     )(*dqkv, tokens, gain.reshape(1, width), middle, triple, *acts, *grads, gains, scales)
+
+
+def finish_kernel(count, *refs):
+    ins, outs = refs[: count + 1], refs[count + 1 :]
+    for k in range(count):
+        outs[k][...] = ins[k][...]
+    sums = ins[count]
+    for row in range(3):
+        outs[count + row][...] = sums[row, 0 : outs[count + row].shape[0]]
+    outs[count + 3][...] = sums[3]
+    row = sums[7:8, :]
+    lane = lax.broadcasted_iota(jnp.int32, row.shape, 1)
+    heads = outs[count + 4].shape[1]
+    for h in range(heads):
+        own = (lane >= h * HEAD) & (lane < (h + 1) * HEAD)
+        outs[count + 4][:, h : h + 1] = jnp.sum(jnp.where(own, row, 0.0), axis=1, keepdims=True)
+
+
+def finish(arrays, sums, own, heads):
+    vmem = pl.BlockSpec(memory_space=pltpu.VMEM)
+    wide = jnp.float32
+    shapes = [jax.ShapeDtypeStruct(a.shape, a.dtype) for a in arrays]
+    shapes += [jax.ShapeDtypeStruct((own,), wide)] * 3 + [jax.ShapeDtypeStruct((sums.shape[1],), wide), jax.ShapeDtypeStruct((1, heads), wide)]
+    return pl.pallas_call(
+        functools.partial(finish_kernel, len(arrays)),
+        out_shape=tuple(shapes),
+        in_specs=[vmem] * (len(arrays) + 1),
+        out_specs=(vmem,) * len(shapes),
+        name="finish",
+    )(*arrays, sums)
 
 
 def per_device(
@@ -1353,13 +1427,9 @@
         lax.all_to_all(triple[:, 2 * width :], "seq", split_axis=1, concat_axis=0, tiled=True),
     )
     heads_here = queries.shape[1] // HEAD
-    own_scale = lax.dynamic_slice_in_dim(
-        head_scale, lax.axis_index("seq") * heads_here, heads_here, 0
-    )
-    scale_wide = jnp.repeat(own_scale, HEAD)[None]
     starts = document_starts(doc_ids)
     attended, scaled, logsum = attend_forward(
-        queries, keys_all, values_all, starts, scale_wide
+        queries, keys_all, values_all, starts, head_scale
     )
     merged = lax.all_to_all(scaled, "seq", split_axis=0, concat_axis=1, tiled=True)
     projected = jnp.dot(merged, output_full, preferred_element_type=jnp.float32)
@@ -1391,7 +1461,7 @@
         grad_merged, "seq", split_axis=1, concat_axis=0, tiled=True
     )
     grad_queries, grad_keys, grad_values, scale_lanes = attend_backward(
-        queries, keys_all, values_all, attended, grad_scaled, starts, scale_wide, logsum
+        queries, keys_all, values_all, attended, grad_scaled, starts, head_scale, logsum
     )
     scale_terms = jnp.sum(scale_lanes.reshape(heads_here, HEAD), axis=1)
     back_queries, back_keys, back_values = (
@@ -1463,22 +1533,15 @@
 ):
     width, hidden = tokens.shape[2], up_weight.shape[1]
     heads_here = width // HEAD // sizes[1]
-    own_scale = lax.dynamic_slice_in_dim(
-        head_scale, lax.axis_index("seq") * heads_here, heads_here, 0
-    )
-    scale_wide = jnp.repeat(own_scale, HEAD)[None]
     values, keys, queries, normed, starts, triple_full, output_full, up_full = front(
         tokens[0], first_gain, segment_ids, triple_weight, output_weight, up_weight
     )
-    attended, scaled, logsum = attend_forward(queries, keys, values, starts, scale_wide)
-    layer_out, grad_middle, grad_scaled, merged, second, grad_hidden, grad_projected, gains, grad_down = middle(
+    attended, scaled, logsum = attend_forward(queries, keys, values, starts, head_scale)
+    layer_out, grad_middle, grad_scaled, merged, second_low, grad_hidden, grad_projected, gains, grad_down = middle(
         scaled, tokens[0], cotangent[0], post_gain, second_gain, mid_gain, output_full, up_full, down_weight
     )
     grad_queries, grad_keys, grad_values, scale_lanes = attend_backward(
-        queries, keys, values, attended, grad_scaled, starts, scale_wide, logsum
-    )
-    gains = jnp.concatenate(
-        (gains[:3, :width], gains[3].reshape(-1, width), jnp.zeros((1, width), jnp.float32)), axis=0
+        queries, keys, values, attended, grad_scaled, starts, head_scale, logsum
     )
     grad_tokens, grad_triple, grad_output, grad_up, sums = tail(
         (grad_queries, grad_keys, grad_values),
@@ -1486,23 +1549,25 @@
         first_gain,
         grad_middle,
         triple_full,
-        (second, merged, normed),
+        (second_low, merged, normed),
         (grad_hidden, grad_projected),
         gains,
         scale_lanes,
     )
-    own = width // 32
+    layer_out, grad_tokens, grad_triple, grad_output, grad_up, grad_down, first, post, second, mid, scale = finish(
+        (layer_out, grad_tokens, grad_triple, grad_output, grad_up, grad_down), sums, width // 32, heads_here
+    )
     return (
         layer_out[None],
         grad_tokens[None],
-        sums[0, :own],
+        first,
         grad_triple,
-        jnp.sum(sums[7].reshape(heads_here, HEAD), axis=1),
+        scale[0],
         grad_output,
-        sums[1, :own],
-        sums[2, :own],
+        post,
+        second,
         grad_up,
-        sums[3],
+        mid,
         grad_down,
     )
 

time: 360 us -> 336 us (0.933)
  Pallas kernels: 347 us -> 335 us
  local copies, waits for them, and re-layouts: 10 us -> 0 us
    pallas_call x1, Pallas kernels: 111 us -> 100 us  [middle(): pl.pallas_call(middle_kernel, out_shape=(act, jax.ShapeDtypeStruct((local...]
    pallas_call x1, Pallas kernels: 111 us -> 104 us  [tail(): pl.pallas_call(tail_kernel, out_shape=(jax.ShapeDtypeStruct((local, width...]
    unnamed x20 -> x0, local copies, waits for them, and re-layouts: 4.77 us -> none
    pallas_call x0 -> x1, Pallas kernels: none -> 3.6 us  [finish(): pl.pallas_call(functools.partial(finish_kernel, len(arrays)), out_shape=t...]
where the time goes in v5:
time: 336 us
  Pallas kernels  335 us (100%)
    pallas_call x1, Pallas kernels, tail(): pl.pallas_call(tail_kernel, out_shape=(jax.ShapeDtypeStruct((local, width...  104 us
    pallas_call x1, Pallas kernels, middle(): pl.pallas_call(middle_kernel, out_shape=(act, jax.ShapeDtypeStruct((local...  100 us
    pallas_call x1, Pallas kernels, front(): pl.pallas_call(front_kernel, out_shape=(one, one, one, jax.ShapeDtypeStru...  81.8 us
    pallas_call x1, Pallas kernels, attend_backward(): pl.pallas_call(functools.partial(backward_kernel, heads), out_shape=(jax....  27.5 us
    pallas_call x1, Pallas kernels, attend_forward(): pl.pallas_call(functools.partial(forward_kernel, heads), out_shape=(jax.S...  17.5 us

profile of v5, /device:TPU:0, one launch (start us, length us, event | category | flops | bytes accessed | tf_op | source)
XLA Modules:
  0.0 335.6 jit_solution(3824920679293750359)
XLA Ops:
  0.6 81.8 %front.1 = (bf16[3072,128]{1,0:T(8,128)(2,1)}, bf16[3072,128]{1,0:T(8,128)(2,1)}, bf16[3072,128]{1,0:T(8,128)(2,1)}, bf16[384,1024]{1,0:T(8,128)(2,1)}, s32[12,1...) custom-call(bf16[384,1024]{1,0:T(8,128)(2,1)} %bitcast.9, ...), custom_call_target="tpu_custom_call" | custom-call | tf_op jit(solution)/shard_map/front/pallas_call | solution.py:795
  82.5 17.5 %attend_forward.1 = (f32[3072,128]{1,0:T(8,128)}, bf16[3072,128]{1,0:T(8,128)(2,1)}, f32[12,1,512]{2,1,0:T(1,128)}) custom-call(s32[12,1,256]{2,1,0:T(1,128)} %get-tuple-element.51.first_ref.start_ref, bf16[3072,128]{1,0:T(8,128)(2,1)} %get-tuple-element.52.q_ref, bf16[3072,128]{1,0:T(8,128)(2,1)} %get-tuple-element.53.k_ref, ...), custom_call_target="tpu_custom_call" | custom-call | flops 1207959552 | bytes 6291456 | tf_op jit(solution)/shard_map/attend_forward/pallas_call | solution.py:136
  100.0 100.0 %middle.1 = (bf16[384,1024]{1,0:T(8,128)(2,1)}, f32[384,1024]{1,0:T(8,128)}, bf16[3072,128]{1,0:T(8,128)(2,1)}, bf16[384,1024]{1,0:T(8,128)(2,1)}, bf16[384,1024...) custom-call(bf16[3072,128]{1,0:T(8,128)(2,1)} %get-tuple-element.55., ...), custom_call_target="tpu_custom_call" | custom-call | tf_op jit(solution)/shard_map/middle/pallas_call | solution.py:1085
  200.0 27.5 %attend_backward.1 = (bf16[3072,128]{1,0:T(8,128)(2,1)}, bf16[3072,128]{1,0:T(8,128)(2,1)}, bf16[3072,128]{1,0:T(8,128)(2,1)}, f32[1,128]{1,0:T(1,128)}) custom-call(s32[12,1,256]{2,1,0:T(1,128)} %get-tuple-element.51.first_ref.start_ref, bf16[3072,128]{1,0:T(8,128)(2,1)} %get-tuple-element.52.q_ref, bf16[3072,128]{1,0:T(8,128)(2,1)} %get-tuple-element.53.k_ref, ...), custom_call_target="tpu_custom_call" | custom-call | flops 3623878656 | bytes 12582912 | tf_op jit(solution)/shard_map/attend_backward/pallas_call | solution.py:246
  227.5 104.3 %tail.1 = (bf16[384,1024]{1,0:T(8,128)(2,1)}, f32[32,3072]{1,0:T(8,128)}, f32[32,1024]{1,0:T(8,128)}, f32[32,4096]{1,0:T(8,128)}, f32[8,128]{1,0:T(8,128)}) custom-call(bf16[3072,128]{1,0:T(8,128)(2,1)} %get-tuple-element.62.dq, bf16[3072,128]{1,0:T(8,128)(2,1)} %get-tuple-element.63.dk, bf16[3072,128]{1,0:T(8,128)(2,1)} %get-tuple-element.64.dv, ...), custom_call_target="tpu_custom_call" | custom-call | tf_op jit(solution)/shard_map/tail/pallas_call | solution.py:1328
  331.9 3.6 %finish.1 = (bf16[384,1024]{1,0:T(8,128)(2,1)}, bf16[384,1024]{1,0:T(8,128)(2,1)}, f32[32,3072]{1,0:T(8,128)}, f32[32,1024]{1,0:T(8,128)}, f32[32,4096]{1,0:T(8,...) custom-call(bf16[384,1024]{1,0:T(8,128)(2,1)} %get-tuple-element.58., ...), custom_call_target="tpu_custom_call" | custom-call | tf_op jit(solution)/shard_map/finish/pallas_call | solution.py:1386

commit v6 on v5

--- a/solution.py
+++ b/solution.py
@@ -370,39 +370,46 @@
 
 class ToHeads:
     def __init__(self, place, part, target, relay, sems, keep_sem):
-        self.place, self.target, self.relay, self.sems = place, target, relay, sems
-        x_send, x_recv, z_send, z_recv = sems
-        local, width = relay.shape[-2:]
+        self.place, self.part, self.target, self.relay, self.sems = place, part, target, relay, sems
+        self.keep_sem, self.moves, self.sends = keep_sem, [], []
+
+    def other(self, m):
+        place = self.place
+        low = place.z0 + (m % 2) * (1 - 2 * place.z0)
+        high = place.z1 + (m // 2) * (1 - 2 * place.z1)
+        return high * 2 + low
+
+    def start(self, steps=(2, 3, 1, 0)):
+        place = self.place
+        x_send, x_recv, z_send, z_recv = self.sems
+        local, width = self.relay.shape[-2:]
         rows = rows_of(place.z, place.x, local)
-        self.moves, self.sends = [], []
-        for k in (2, 1, 3, 0):
-            source = part.at[:, lanes_of((place.z + k) % 4, 1 - place.x, width)]
-            landing = target.at[rows, :] if k == 0 else relay.at[k - 1]
-            move = remote(source, landing, x_send.at[k], x_recv.at[k], place.x_partner())
+        for m in steps:
+            source = self.part.at[:, lanes_of(self.other(m), 1 - place.x, width)]
+            landing = self.target.at[rows, :] if m == 0 else self.relay.at[m - 1]
+            move = remote(source, landing, x_send.at[m], x_recv.at[m], place.x_partner())
             move.start()
-            (self.moves if k == 0 else self.sends).append(move)
-        for k in (2, 1, 3):
-            z = (place.z + k) % 4
-            source = part.at[:, lanes_of(z, place.x, width)]
-            move = remote(
-                source, target.at[rows, :], z_send.at[k - 1], z_recv.at[k - 1], (place.dp, z * 2 + place.x)
-            )
+            (self.moves if m == 0 else self.sends).append(move)
+        for m in steps:
+            z = self.other(m)
+            source = self.part.at[:, lanes_of(z, place.x, width)]
+            if m == 0:
+                move = pltpu.make_async_copy(source, self.target.at[rows, :], self.keep_sem)
+            else:
+                device = (place.dp, z * 2 + place.x)
+                move = remote(source, self.target.at[rows, :], z_send.at[m - 1], z_recv.at[m - 1], device)
             move.start()
             self.moves.append(move)
-        source = part.at[:, lanes_of(place.z, place.x, width)]
-        move = pltpu.make_async_copy(source, target.at[rows, :], keep_sem)
-        move.start()
-        self.moves.append(move)
-
-    def pass_on(self):
+
+    def pass_on(self, steps=(2, 3, 1)):
         place, local = self.place, self.relay.shape[-2]
         x_send, x_recv, z_send, z_recv = self.sems
         rows = rows_of(place.z, 1 - place.x, local)
-        for k in (2, 1, 3):
-            here = self.relay.at[k - 1]
-            remote(here, here, x_send.at[k], x_recv.at[k], place.x_partner()).wait_recv()
-            device = (place.dp, (place.z + k) % 4 * 2 + place.x)
-            move = remote(here, self.target.at[rows, :], z_send.at[k + 2], z_recv.at[k + 2], device)
+        for m in steps:
+            here = self.relay.at[m - 1]
+            remote(here, here, x_send.at[m], x_recv.at[m], place.x_partner()).wait_recv()
+            device = (place.dp, self.other(m) * 2 + place.x)
+            move = remote(here, self.target.at[rows, :], z_send.at[m + 2], z_recv.at[m + 2], device)
             move.start()
             self.moves.append(move)
 
@@ -643,10 +650,10 @@
         return out
 
 
-FRONT_ALONE = (0, 2, 5, 7)
+FRONT_ALONE = (0, 2, 5, 8)
 FRONT_ORDER = (
-    500, 200, 0, 101, 300, 600, 202, 2, 201, 1, 103, 104, 302, 301, 205, 203, 106, 204,
-    206, 207, 405, 403, 404, 406, 407,
+    500, 200, 101, 0, 201, 1, 300, 600, 202, 301, 2, 103, 104, 302, 203, 3, 205, 204,
+    106, 303, 107, 206, 208, 207, 405, 406, 404, 408, 407,
 )
 
 
@@ -662,20 +669,23 @@
     meet([(place.dp, (place.seq + k) % 8) for k in range(1, 8)] + [place.core_partner(), place.y_partner()])
     gather = Gather(place, (send, receive))
 
-    def columns(weight, rows, column):
-        at = pl.ds(column * width, width)
-
+    def columns(weight, at):
         def full(d, first, count):
-            return weight.at[pl.ds(pl.multiple_of(d * rows + first, 128), count), at]
+            return weight.at[pl.ds(pl.multiple_of(d * 256 + first, 128), count), at]
 
         return full
 
+    half = width // 2
+    spans = [
+        (2 * width + (1 - place.z1) * half, half), (2 * width + place.z1 * half, half), (width, width), (0, width)
+    ]
+    spans = [(pl.multiple_of(first, 512), count) for first, count in spans]
     plans = []
-    for n, t in enumerate((2, 1, 0)):
-        plans.append((w_triple.at[:, pl.ds(t * width, width)], columns(triple_s, 256, t)))
-    plans.append((w_out, columns(o_out, 256, 0)))
+    for first, count in spans:
+        plans.append((w_triple.at[:, pl.ds(first, count)], columns(triple_s, pl.ds(first, count))))
+    plans.append((w_out, columns(o_out, pl.ds(0, width))))
     for k in range(w_up.shape[1] // width):
-        plans.append((w_up.at[:, pl.ds(k * width, width)], columns(o_up, 256, k)))
+        plans.append((w_up.at[:, pl.ds(k * width, width)], columns(o_up, pl.ds(k * width, width))))
     alone = FRONT_ALONE
     chunks = [
         gather.copies(n, own, full, 256, n not in alone) for n, (own, full) in enumerate(plans)
@@ -684,7 +694,7 @@
     for n, (own, full) in enumerate(plans):
         chunks[n][1].start()
         chunks[n][0].start()
-        target = full(place.dp, 0, 256) if n < 3 else bounce.at[n - 3]
+        target = full(place.dp, 0, 256) if n < 4 else bounce.at[n - 4]
         copy = pltpu.make_async_copy(own, target, local_sem.at[n])
         copy.start()
         mine.append(copy)
@@ -704,29 +714,37 @@
         return carry
 
     moves = []
-    exchanges = {}
+    exchanges = [
+        ToHeads(
+            place, part_s.at[t], target, relay.at[t], [sem.at[t] for sem in exchange_sem], local_sem.at[12 + t]
+        )
+        for t, target in enumerate((o_v, o_k, o_q))
+    ]
+    far, near = (2, 3), (1, 0)
+    steps = ((0, far), (0, near), (1, far + near), (2, far + near))
 
     def project(n):
-        t, target = (2, 1, 0)[n], (o_v, o_k, o_q)[n]
+        first, count = spans[n]
+        t, reach = steps[n]
 
         def one(c, carry):
-            at = pl.ds(pl.multiple_of(c * 256, 256), 256)
-            from_at = pl.ds(pl.multiple_of(t * width + c * 256, 256), 256)
-            part_s[n, :, at] = jnp.dot(
+            from_at = pl.ds(pl.multiple_of(first + c * 256, 256), 256)
+            at = pl.ds(pl.multiple_of(first - (2 - t) * width + c * 256, 256), 256)
+            part_s[t, :, at] = jnp.dot(
                 o_normed[...], triple_s[:, from_at], preferred_element_type=jnp.float32
             ).astype(LOW)
             return carry
 
-        lax.fori_loop(0, width // 256, one, 0)
-        exchange = ToHeads(
-            place, part_s.at[n], target, relay.at[n], [sem.at[n] for sem in exchange_sem], local_sem.at[12 + n]
-        )
-        exchanges[n] = exchange
-        save = pltpu.make_async_copy(
-            triple_s.at[:, pl.ds(t * width, width)], o_triple.at[:, pl.ds(t * width, width)], local_sem.at[15 + n]
-        )
+        lax.fori_loop(0, count // 256, one, 0)
+        exchanges[t].start(reach)
+        at = pl.ds(first, count)
+        save = pltpu.make_async_copy(triple_s.at[:, at], o_triple.at[:, at], local_sem.at[15 + n])
         save.start()
         moves.append(save)
+
+    def pass_on(n):
+        t, reach = steps[n]
+        exchanges[t].pass_on(tuple(m for m in reach if m))
 
     def forward(n):
         if chunks[n][2] is not None:
@@ -747,7 +765,7 @@
         chunks[n][0].wait_recv()
         chunks[n][3].wait_recv()
         mine[n].wait()
-        copy = pltpu.make_async_copy(bounce.at[n - 3], plans[n][1](place.dp, 0, 256), local_sem.at[n])
+        copy = pltpu.make_async_copy(bounce.at[n - 4], plans[n][1](place.dp, 0, 256), local_sem.at[n])
         copy.start()
         moves.append(copy)
 
@@ -768,14 +786,14 @@
                 ]
 
     act = (
-        finish, forward, across, lambda n: exchanges[n].pass_on(), put_back,
+        finish, forward, across, pass_on, put_back,
         lambda n: lax.fori_loop(0, local // 128, norm_rows, 0), document_starts_here,
     )
     for code in FRONT_ORDER:
         act[code // 100](code % 100)
     for move in moves:
         move.wait()
-    for exchange in exchanges.values():
+    for exchange in exchanges:
         exchange.finish()
     for chunk in chunks:
         for copy in chunk:
@@ -810,8 +828,8 @@
             pltpu.VMEM((8, 1, local), jnp.int32),
             pltpu.VMEM((1 + hidden // width, 256, width), LOW),
             pltpu.VMEM((3, 3, local, heads_width), LOW),
-            dma((4, 8)),
-            dma((4, 8)),
+            dma((4, 9)),
+            dma((4, 9)),
             *exchange_sems(3),
             dma((7,)),
             dma((7,)),
@@ -824,12 +842,12 @@
     )(tokens, gain.reshape(1, width), ids, w_triple, w_out, w_up)
 
 
-MIDDLE_ALONE = (3,)
-MIDDLE_X_FIRST = (0, 2)
+MIDDLE_ALONE = (1, 3)
+MIDDLE_X_FIRST = (1, 3)
 MIDDLE_ORDER = (
-    1100, 500, 501, 502, 1200, 1300, 1400, 700, 701, 702, 703, 1500, 603, 601, 600, 2, 602, 0,
-    1, 800, 801, 802, 900, 901, 902, 102, 903, 1000, 101, 3, 1001, 202, 1600, 1700, 100, 302,
-    201, 103, 1800, 200, 301, 402, 203, 1900, 300, 303, 401, 400, 403,
+    1100, 500, 601, 1200, 1300, 1400, 700, 701, 502, 702, 703, 1500, 600, 602, 1, 603, 0, 3,
+    800, 801, 802, 900, 901, 902, 903, 101, 2, 1000, 1001, 1600, 201, 1700, 103, 100, 301, 1800,
+    102, 401, 203, 200, 303, 202, 1900, 300, 403, 302, 400, 402,
 )
 
 
@@ -1040,6 +1058,7 @@
         later["out"] = ToHeads(
             place, merged_s, o_heads, relay.at[1], [sem.at[1] for sem in exchange_sem], local_sem.at[17]
         )
+        later["out"].start()
 
     act = (
         compute,
@@ -1139,13 +1158,13 @@
 
 
 HALF = 512
-X_FIRST = (0, 3, 8, 13)
+X_FIRST = (0, 4, 6, 12)
 TAIL_ORDER = (
-    1, 2, 0, 4, 500, 6, 7, 9, 101, 8, 5, 100, 3, 102, 600, 700, 15, 501, 201, 14,
-    104, 108, 106, 103, 107, 202, 109, 302, 601, 502, 701, 301, 105, 12, 13, 200, 206, 204, 207, 402,
-    300, 209, 115, 307, 306, 304, 309, 400, 602, 702, 208, 114, 800, 900, 205, 308, 11, 10, 203, 305,
-    901, 303, 215, 409, 405, 112, 404, 406, 408, 407, 113, 214, 111, 212, 902, 314, 315, 403, 211, 110,
-    312, 414, 213, 311, 415, 210, 412, 313, 401, 310, 411, 413, 410,
+    1, 2, 4, 5, 6, 9, 500, 7, 101, 0, 104, 8, 3, 102, 106, 600, 700, 501, 201, 14,
+    15, 109, 105, 107, 100, 204, 601, 502, 701, 304, 301, 108, 12, 103, 205, 209, 202, 13, 206, 305,
+    404, 309, 207, 401, 602, 702, 800, 900, 10, 405, 11, 306, 200, 115, 114, 307, 302, 208, 112, 409,
+    300, 203, 901, 308, 407, 113, 215, 402, 400, 406, 303, 214, 110, 213, 902, 315, 210, 408, 111, 314,
+    313, 212, 415, 310, 403, 414, 211, 413, 312, 311, 410, 412, 411,
 )
 
 

time: 336 us -> 330 us (0.982)
  Pallas kernels: 335 us -> 328 us
    pallas_call x1, Pallas kernels: 100 us -> 96.4 us  [middle(): pl.pallas_call(middle_kernel, out_shape=(act, jax.ShapeDtypeStruct((local...]
where the time goes in v6:
time: 330 us; the launch traced here: 329 us
  Pallas kernels  328 us (99%)
    pallas_call x1, Pallas kernels, tail(): pl.pallas_call(tail_kernel, out_shape=(jax.ShapeDtypeStruct((local, width...  104 us
    pallas_call x1, Pallas kernels, middle(): pl.pallas_call(middle_kernel, out_shape=(act, jax.ShapeDtypeStruct((local...  96.4 us
    pallas_call x1, Pallas kernels, front(): pl.pallas_call(front_kernel, out_shape=(one, one, one, jax.ShapeDtypeStru...  79 us
    pallas_call x1, Pallas kernels, attend_backward(): pl.pallas_call(functools.partial(backward_kernel, heads), out_shape=(jax....  27.5 us
    pallas_call x1, Pallas kernels, attend_forward(): pl.pallas_call(functools.partial(forward_kernel, heads), out_shape=(jax.S...  17.5 us

profile of v6, /device:TPU:0, one launch (start us, length us, event | category | flops | bytes accessed | tf_op | source)
XLA Modules:
  0.0 328.5 jit_solution(7217277344354968659)
XLA Ops:
  0.6 79.0 %front.1 = (bf16[3072,128]{1,0:T(8,128)(2,1)}, bf16[3072,128]{1,0:T(8,128)(2,1)}, bf16[3072,128]{1,0:T(8,128)(2,1)}, bf16[384,1024]{1,0:T(8,128)(2,1)}, s32[12,1...) custom-call(bf16[384,1024]{1,0:T(8,128)(2,1)} %bitcast.9, ...), custom_call_target="tpu_custom_call" | custom-call | tf_op jit(solution)/shard_map/front/pallas_call | solution.py:813
  79.6 17.5 %attend_forward.1 = (f32[3072,128]{1,0:T(8,128)}, bf16[3072,128]{1,0:T(8,128)(2,1)}, f32[12,1,512]{2,1,0:T(1,128)}) custom-call(s32[12,1,256]{2,1,0:T(1,128)} %get-tuple-element.51.first_ref.start_ref, bf16[3072,128]{1,0:T(8,128)(2,1)} %get-tuple-element.52.q_ref, bf16[3072,128]{1,0:T(8,128)(2,1)} %get-tuple-element.53.k_ref, ...), custom_call_target="tpu_custom_call" | custom-call | flops 1207959552 | bytes 6291456 | tf_op jit(solution)/shard_map/attend_forward/pallas_call | solution.py:136
  97.2 96.4 %middle.1 = (bf16[384,1024]{1,0:T(8,128)(2,1)}, f32[384,1024]{1,0:T(8,128)}, bf16[3072,128]{1,0:T(8,128)(2,1)}, bf16[384,1024]{1,0:T(8,128)(2,1)}, bf16[384,1024...) custom-call(bf16[3072,128]{1,0:T(8,128)(2,1)} %get-tuple-element.55., ...), custom_call_target="tpu_custom_call" | custom-call | tf_op jit(solution)/shard_map/middle/pallas_call | solution.py:1104
  193.6 27.5 %attend_backward.1 = (bf16[3072,128]{1,0:T(8,128)(2,1)}, bf16[3072,128]{1,0:T(8,128)(2,1)}, bf16[3072,128]{1,0:T(8,128)(2,1)}, f32[1,128]{1,0:T(1,128)}) custom-call(s32[12,1,256]{2,1,0:T(1,128)} %get-tuple-element.51.first_ref.start_ref, bf16[3072,128]{1,0:T(8,128)(2,1)} %get-tuple-element.52.q_ref, bf16[3072,128]{1,0:T(8,128)(2,1)} %get-tuple-element.53.k_ref, ...), custom_call_target="tpu_custom_call" | custom-call | flops 3623878656 | bytes 12582912 | tf_op jit(solution)/shard_map/attend_backward/pallas_call | solution.py:246
  221.1 103.6 %tail.1 = (bf16[384,1024]{1,0:T(8,128)(2,1)}, f32[32,3072]{1,0:T(8,128)}, f32[32,1024]{1,0:T(8,128)}, f32[32,4096]{1,0:T(8,128)}, f32[8,128]{1,0:T(8,128)}) custom-call(bf16[3072,128]{1,0:T(8,128)(2,1)} %get-tuple-element.62.dq, bf16[3072,128]{1,0:T(8,128)(2,1)} %get-tuple-element.63.dk, bf16[3072,128]{1,0:T(8,128)(2,1)} %get-tuple-element.64.dv, ...), custom_call_target="tpu_custom_call" | custom-call | tf_op jit(solution)/shard_map/tail/pallas_call | solution.py:1347
  324.8 3.6 %finish.1 = (bf16[384,1024]{1,0:T(8,128)(2,1)}, bf16[384,1024]{1,0:T(8,128)(2,1)}, f32[32,3072]{1,0:T(8,128)}, f32[32,1024]{1,0:T(8,128)}, f32[32,4096]{1,0:T(8,...) custom-call(bf16[384,1024]{1,0:T(8,128)(2,1)} %get-tuple-element.58., ...), custom_call_target="tpu_custom_call" | custom-call | tf_op jit(solution)/shard_map/finish/pallas_call | solution.py:1405

commit v7 on v6

--- a/solution.py
+++ b/solution.py
@@ -421,14 +421,14 @@
 
 
 class ToTokens:
-    def __init__(self, place, source, target, relay, sems, keep_sem):
+    def __init__(self, place, source, target, relay, sems, keep_sem, steps=(2, 1, 3)):
         self.place, self.target, self.relay, self.sems = place, target, relay, sems
         x_send, x_recv, z_send, z_recv = sems
         local, width = relay.shape[-2:]
         self.moves, self.sends = [], []
         lanes = lanes_of(place.z, place.x, width)
         for x, first in ((1 - place.x, 0), (place.x, 3)):
-            for k in (2, 1, 3):
+            for k in steps:
                 z, index = (place.z + k) % 4, first + k - 1
                 landing = relay.at[k - 1] if first == 0 else target.at[:, lanes]
                 move = remote(
@@ -650,10 +650,10 @@
         return out
 
 
-FRONT_ALONE = (0, 2, 5, 8)
+FRONT_ALONE = (2, 5, 8)
 FRONT_ORDER = (
-    500, 200, 101, 0, 201, 1, 300, 600, 202, 301, 2, 103, 104, 302, 203, 3, 205, 204,
-    106, 303, 107, 206, 208, 207, 405, 406, 404, 408, 407,
+    500, 100, 101, 200, 0, 201, 1, 300, 600, 202, 301, 2, 103, 104, 302, 203, 3, 205,
+    204, 106, 303, 107, 404, 405, 206, 208, 207, 406, 408, 407,
 )
 
 
@@ -867,7 +867,9 @@
     meet(column_peers + [place.x_partner(), place.core_partner(), place.y_partner()])
     exchange_sem = (x_send, x_recv, z_send, z_recv)
 
-    inbound = ToTokens(place, u, merged_s, relay.at[0], [sem.at[0] for sem in exchange_sem], local_sem.at[0])
+    inbound = ToTokens(
+        place, u, merged_s, relay.at[0], [sem.at[0] for sem in exchange_sem], local_sem.at[0], (2, 3, 1)
+    )
     gather = Gather(place, (g_send, g_recv))
     alone = MIDDLE_ALONE
     chunks, mine = [], []
@@ -1158,13 +1160,13 @@
 
 
 HALF = 512
-X_FIRST = (0, 4, 6, 12)
+X_FIRST = (2, 3, 9, 13)
 TAIL_ORDER = (
-    1, 2, 4, 5, 6, 9, 500, 7, 101, 0, 104, 8, 3, 102, 106, 600, 700, 501, 201, 14,
-    15, 109, 105, 107, 100, 204, 601, 502, 701, 304, 301, 108, 12, 103, 205, 209, 202, 13, 206, 305,
-    404, 309, 207, 401, 602, 702, 800, 900, 10, 405, 11, 306, 200, 115, 114, 307, 302, 208, 112, 409,
-    300, 203, 901, 308, 407, 113, 215, 402, 400, 406, 303, 214, 110, 213, 902, 315, 210, 408, 111, 314,
-    313, 212, 415, 310, 403, 414, 211, 413, 312, 311, 410, 412, 411,
+    0, 2, 3, 4, 5, 7, 500, 6, 8, 100, 102, 1, 9, 104, 103, 105, 600, 700, 501, 14,
+    15, 107, 200, 106, 109, 204, 205, 300, 108, 304, 502, 305, 601, 701, 12, 207, 101, 202, 203, 206,
+    13, 307, 400, 404, 303, 208, 114, 602, 702, 800, 900, 306, 308, 403, 10, 201, 407, 209, 302, 11,
+    115, 406, 301, 901, 112, 309, 214, 402, 401, 215, 408, 113, 405, 110, 212, 902, 314, 409, 210, 315,
+    111, 312, 213, 414, 310, 211, 415, 313, 412, 311, 410, 413, 411,
 )
 
 

time: 330 us -> 328 us (level)
  no operation moved by 1% of the time
where the time goes in v7:
time: 328 us
  Pallas kernels  327 us (100%)
    pallas_call x1, Pallas kernels, tail(): pl.pallas_call(tail_kernel, out_shape=(jax.ShapeDtypeStruct((local, width...  103 us
    pallas_call x1, Pallas kernels, middle(): pl.pallas_call(middle_kernel, out_shape=(act, jax.ShapeDtypeStruct((local...  98.8 us
    pallas_call x1, Pallas kernels, front(): pl.pallas_call(front_kernel, out_shape=(one, one, one, jax.ShapeDtypeStru...  77.1 us
    pallas_call x1, Pallas kernels, attend_backward(): pl.pallas_call(functools.partial(backward_kernel, heads), out_shape=(jax....  27 us
    pallas_call x1, Pallas kernels, attend_forward(): pl.pallas_call(functools.partial(forward_kernel, heads), out_shape=(jax.S...  17.5 us

profile of v7, /device:TPU:0, one launch (start us, length us, event | category | flops | bytes accessed | tf_op | source)
XLA Modules:
  0.0 327.8 jit_solution(8870203869189630273)
XLA Ops:
  0.6 77.1 %front.1 = (bf16[3072,128]{1,0:T(8,128)(2,1)}, bf16[3072,128]{1,0:T(8,128)(2,1)}, bf16[3072,128]{1,0:T(8,128)(2,1)}, bf16[384,1024]{1,0:T(8,128)(2,1)}, s32[12,1...) custom-call(bf16[384,1024]{1,0:T(8,128)(2,1)} %bitcast.9, ...), custom_call_target="tpu_custom_call" | custom-call | tf_op jit(solution)/shard_map/front/pallas_call | solution.py:813
  77.7 17.5 %attend_forward.1 = (f32[3072,128]{1,0:T(8,128)}, bf16[3072,128]{1,0:T(8,128)(2,1)}, f32[12,1,512]{2,1,0:T(1,128)}) custom-call(s32[12,1,256]{2,1,0:T(1,128)} %get-tuple-element.51.first_ref.start_ref, bf16[3072,128]{1,0:T(8,128)(2,1)} %get-tuple-element.52.q_ref, bf16[3072,128]{1,0:T(8,128)(2,1)} %get-tuple-element.53.k_ref, ...), custom_call_target="tpu_custom_call" | custom-call | flops 1207959552 | bytes 6291456 | tf_op jit(solution)/shard_map/attend_forward/pallas_call | solution.py:136
  95.2 98.8 %middle.1 = (bf16[384,1024]{1,0:T(8,128)(2,1)}, f32[384,1024]{1,0:T(8,128)}, bf16[3072,128]{1,0:T(8,128)(2,1)}, bf16[384,1024]{1,0:T(8,128)(2,1)}, bf16[384,1024...) custom-call(bf16[3072,128]{1,0:T(8,128)(2,1)} %get-tuple-element.55., ...), custom_call_target="tpu_custom_call" | custom-call | tf_op jit(solution)/shard_map/middle/pallas_call | solution.py:1106
  194.0 27.0 %attend_backward.1 = (bf16[3072,128]{1,0:T(8,128)(2,1)}, bf16[3072,128]{1,0:T(8,128)(2,1)}, bf16[3072,128]{1,0:T(8,128)(2,1)}, f32[1,128]{1,0:T(1,128)}) custom-call(s32[12,1,256]{2,1,0:T(1,128)} %get-tuple-element.51.first_ref.start_ref, bf16[3072,128]{1,0:T(8,128)(2,1)} %get-tuple-element.52.q_ref, bf16[3072,128]{1,0:T(8,128)(2,1)} %get-tuple-element.53.k_ref, ...), custom_call_target="tpu_custom_call" | custom-call | flops 3623878656 | bytes 12582912 | tf_op jit(solution)/shard_map/attend_backward/pallas_call | solution.py:246
  221.1 103.0 %tail.1 = (bf16[384,1024]{1,0:T(8,128)(2,1)}, f32[32,3072]{1,0:T(8,128)}, f32[32,1024]{1,0:T(8,128)}, f32[32,4096]{1,0:T(8,128)}, f32[8,128]{1,0:T(8,128)}) custom-call(bf16[3072,128]{1,0:T(8,128)(2,1)} %get-tuple-element.62.dq, bf16[3072,128]{1,0:T(8,128)(2,1)} %get-tuple-element.63.dk, bf16[3072,128]{1,0:T(8,128)(2,1)} %get-tuple-element.64.dv, ...), custom_call_target="tpu_custom_call" | custom-call | tf_op jit(solution)/shard_map/tail/pallas_call | solution.py:1349
  324.1 3.6 %finish.1 = (bf16[384,1024]{1,0:T(8,128)(2,1)}, bf16[384,1024]{1,0:T(8,128)(2,1)}, f32[32,3072]{1,0:T(8,128)}, f32[32,1024]{1,0:T(8,128)}, f32[32,4096]{1,0:T(8,...) custom-call(bf16[384,1024]{1,0:T(8,128)(2,1)} %get-tuple-element.58., ...), custom_call_target="tpu_custom_call" | custom-call | tf_op jit(solution)/shard_map/finish/pallas_call | solution.py:1407

commit v8 on v7

--- a/solution.py
+++ b/solution.py
@@ -154,8 +154,16 @@
     )(starts, queries, keys, values, starts, scales)
 
 
-def backward_kernel(heads, first_ref, q_ref, k_ref, v_ref, o_ref, du_ref, start_ref, scale_ref, lse_ref,
-                    dq_ref, dk_ref, dv_ref, ds_ref, qs_s, dos_s, delta_s, dqt_s, dk_s, dv_s):
+def backward_kernel(heads, count, first_ref, q_ref, k_ref, v_ref, o_ref, du_ref, start_ref, scale_ref, lse_ref, *refs):
+    carried, refs = refs[:count], refs[count:]
+    (dq_ref, dk_ref, dv_ref, ds_ref), refs = refs[:4], refs[4:]
+    placed, refs = refs[:count], refs[count:]
+    (qs_s, dos_s, delta_s, dqt_s, dk_s, dv_s), refs = refs[:6], refs[6:]
+    held, sem = refs[:count], refs[count:]
+    takes = [pltpu.make_async_copy(carried[n], held[n], sem[0].at[n]) for n in range(count)]
+    puts = [pltpu.make_async_copy(held[n], placed[n], sem[0].at[count + n]) for n in range(count)]
+    for copy in takes:
+        copy.start()
     rows, group = BQ, 1
     blocks = qs_s.shape[0]
     scale = scale_row(scale_ref, q_ref.shape[1])
@@ -176,6 +184,9 @@
         return total + jnp.sum(grad * out, axis=0, keepdims=True)
 
     ds_ref[...] = lax.fori_loop(0, blocks, prepare, jnp.zeros(ds_ref.shape, jnp.float32))
+    for take, put in zip(takes, puts):
+        take.wait()
+        put.start()
 
     def one(j, carry):
         mine = pl.ds(pl.multiple_of(j * BQ, BQ), BQ)
@@ -236,19 +247,23 @@
         return carry
 
     lax.fori_loop(0, blocks, finish, 0)
-
-
-def attend_backward(queries, keys, values, outs, grads, starts, scales, logsum):
+    for put in puts:
+        put.wait()
+
+
+def attend_backward(queries, keys, values, outs, grads, starts, scales, logsum, carried=()):
     length, width = queries.shape
     heads = width // HEAD
     blocks = length // BQ
     vmem = pl.BlockSpec(memory_space=pltpu.VMEM)
     return pl.pallas_call(
-        functools.partial(backward_kernel, heads),
+        functools.partial(backward_kernel, heads, len(carried)),
         out_shape=(jax.ShapeDtypeStruct((length, width), jnp.bfloat16),) * 3
-        + (jax.ShapeDtypeStruct((1, width), jnp.float32),),
-        in_specs=[pl.BlockSpec(memory_space=pltpu.SMEM)] + [vmem] * 6 + [pl.BlockSpec(memory_space=pltpu.SMEM), vmem],
-        out_specs=(vmem,) * 4,
+        + (jax.ShapeDtypeStruct((1, width), jnp.float32),)
+        + tuple(jax.ShapeDtypeStruct(a.shape, a.dtype) for a in carried),
+        in_specs=[pl.BlockSpec(memory_space=pltpu.SMEM)] + [vmem] * 6 + [pl.BlockSpec(memory_space=pltpu.SMEM), vmem]
+        + [pl.BlockSpec(memory_space=pl.ANY)] * len(carried),
+        out_specs=(vmem,) * 4 + (pl.BlockSpec(memory_space=pl.ANY),) * len(carried),
         scratch_shapes=[
             pltpu.VMEM((blocks, heads * BQ, width), jnp.bfloat16),
             pltpu.VMEM((blocks, heads * BQ, width), jnp.bfloat16),
@@ -256,12 +271,14 @@
             pltpu.VMEM((blocks, width, heads * BQ), jnp.float32),
             pltpu.VMEM((BQ, width), jnp.float32),
             pltpu.VMEM((BQ, width), jnp.float32),
-        ],
+        ]
+        + [pltpu.VMEM(a.shape, a.dtype) for a in carried]
+        + ([pltpu.SemaphoreType.DMA((2 * len(carried),))] if carried else []),
         cost_estimate=pl.CostEstimate(
             flops=3 * length * length * width, bytes_accessed=32 * length * width, transcendentals=0
         ),
         name="attend_backward",
-    )(starts, queries, keys, values, outs, grads, starts, scales, logsum)
+    )(starts, queries, keys, values, outs, grads, starts, scales, logsum, *carried)
 
 
 def document_starts(doc_ids):
@@ -1561,8 +1578,8 @@
     layer_out, grad_middle, grad_scaled, merged, second_low, grad_hidden, grad_projected, gains, grad_down = middle(
         scaled, tokens[0], cotangent[0], post_gain, second_gain, mid_gain, output_full, up_full, down_weight
     )
-    grad_queries, grad_keys, grad_values, scale_lanes = attend_backward(
-        queries, keys, values, attended, grad_scaled, starts, head_scale, logsum
+    grad_queries, grad_keys, grad_values, scale_lanes, layer_out, grad_down = attend_backward(
+        queries, keys, values, attended, grad_scaled, starts, head_scale, logsum, (layer_out, grad_down)
     )
     grad_tokens, grad_triple, grad_output, grad_up, sums = tail(
         (grad_queries, grad_keys, grad_values),
@@ -1575,8 +1592,8 @@
         gains,
         scale_lanes,
     )
-    layer_out, grad_tokens, grad_triple, grad_output, grad_up, grad_down, first, post, second, mid, scale = finish(
-        (layer_out, grad_tokens, grad_triple, grad_output, grad_up, grad_down), sums, width // 32, heads_here
+    grad_tokens, grad_triple, grad_output, grad_up, first, post, second, mid, scale = finish(
+        (grad_tokens, grad_triple, grad_output, grad_up), sums, width // 32, heads_here
     )
     return (
         layer_out[None],

time: 328 us -> 324 us (0.988)
  Pallas kernels: 327 us -> 323 us
where the time goes in v8:
time: 324 us
  Pallas kernels  323 us (100%)
    pallas_call x1, Pallas kernels, tail(): pl.pallas_call(tail_kernel, out_shape=(jax.ShapeDtypeStruct((local, width...  101 us
    pallas_call x1, Pallas kernels, middle(): pl.pallas_call(middle_kernel, out_shape=(act, jax.ShapeDtypeStruct((local...  97 us
    pallas_call x1, Pallas kernels, front(): pl.pallas_call(front_kernel, out_shape=(one, one, one, jax.ShapeDtypeStru...  77.1 us
    pallas_call x1, Pallas kernels, attend_backward(): pl.pallas_call(functools.partial(backward_kernel, heads, len(carried)), o...  27.7 us
    pallas_call x1, Pallas kernels, attend_forward(): pl.pallas_call(functools.partial(forward_kernel, heads), out_shape=(jax.S...  17.5 us

profile of v8, /device:TPU:0, one launch (start us, length us, event | category | flops | bytes accessed | tf_op | source)
XLA Modules:
  0.0 324.0 jit_solution(14365754801786000615)
XLA Ops:
  0.6 77.1 %front.1 = (bf16[3072,128]{1,0:T(8,128)(2,1)}, bf16[3072,128]{1,0:T(8,128)(2,1)}, bf16[3072,128]{1,0:T(8,128)(2,1)}, bf16[384,1024]{1,0:T(8,128)(2,1)}, s32[12,1...) custom-call(bf16[384,1024]{1,0:T(8,128)(2,1)} %bitcast.9, ...), custom_call_target="tpu_custom_call" | custom-call | tf_op jit(solution)/shard_map/front/pallas_call | solution.py:830
  77.7 17.5 %attend_forward.1 = (f32[3072,128]{1,0:T(8,128)}, bf16[3072,128]{1,0:T(8,128)(2,1)}, f32[12,1,512]{2,1,0:T(1,128)}) custom-call(s32[12,1,256]{2,1,0:T(1,128)} %get-tuple-element.51.first_ref.start_ref, bf16[3072,128]{1,0:T(8,128)(2,1)} %get-tuple-element.52.q_ref, bf16[3072,128]{1,0:T(8,128)(2,1)} %get-tuple-element.53.k_ref, ...), custom_call_target="tpu_custom_call" | custom-call | flops 1207959552 | bytes 6291456 | tf_op jit(solution)/shard_map/attend_forward/pallas_call | solution.py:136
  95.2 97.0 %middle.1 = (bf16[384,1024]{1,0:T(8,128)(2,1)}, f32[384,1024]{1,0:T(8,128)}, bf16[3072,128]{1,0:T(8,128)(2,1)}, bf16[384,1024]{1,0:T(8,128)(2,1)}, bf16[384,1024...) custom-call(bf16[3072,128]{1,0:T(8,128)(2,1)} %get-tuple-element.56., ...), custom_call_target="tpu_custom_call" | custom-call | tf_op jit(solution)/shard_map/middle/pallas_call | solution.py:1123
  192.2 27.7 %attend_backward.1 = (bf16[3072,128]{1,0:T(8,128)(2,1)}, bf16[3072,128]{1,0:T(8,128)(2,1)}, bf16[3072,128]{1,0:T(8,128)(2,1)}, f32[1,128]{1,0:T(1,128)}, bf16[384,1024]{1,0:T(8,128)(2,1)}, /*index=5*/f32[128,1024]{1,0:T(8,128)}) custom-call(s32[12,1,256]{2,1,0:T(1,128)} %get-tuple-element.51.first_ref.start_ref, bf16[3072,128]{1,0:T(8,128)(2,1)} %get-tuple-element.52.q_ref, ...), custom_call_target="tpu_custom_call" | custom-call | flops 3623878656 | bytes 12582912 | tf_op jit(solution)/shard_map/attend_backward/pallas_call | solution.py:259
  219.9 101.5 %tail.1 = (bf16[384,1024]{1,0:T(8,128)(2,1)}, f32[32,3072]{1,0:T(8,128)}, f32[32,1024]{1,0:T(8,128)}, f32[32,4096]{1,0:T(8,128)}, f32[8,128]{1,0:T(8,128)}) custom-call(bf16[3072,128]{1,0:T(8,128)(2,1)} %get-tuple-element.64.dq, bf16[3072,128]{1,0:T(8,128)(2,1)} %get-tuple-element.65.dk, bf16[3072,128]{1,0:T(8,128)(2,1)} %get-tuple-element.66.dv, ...), custom_call_target="tpu_custom_call" | custom-call | tf_op jit(solution)/shard_map/tail/pallas_call | solution.py:1366
  321.4 2.7 finish.1
